TPU v7x, 32 devices: a whole 2x2x4 slice. The times are simulated.
32 devices in a mesh: fsdp: 8 (over y, x, core), sp: 4 (over z).
Axes of the slice: x: 2, y: 2, z: 4, core: 2. Of those that a mesh axis runs over, the one named last changes fastest.
Arguments:
- tokens: bfloat16 [5120, 1536], P(('fsdp', 'sp')), may hold values from -6 to 6
- condition: bfloat16 [32, 1536], P('fsdp'), may hold values from -6 to 6
- caption: bfloat16 [4096, 4096], P(('fsdp', 'sp')), may hold values from -6 to 6
- clip_lengths: int32 [8, 4], P('fsdp'), may hold values from 0 to 640, as said below
- caption_lengths: int32 [32], P('fsdp'), may hold values from 1 to 128, as said below
- positions: int32 [5120], P(('fsdp', 'sp')), may hold values from 0 to 639, as said below
- ada_weight: bfloat16 [1536, 9216], P(('fsdp', 'sp')), may hold values from -0.15625 to 0.15625
- ada_bias: bfloat16 [9216], P(('fsdp', 'sp')), may hold values from -3 to 3
- attention_gain: bfloat16 [1536], P(('fsdp', 'sp')), may hold values from 0.5 to 1.5
- qkv_weight: bfloat16 [1536, 4608], P(('fsdp', 'sp')), may hold values from -0.15625 to 0.15625
- query_gain: bfloat16 [1536], P(('fsdp', 'sp')), may hold values from 0.5 to 1.5
- key_gain: bfloat16 [1536], P(('fsdp', 'sp')), may hold values from 0.5 to 1.5
- text_key_weight: bfloat16 [4096, 1536], P(('fsdp', 'sp')), may hold values from -0.09375 to 0.09375
- text_key_gain: bfloat16 [1536], P(('fsdp', 'sp')), may hold values from 0.5 to 1.5
- text_value_weight: bfloat16 [4096, 1536], P(('fsdp', 'sp')), may hold values from -0.09375 to 0.09375
- cross_gate: bfloat16 [1536], P(('fsdp', 'sp')), may hold values from -3 to 3
- out_weight: bfloat16 [1536, 1536], P(('fsdp', 'sp')), may hold values from -5 to 5
- feedforward_gain: bfloat16 [1536], P(('fsdp', 'sp')), may hold values from 0.5 to 1.5
- gate_weight: bfloat16 [1536, 4096], P(('fsdp', 'sp')), may hold values from -0.15625 to 0.15625
- up_weight: bfloat16 [1536, 4096], P(('fsdp', 'sp')), may hold values from -0.15625 to 0.15625
- down_weight: bfloat16 [4096, 1536], P(('fsdp', 'sp')), may hold values from -0.09375 to 0.09375
- out_grad: bfloat16 [5120, 1536], P(('fsdp', 'sp')), may hold values from -6 to 6
Outputs:
- output: bfloat16 [5120, 1536], P(('fsdp', 'sp'))
- tokens_grad: float32 [5120, 1536], P(('fsdp', 'sp'))
- ada_weight_grad: float32 [1536, 9216], P(('fsdp', 'sp'))
- ada_bias_grad: float32 [9216], P(('fsdp', 'sp'))
- attention_gain_grad: float32 [1536], P(('fsdp', 'sp'))
- qkv_weight_grad: float32 [1536, 4608], P(('fsdp', 'sp'))
- query_gain_grad: float32 [1536], P(('fsdp', 'sp'))
- key_gain_grad: float32 [1536], P(('fsdp', 'sp'))
- text_key_weight_grad: float32 [4096, 1536], P(('fsdp', 'sp'))
- text_key_gain_grad: float32 [1536], P(('fsdp', 'sp'))
- text_value_weight_grad: float32 [4096, 1536], P(('fsdp', 'sp'))
- cross_gate_grad: float32 [1536], P(('fsdp', 'sp'))
- out_weight_grad: float32 [1536, 1536], P(('fsdp', 'sp'))
- feedforward_gain_grad: float32 [1536], P(('fsdp', 'sp'))
- gate_weight_grad: float32 [1536, 4096], P(('fsdp', 'sp'))
- up_weight_grad: float32 [1536, 4096], P(('fsdp', 'sp'))
- down_weight_grad: float32 [4096, 1536], P(('fsdp', 'sp'))
Inputs may be any that keep to these rules, and one draw needn't show every extreme that they name: `clip_lengths`: each row (one group of 640 tokens) sums to 640. In one row, chosen from the seed, slot 0 holds a single clip of 640 tokens and the other slots are 0; every other row has 4 clips of 1 token or more, one of exactly 512. `caption_lengths`: every group has a clip slot whose caption has exactly 128 live tokens, slot 0 in the group of the single clip. `positions`: each token's index within its clip.
All inputs are finite; a program needn't handle non-finite values.
Results may differ from a plain program's by a relative error of at most 0.013.
Values may be sent and summed in bfloat16 or wider, within the bound.
A program may use at most 448 MiB of HBM per device.

v0:
```python
from functools import partial
import math

import jax
import jax.numpy as jnp
from jax import lax
from jax.sharding import PartitionSpec as P

H = 24
HD = 64
CPG = 4
CAP = 128
QBLOCK = 640


HIGHEST = lax.Precision.HIGHEST
EPSILON = 1e-06
NEGATIVE = -1e30


def rms_gain(values, gain):
    return values * lax.rsqrt(jnp.mean(values * values, axis=-1, keepdims=True) + EPSILON) * gain


def norm_modulate(values, gain, scale, shift):
    return rms_gain(values, gain) * (1.0 + scale) + shift


def rope_angles(positions, half):
    freqs = jnp.exp(jnp.arange(half, dtype=jnp.float32) * (-math.log(10000.0) / half))
    return positions.astype(jnp.float32)[:, None] * freqs[None, :]


def rotate(values, angles):
    half = values.shape[-1] // 2
    cosine = jnp.cos(angles)[:, None, :]
    sine = jnp.sin(angles)[:, None, :]
    first = values[..., :half]
    second = values[..., half:]
    return jnp.concatenate(
        [first * cosine - second * sine, first * sine + second * cosine], axis=-1
    )


def query_key(angles, q_raw, k_raw, query_gain, key_gain):
    rows = q_raw.shape[0]
    query_rot = rotate(rms_gain(q_raw, query_gain).reshape(rows, -1, HD), angles)
    key_rot = rotate(rms_gain(k_raw, key_gain).reshape(rows, -1, HD), angles)
    return (query_rot, key_rot)


def clip_ids(lengths, total):
    ends = jnp.cumsum(lengths)
    place = jnp.arange(total, dtype=jnp.int32)
    return jnp.sum((place[:, None] >= ends[None, :]).astype(jnp.int32), axis=1)


def softmax_rows(scores):
    top = jnp.max(scores, axis=-1, keepdims=True)
    expo = jnp.exp(scores - top)
    return expo / jnp.sum(expo, axis=-1, keepdims=True)


def left_product(left, right):
    return lax.dot_general(
        left, right, (((0,), (0,)), ((), ())), preferred_element_type=jnp.float32
    )


def right_product(left, right):
    return lax.dot_general(
        left, right, (((1,), (1,)), ((), ())), preferred_element_type=jnp.float32
    )


def as_rows(grad, count):
    return grad.reshape(8 * count, -1)


def pack_small(vectors, count):
    return jnp.concatenate([vector.reshape(count, -1) for vector in vectors], axis=1)


def unpack_small(packed, widths):
    pieces = []
    begin = 0
    for width in widths:
        pieces.append(packed[:, begin : begin + width].reshape(-1))
        begin = begin + width
    return pieces


def block_probs(query_block, clip_block, context):
    (
        query_heads,
        key_heads,
        value_heads,
        tkey_heads,
        tvalue_heads,
        group_clip,
        caption_clip,
        caption_live,
        gate_tanh,
    ) = context
    scale = query_heads.shape[-1] ** (-0.5)
    self_scores = (
        jnp.einsum("qhd,khd->hqk", query_block, key_heads, preferred_element_type=jnp.float32)
        * scale
    )
    same_clip = (clip_block[:, None] == group_clip[None, :])[None]
    self_prob = softmax_rows(jnp.where(same_clip, self_scores, NEGATIVE))
    cross_scores = (
        jnp.einsum("qhd,khd->hqk", query_block, tkey_heads, preferred_element_type=jnp.float32)
        * scale
    )
    cross_ok = ((clip_block[:, None] == caption_clip[None, :]) & caption_live[None, :])[None]
    cross_prob = softmax_rows(jnp.where(cross_ok, cross_scores, NEGATIVE))
    return (self_prob, cross_prob)


def attention_forward(context):
    query_heads = context[0]
    value_heads = context[2]
    tvalue_heads = context[4]
    group_clip = context[5]
    gate_tanh = context[8]
    seq_len, heads, head_dim = query_heads.shape
    blocks = seq_len // QBLOCK

    def one_block(block_input):
        query_block, clip_block = block_input
        self_prob, cross_prob = block_probs(query_block, clip_block, context)
        self_out = jnp.einsum(
            "hqk,khd->qhd",
            self_prob.astype(jnp.bfloat16),
            value_heads,
            preferred_element_type=jnp.float32,
        )
        cross_out = jnp.einsum(
            "hqk,khd->qhd",
            cross_prob.astype(jnp.bfloat16),
            tvalue_heads,
            preferred_element_type=jnp.float32,
        )
        return (self_out + gate_tanh[None] * cross_out).astype(jnp.bfloat16)

    mixed = lax.map(
        one_block,
        (query_heads.reshape(blocks, QBLOCK, heads, head_dim), group_clip.reshape(blocks, QBLOCK)),
    )
    return mixed.reshape(seq_len, heads, head_dim)


def attention_backward(context, grad_heads):
    (
        query_heads,
        key_heads,
        value_heads,
        tkey_heads,
        tvalue_heads,
        group_clip,
        caption_clip,
        caption_live,
        gate_tanh,
    ) = context
    seq_len, heads, head_dim = query_heads.shape
    blocks = seq_len // QBLOCK
    scale = head_dim ** (-0.5)

    def one_block(carry, block_input):
        key_total, value_total, tkey_total, tvalue_total, gate_total = carry
        query_block, clip_block, grad_block = block_input
        self_prob, cross_prob = block_probs(query_block, clip_block, context)
        grad_float = grad_block.astype(jnp.float32)
        self_low = self_prob.astype(jnp.bfloat16)
        grad_self = jnp.einsum(
            "qhd,khd->hqk", grad_block, value_heads, preferred_element_type=jnp.float32
        )
        score_grad = (
            self_prob * (grad_self - jnp.sum(self_prob * grad_self, axis=-1, keepdims=True))
        ).astype(jnp.bfloat16)
        query_grad = (
            jnp.einsum("hqk,khd->qhd", score_grad, key_heads, preferred_element_type=jnp.float32)
            * scale
        )
        key_total = (
            key_total
            + jnp.einsum(
                "hqk,qhd->khd", score_grad, query_block, preferred_element_type=jnp.float32
            )
            * scale
        )
        value_total = value_total + jnp.einsum(
            "hqk,qhd->khd", self_low, grad_block, preferred_element_type=jnp.float32
        )
        cross_low = cross_prob.astype(jnp.bfloat16)
        cross_out = jnp.einsum(
            "hqk,khd->qhd", cross_low, tvalue_heads, preferred_element_type=jnp.float32
        )
        gate_total = gate_total + jnp.sum(grad_float * cross_out, axis=0)
        cross_grad = (gate_tanh[None] * grad_float).astype(jnp.bfloat16)
        grad_cross = jnp.einsum(
            "qhd,khd->hqk", cross_grad, tvalue_heads, preferred_element_type=jnp.float32
        )
        cscore_grad = (
            cross_prob * (grad_cross - jnp.sum(cross_prob * grad_cross, axis=-1, keepdims=True))
        ).astype(jnp.bfloat16)
        query_grad = (
            query_grad
            + jnp.einsum(
                "hqk,khd->qhd", cscore_grad, tkey_heads, preferred_element_type=jnp.float32
            )
            * scale
        )
        tkey_total = (
            tkey_total
            + jnp.einsum(
                "hqk,qhd->khd", cscore_grad, query_block, preferred_element_type=jnp.float32
            )
            * scale
        )
        tvalue_total = tvalue_total + jnp.einsum(
            "hqk,qhd->khd", cross_low, cross_grad, preferred_element_type=jnp.float32
        )
        return (
            (key_total, value_total, tkey_total, tvalue_total, gate_total),
            query_grad.astype(jnp.bfloat16),
        )

    start_carry = (
        jnp.zeros(key_heads.shape, jnp.float32),
        jnp.zeros(value_heads.shape, jnp.float32),
        jnp.zeros(tkey_heads.shape, jnp.float32),
        jnp.zeros(tvalue_heads.shape, jnp.float32),
        jnp.zeros((heads, head_dim), jnp.float32),
    )
    final, query_grads = lax.scan(
        one_block,
        start_carry,
        (
            query_heads.reshape(blocks, QBLOCK, heads, head_dim),
            group_clip.reshape(blocks, QBLOCK),
            grad_heads.reshape(blocks, QBLOCK, heads, head_dim),
        ),
    )
    key_total, value_total, tkey_total, tvalue_total, gate_total = final
    gate_local = (gate_total * (1.0 - gate_tanh * gate_tanh)).reshape(-1)
    return (
        query_grads.reshape(seq_len, heads, head_dim),
        key_total.astype(jnp.bfloat16),
        value_total.astype(jnp.bfloat16),
        tkey_total.astype(jnp.bfloat16),
        tvalue_total.astype(jnp.bfloat16),
        gate_local,
    )


def layer_forward(weights, modulation, tokens, caption, clip_lengths, caption_lengths, positions):
    (
        attention_gain,
        qkv_weight,
        query_gain,
        key_gain,
        text_key_weight,
        text_key_gain,
        text_value_weight,
        cross_gate,
        out_weight,
        feedforward_gain,
        gate_weight,
        up_weight,
        down_weight,
    ) = weights
    rows = tokens.shape[0]
    sp_count = lax.axis_size("sp")
    sp_place = lax.axis_index("sp")
    seq_len = sp_count * rows
    heads_local = H // sp_count
    group_clip = clip_ids(clip_lengths[0], seq_len)
    token_clip = lax.dynamic_slice_in_dim(group_clip, sp_place * rows, rows)
    one_hot = (token_clip[:, None] == jnp.arange(CPG, dtype=jnp.int32)[None, :]).astype(jnp.float32)
    token_mod = jnp.dot(one_hot, modulation, precision=HIGHEST, preferred_element_type=jnp.float32)
    shift_one, scale_one, gate_one, shift_two, scale_two, gate_two = jnp.split(token_mod, 6, axis=1)
    values = tokens.astype(jnp.float32)
    normed_one = norm_modulate(
        values, attention_gain.astype(jnp.float32), scale_one, shift_one
    ).astype(jnp.bfloat16)
    projected = jnp.dot(normed_one, qkv_weight, preferred_element_type=jnp.float32)
    q_raw, k_raw, v_raw = jnp.split(projected, 3, axis=1)
    angles = rope_angles(positions, HD // 2)
    query_rot, key_rot = query_key(
        angles, q_raw, k_raw, query_gain.astype(jnp.float32), key_gain.astype(jnp.float32)
    )
    text_key_raw = jnp.dot(caption, text_key_weight, preferred_element_type=jnp.float32)
    text_key = rms_gain(text_key_raw, text_key_gain.astype(jnp.float32))
    text_value = jnp.dot(caption, text_value_weight, preferred_element_type=jnp.float32)
    text_rows = caption.shape[0]
    query_heads, key_heads, value_heads, tkey_heads, tvalue_heads = (
        lax.all_to_all(
            query_rot.astype(jnp.bfloat16), "sp", split_axis=1, concat_axis=0, tiled=True
        ),
        lax.all_to_all(key_rot.astype(jnp.bfloat16), "sp", split_axis=1, concat_axis=0, tiled=True),
        lax.all_to_all(
            v_raw.astype(jnp.bfloat16).reshape(rows, H, HD),
            "sp",
            split_axis=1,
            concat_axis=0,
            tiled=True,
        ),
        lax.all_to_all(
            text_key.astype(jnp.bfloat16).reshape(text_rows, H, HD),
            "sp",
            split_axis=1,
            concat_axis=0,
            tiled=True,
        ),
        lax.all_to_all(
            text_value.astype(jnp.bfloat16).reshape(text_rows, H, HD),
            "sp",
            split_axis=1,
            concat_axis=0,
            tiled=True,
        ),
    )
    caption_total = tkey_heads.shape[0]
    caption_row = jnp.arange(caption_total, dtype=jnp.int32)
    caption_clip = caption_row // CAP
    caption_limit = jnp.sum(
        jnp.where(
            caption_clip[:, None] == jnp.arange(CPG, dtype=jnp.int32)[None, :],
            caption_lengths[None, :],
            0,
        ),
        axis=1,
    )
    caption_live = caption_row % CAP < caption_limit
    gate_tanh = jnp.tanh(
        lax.dynamic_slice_in_dim(
            cross_gate.astype(jnp.float32), sp_place * heads_local * HD, heads_local * HD
        )
    ).reshape(heads_local, HD)
    context = (
        query_heads,
        key_heads,
        value_heads,
        tkey_heads,
        tvalue_heads,
        group_clip,
        caption_clip,
        caption_live,
        gate_tanh,
    )
    mixed_heads = attention_forward(context)
    mixed = lax.all_to_all(mixed_heads, "sp", split_axis=0, concat_axis=1, tiled=True).reshape(
        rows, -1
    )
    attended = jnp.dot(mixed, out_weight, preferred_element_type=jnp.float32)
    middle = values + gate_one * attended
    normed_two = norm_modulate(
        middle, feedforward_gain.astype(jnp.float32), scale_two, shift_two
    ).astype(jnp.bfloat16)
    gate_act = jnp.dot(normed_two, gate_weight, preferred_element_type=jnp.float32)
    up_act = jnp.dot(normed_two, up_weight, preferred_element_type=jnp.float32)
    hidden = (jax.nn.silu(gate_act) * up_act).astype(jnp.bfloat16)
    ffn_out = jnp.dot(hidden, down_weight, preferred_element_type=jnp.float32)
    output = middle + gate_two * ffn_out
    saved = (
        values,
        one_hot,
        token_mod,
        normed_one,
        q_raw,
        k_raw,
        angles,
        text_key_raw,
        context,
        mixed,
        attended,
        middle,
        normed_two,
        gate_act,
        up_act,
        hidden,
        ffn_out,
    )
    return (output, saved)


def body(
    tokens,
    condition,
    caption,
    clip_lengths,
    caption_lengths,
    positions,
    ada_weight,
    ada_bias,
    attention_gain,
    qkv_weight,
    query_gain,
    key_gain,
    text_key_weight,
    text_key_gain,
    text_value_weight,
    cross_gate,
    out_weight,
    feedforward_gain,
    gate_weight,
    up_weight,
    down_weight,
    out_grad,
):
    bias_rows = ada_bias.shape[0]
    gain_rows = attention_gain.shape[0]
    count = lax.axis_size(("fsdp", "sp"))
    gathered = (
        lax.all_gather(ada_weight, ("fsdp", "sp"), axis=0, tiled=True),
        lax.all_gather(ada_bias, ("fsdp", "sp"), axis=0, tiled=True),
        lax.all_gather(attention_gain, ("fsdp", "sp"), axis=0, tiled=True),
        lax.all_gather(qkv_weight, ("fsdp", "sp"), axis=0, tiled=True),
        lax.all_gather(query_gain, ("fsdp", "sp"), axis=0, tiled=True),
        lax.all_gather(key_gain, ("fsdp", "sp"), axis=0, tiled=True),
        lax.all_gather(text_key_weight, ("fsdp", "sp"), axis=0, tiled=True),
        lax.all_gather(text_key_gain, ("fsdp", "sp"), axis=0, tiled=True),
        lax.all_gather(text_value_weight, ("fsdp", "sp"), axis=0, tiled=True),
        lax.all_gather(cross_gate, ("fsdp", "sp"), axis=0, tiled=True),
        lax.all_gather(out_weight, ("fsdp", "sp"), axis=0, tiled=True),
        lax.all_gather(feedforward_gain, ("fsdp", "sp"), axis=0, tiled=True),
        lax.all_gather(gate_weight, ("fsdp", "sp"), axis=0, tiled=True),
        lax.all_gather(up_weight, ("fsdp", "sp"), axis=0, tiled=True),
        lax.all_gather(down_weight, ("fsdp", "sp"), axis=0, tiled=True),
    )
    ada_full = gathered[0]
    bias_full = gathered[1]
    front = gathered[2:]
    silu_cond = jax.nn.silu(condition.astype(jnp.float32)).astype(jnp.bfloat16)
    modulation = jnp.dot(
        silu_cond, ada_full, preferred_element_type=jnp.float32
    ) + bias_full.astype(jnp.float32)
    output, unused = layer_forward(
        front, modulation, tokens, caption, clip_lengths, caption_lengths, positions
    )
    weights = (
        lax.all_gather(attention_gain, ("fsdp", "sp"), axis=0, tiled=True),
        lax.all_gather(qkv_weight, ("fsdp", "sp"), axis=0, tiled=True),
        lax.all_gather(query_gain, ("fsdp", "sp"), axis=0, tiled=True),
        lax.all_gather(key_gain, ("fsdp", "sp"), axis=0, tiled=True),
        lax.all_gather(text_key_weight, ("fsdp", "sp"), axis=0, tiled=True),
        lax.all_gather(text_key_gain, ("fsdp", "sp"), axis=0, tiled=True),
        lax.all_gather(text_value_weight, ("fsdp", "sp"), axis=0, tiled=True),
        lax.all_gather(cross_gate, ("fsdp", "sp"), axis=0, tiled=True),
        lax.all_gather(out_weight, ("fsdp", "sp"), axis=0, tiled=True),
        lax.all_gather(feedforward_gain, ("fsdp", "sp"), axis=0, tiled=True),
        lax.all_gather(gate_weight, ("fsdp", "sp"), axis=0, tiled=True),
        lax.all_gather(up_weight, ("fsdp", "sp"), axis=0, tiled=True),
        lax.all_gather(down_weight, ("fsdp", "sp"), axis=0, tiled=True),
    )
    recomputed, saved = layer_forward(
        weights, modulation, tokens, caption, clip_lengths, caption_lengths, positions
    )
    (
        values,
        one_hot,
        token_mod,
        normed_one,
        q_raw,
        k_raw,
        angles,
        text_key_raw,
        context,
        mixed,
        attended,
        middle,
        normed_two,
        gate_act,
        up_act,
        hidden,
        ffn_out,
    ) = saved
    (
        attention_full,
        qkv_full,
        query_full,
        key_full,
        text_key_full,
        text_gain_full,
        text_value_full,
        cross_full,
        out_full,
        feedforward_full,
        gate_full,
        up_full,
        down_full,
    ) = weights
    shift_one, scale_one, gate_one, shift_two, scale_two, gate_two = jnp.split(token_mod, 6, axis=1)
    rows = tokens.shape[0]
    grad_top = out_grad.astype(jnp.float32)
    grad_gate_two = grad_top * ffn_out
    grad_ffn = (gate_two * grad_top).astype(jnp.bfloat16)
    down_grad = left_product(hidden, grad_ffn)
    grad_hidden = right_product(grad_ffn, down_full)
    sigmoid = jax.nn.sigmoid(gate_act)
    grad_gate_act = (grad_hidden * up_act * sigmoid * (1.0 + gate_act * (1.0 - sigmoid))).astype(
        jnp.bfloat16
    )
    grad_up_act = (grad_hidden * gate_act * sigmoid).astype(jnp.bfloat16)
    gate_grad = left_product(normed_two, grad_gate_act)
    up_grad = left_product(normed_two, grad_up_act)
    grad_normed_two = right_product(grad_gate_act, gate_full) + right_product(grad_up_act, up_full)
    unused_two, pull_two = jax.vjp(
        norm_modulate, middle, feedforward_full.astype(jnp.float32), scale_two, shift_two
    )
    grad_middle_norm, feedforward_grad, grad_scale_two, grad_shift_two = pull_two(grad_normed_two)
    grad_middle = grad_top + grad_middle_norm
    gate_rows, up_rows, down_rows = (
        lax.psum_scatter(
            as_rows(gate_grad, count), ("fsdp", "sp"), scatter_dimension=0, tiled=True
        ),
        lax.psum_scatter(as_rows(up_grad, count), ("fsdp", "sp"), scatter_dimension=0, tiled=True),
        lax.psum_scatter(
            as_rows(down_grad, count), ("fsdp", "sp"), scatter_dimension=0, tiled=True
        ),
    )
    gate_shard = gate_rows.reshape(gate_weight.shape)
    up_shard = up_rows.reshape(up_weight.shape)
    down_shard = down_rows.reshape(down_weight.shape)
    grad_gate_one = grad_middle * attended
    grad_attended = (gate_one * grad_middle).astype(jnp.bfloat16)
    out_weight_grad = left_product(mixed, grad_attended)
    grad_mixed = right_product(grad_attended, out_full).astype(jnp.bfloat16).reshape(rows, -1, HD)
    grad_heads = lax.all_to_all(grad_mixed, "sp", split_axis=1, concat_axis=0, tiled=True)
    query_grads, key_grads, value_grads, tkey_grads, tvalue_grads, gate_local = attention_backward(
        context, grad_heads
    )
    query_back, key_back, value_back, tkey_back, tvalue_back = (
        lax.all_to_all(query_grads, "sp", split_axis=0, concat_axis=1, tiled=True),
        lax.all_to_all(key_grads, "sp", split_axis=0, concat_axis=1, tiled=True),
        lax.all_to_all(value_grads, "sp", split_axis=0, concat_axis=1, tiled=True),
        lax.all_to_all(tkey_grads, "sp", split_axis=0, concat_axis=1, tiled=True),
        lax.all_to_all(tvalue_grads, "sp", split_axis=0, concat_axis=1, tiled=True),
    )
    gate_width = gate_local.shape[0]
    cross_grad = lax.dynamic_update_slice_in_dim(
        jnp.zeros((cross_full.shape[0],), jnp.float32),
        gate_local,
        lax.axis_index("sp") * gate_width,
        0,
    )
    unused_three, pull_rope = jax.vjp(
        partial(query_key, angles),
        q_raw,
        k_raw,
        query_full.astype(jnp.float32),
        key_full.astype(jnp.float32),
    )
    grad_q_raw, grad_k_raw, query_grad, key_grad = pull_rope(
        (query_back.astype(jnp.float32), key_back.astype(jnp.float32))
    )
    grad_projected = jnp.concatenate(
        [
            grad_q_raw.astype(jnp.bfloat16),
            grad_k_raw.astype(jnp.bfloat16),
            value_back.reshape(rows, -1),
        ],
        axis=1,
    )
    qkv_grad = left_product(normed_one, grad_projected)
    grad_normed_one = right_product(grad_projected, qkv_full)
    unused_four, pull_one = jax.vjp(
        norm_modulate, values, attention_full.astype(jnp.float32), scale_one, shift_one
    )
    grad_tokens_norm, attention_grad, grad_scale_one, grad_shift_one = pull_one(grad_normed_one)
    tokens_grad = grad_middle + grad_tokens_norm
    text_rows = caption.shape[0]
    unused_five, pull_text = jax.vjp(rms_gain, text_key_raw, text_gain_full.astype(jnp.float32))
    grad_text_raw, text_gain_grad = pull_text(tkey_back.reshape(text_rows, -1).astype(jnp.float32))
    text_key_grad = left_product(caption, grad_text_raw.astype(jnp.bfloat16))
    text_value_grad = left_product(caption, tvalue_back.reshape(text_rows, -1))
    grad_token_mod = jnp.concatenate(
        [
            grad_shift_one,
            grad_scale_one,
            grad_gate_one,
            grad_shift_two,
            grad_scale_two,
            grad_gate_two,
        ],
        axis=1,
    )
    grad_modulation = lax.dot_general(
        one_hot,
        grad_token_mod,
        (((0,), (0,)), ((), ())),
        precision=HIGHEST,
        preferred_element_type=jnp.float32,
    )
    gains = [attention_grad, query_grad, key_grad, text_gain_grad, cross_grad, feedforward_grad]
    ada_grad = lax.dot_general(
        silu_cond.astype(jnp.float32),
        grad_modulation,
        (((0,), (0,)), ((), ())),
        precision=HIGHEST,
        preferred_element_type=jnp.float32,
    )
    bias_grad = jnp.sum(grad_modulation, axis=0)
    ada_rows, qkv_rows, text_key_rows, text_value_rows, out_rows, small_rows = (
        lax.psum_scatter(as_rows(ada_grad, count), ("fsdp", "sp"), scatter_dimension=0, tiled=True),
        lax.psum_scatter(as_rows(qkv_grad, count), ("fsdp", "sp"), scatter_dimension=0, tiled=True),
        lax.psum_scatter(
            as_rows(text_key_grad, count), ("fsdp", "sp"), scatter_dimension=0, tiled=True
        ),
        lax.psum_scatter(
            as_rows(text_value_grad, count), ("fsdp", "sp"), scatter_dimension=0, tiled=True
        ),
        lax.psum_scatter(
            as_rows(out_weight_grad, count), ("fsdp", "sp"), scatter_dimension=0, tiled=True
        ),
        lax.psum_scatter(
            pack_small([bias_grad] + gains, count), ("fsdp", "sp"), scatter_dimension=0, tiled=True
        ),
    )
    ada_shard = ada_rows.reshape(ada_weight.shape)
    small_pieces = unpack_small(small_rows, [bias_rows] + [gain_rows] * 6)
    bias_shard = small_pieces[0]
    gain_pieces = small_pieces[1:]
    qkv_shard = qkv_rows.reshape(qkv_weight.shape)
    text_key_shard = text_key_rows.reshape(text_key_weight.shape)
    text_value_shard = text_value_rows.reshape(text_value_weight.shape)
    out_shard = out_rows.reshape(out_weight.shape)
    attention_shard, query_shard, key_shard, text_gain_shard, cross_shard, feedforward_shard = (
        gain_pieces
    )
    return (
        output.astype(jnp.bfloat16),
        tokens_grad,
        ada_shard,
        bias_shard,
        attention_shard,
        qkv_shard,
        query_shard,
        key_shard,
        text_key_shard,
        text_gain_shard,
        text_value_shard,
        cross_shard,
        out_shard,
        feedforward_shard,
        gate_shard,
        up_shard,
        down_shard,
    )


def solution(mesh):
    return jax.shard_map(
        body,
        mesh=mesh,
        in_specs=(
            P(("fsdp", "sp"), None),
            P("fsdp", None),
            P(("fsdp", "sp"), None),
            P("fsdp", None),
            P("fsdp"),
            P(("fsdp", "sp")),
            P(("fsdp", "sp"), None),
            P(("fsdp", "sp")),
            P(("fsdp", "sp")),
            P(("fsdp", "sp"), None),
            P(("fsdp", "sp")),
            P(("fsdp", "sp")),
            P(("fsdp", "sp"), None),
            P(("fsdp", "sp")),
            P(("fsdp", "sp"), None),
            P(("fsdp", "sp")),
            P(("fsdp", "sp"), None),
            P(("fsdp", "sp")),
            P(("fsdp", "sp"), None),
            P(("fsdp", "sp"), None),
            P(("fsdp", "sp"), None),
            P(("fsdp", "sp"), None),
        ),
        out_specs=(
            P(("fsdp", "sp"), None),
            P(("fsdp", "sp"), None),
            P(("fsdp", "sp"), None),
            P(("fsdp", "sp")),
            P(("fsdp", "sp")),
            P(("fsdp", "sp"), None),
            P(("fsdp", "sp")),
            P(("fsdp", "sp")),
            P(("fsdp", "sp"), None),
            P(("fsdp", "sp")),
            P(("fsdp", "sp"), None),
            P(("fsdp", "sp")),
            P(("fsdp", "sp"), None),
            P(("fsdp", "sp")),
            P(("fsdp", "sp"), None),
            P(("fsdp", "sp"), None),
            P(("fsdp", "sp"), None),
        ),
        check_vma=False,
    )
```

profile of v0, /device:TPU:0, one launch (start us, length us, event | category | flops | bytes accessed | tf_op | source)
XLA Modules:
  0.0 3437.1 jit_solution(13364238152241496413)
XLA Ops:
  20.1 43.4 %all-reduce.12 = (bf16[9216]{0:T(1024)(128)(2,1)S(1)}, bf16[1536]{0:T(1024)(128)(2,1)S(1)}, bf16[1536]{0:T(1024)(128)(2,1)S(1)}, bf16[1536]{0:T(1024)(128)(2,1)S...) all-reduce(bf16[9216]{0:T(1024)(128)(2,1)S(1)} %dynamic-update-slic, ...), channel_id=1, replica_groups=mesh['fsdp'=8,'sp'=4] {'fsdp','sp'}, use_global_device_ids=true, to_apply=%add.4 | all-reduce | flops 18432 | bytes 73728
  67.4 41.7 %all-gather.15.cloned.1.call-done = bf16[4096,1536]{1,0:T(8,128)(2,1)} async-done(((bf16[128,1536]{1,0:T(8,128)(2,1)}), bf16[4096,1536]{1,0:T(8,128)(2,1)}) %all-gather.15.cloned.1.call-update) | async-done | bytes 12582928 | tf_op jit(solution)/shard_map/all_gather | solution.py:423
  121.2 166.4 %all-gather.9.cloned.1.call-done = bf16[1536,9216]{1,0:T(8,128)(2,1)} async-done(((bf16[48,9216]{1,0:T(8,128)(2,1)}), bf16[1536,9216]{1,0:T(8,128)(2,1)}) %all-gather.9.cloned.1.call-update) | async-done | bytes 28311568 | tf_op jit(solution)/shard_map/all_gather | solution.py:417
  304.1 86.9 %all-gather.11.cloned.1.call-done = bf16[1536,4608]{1,0:T(8,128)(2,1)} async-done(((bf16[48,4608]{1,0:T(8,128)(2,1)}), bf16[1536,4608]{1,0:T(8,128)(2,1)}) %all-gather.11.cloned.1.call-update) | async-done | bytes 14155792 | tf_op jit(solution)/shard_map/all_gather | solution.py:420
  450.8 30.2 all-to-all-done.1
  484.4 33.7 all-gather.13.cloned.1.call-done
  602.0 85.7 %all-gather.21.cloned.1.call-done = bf16[1536,4096]{1,0:T(8,128)(2,1)} async-done(((bf16[48,4096]{1,0:T(8,128)(2,1)}), bf16[1536,4096]{1,0:T(8,128)(2,1)}) %all-gather.21.cloned.1.call-update) | async-done | bytes 12582928 | tf_op jit(solution)/shard_map/all_gather | solution.py:430
  695.9 88.5 %all-gather.19.cloned.1.call-done = bf16[1536,4096]{1,0:T(8,128)(2,1)} async-done(((bf16[48,4096]{1,0:T(8,128)(2,1)}), bf16[1536,4096]{1,0:T(8,128)(2,1)}) %all-gather.19.cloned.1.call-update) | async-done | bytes 12582928 | tf_op jit(solution)/shard_map/all_gather | solution.py:429
  792.7 88.4 %all-gather.23.cloned.1.call-done = bf16[4096,1536]{1,0:T(8,128)(2,1)} async-done(((bf16[128,1536]{1,0:T(8,128)(2,1)}), bf16[4096,1536]{1,0:T(8,128)(2,1)}) %all-gather.23.cloned.1.call-update) | async-done | bytes 12582928 | tf_op jit(solution)/shard_map/all_gather | solution.py:431
  928.0 24.3 all_to_all.204
  1229.7 26.8 reshape.534
  1268.0 26.8 reshape.532
  1307.2 25.5 copy.257
  1394.8 24.9 copy.262
  1458.8 30.6 reshape.518
  1490.3 27.2 fusion.127
  1517.5 57.9 %reshape.507 = f32[256,55296]{1,0:T(8,128)} reshape(f32[1536,9216]{1,0:T(8,128)} %fusion.127) | data formatting | bytes 113246208 | tf_op jit(solution)/shard_map/reshape | solution.py:77
  1580.0 105.8 %reduce-scatter.23.cloned.1.call-done = f32[8,24576]{1,0:T(8,128)} async-done(((f32[256,24576]{1,0:T(8,128)}), f32[8,24576]{1,0:T(8,128)}) %reduce-scatter.23.cloned.1.call-update) | async-done | bytes 786448 | tf_op jit(solution)/shard_map/reduce_scatter | solution.py:520
  1688.0 246.7 %reduce-scatter.21.cloned.1.call-done = f32[8,24576]{1,0:T(8,128)} async-done(((f32[256,24576]{1,0:T(8,128)}), f32[8,24576]{1,0:T(8,128)}) %reduce-scatter.21.cloned.1.call-update) | async-done | bytes 786448 | tf_op jit(solution)/shard_map/reduce_scatter | solution.py:519
  1936.9 246.9 %reduce-scatter.19.cloned.1.call-done = f32[8,24576]{1,0:T(8,128)} async-done(((f32[256,24576]{1,0:T(8,128)}), f32[8,24576]{1,0:T(8,128)}) %reduce-scatter.19.cloned.1.call-update) | async-done | bytes 786448 | tf_op jit(solution)/shard_map/reduce_scatter | solution.py:516
  2185.9 246.7 %reduce-scatter.13.cloned.1.call-done = f32[8,24576]{1,0:T(8,128)} async-done(((f32[256,24576]{1,0:T(8,128)}), f32[8,24576]{1,0:T(8,128)}) %reduce-scatter.13.cloned.1.call-update) | async-done | bytes 786448 | tf_op jit(solution)/shard_map/reduce_scatter | solution.py:609
  2434.8 246.7 %reduce-scatter.15.cloned.1.call-done = f32[8,24576]{1,0:T(8,128)} async-done(((f32[256,24576]{1,0:T(8,128)}), f32[8,24576]{1,0:T(8,128)}) %reduce-scatter.15.cloned.1.call-update) | async-done | bytes 786448 | tf_op jit(solution)/shard_map/reduce_scatter | solution.py:612
  2683.7 266.6 %reduce-scatter.11.cloned.1.call-done = f32[8,27648]{1,0:T(8,128)} async-done(((f32[256,27648]{1,0:T(8,128)}), f32[8,27648]{1,0:T(8,128)}) %reduce-scatter.11.cloned.1.call-update) | async-done | bytes 884752 | tf_op jit(solution)/shard_map/reduce_scatter | solution.py:608
  2952.5 474.8 %reduce-scatter.9.cloned.1.call-done = f32[8,55296]{1,0:T(8,128)} async-done(((f32[256,55296]{1,0:T(8,128)}), f32[8,55296]{1,0:T(8,128)}) %reduce-scatter.9.cloned.1.call-update) | async-done | bytes 1769488 | tf_op jit(solution)/shard_map/reduce_scatter | solution.py:607
  (422 shorter events, 678.8 us)
Async XLA Ops:
  7.2 101.9 %all-gather.15.cloned.1.call-start = ((), (), s32[]{:S(2)}) async-start(), calls=%async_computation.23 | async-start | bytes 12976128 | tf_op jit(solution)/shard_map/all_gather | solution.py:423
  7.9 279.7 %all-gather.9.cloned.1.call-start = ((), (), s32[]{:S(2)}) async-start(), calls=%async_computation.20 | async-start | bytes 29196288 | tf_op jit(solution)/shard_map/all_gather | solution.py:417
  8.7 382.3 %all-gather.11.cloned.1.call-start = ((), (), s32[]{:S(2)}) async-start(), calls=%async_computation.21 | async-start | bytes 14598144 | tf_op jit(solution)/shard_map/all_gather | solution.py:420
  9.4 508.7 %all-gather.13.cloned.1.call-start = ((), (), s32[]{:S(2)}) async-start(), calls=%async_computation.22 | async-start | bytes 12976128 | tf_op jit(solution)/shard_map/all_gather | solution.py:425
  10.0 585.3 %all-gather.17.cloned.1.call-start = ((), (), s32[]{:S(2)}) async-start(), calls=%async_computation.24 | async-start | bytes 4866048 | tf_op jit(solution)/shard_map/all_gather | solution.py:427
  10.6 677.1 %all-gather.21.cloned.1.call-start = ((), (), s32[]{:S(2)}) async-start(), calls=%async_computation.26 | async-start | bytes 12976128 | tf_op jit(solution)/shard_map/all_gather | solution.py:430
  11.2 773.2 %all-gather.19.cloned.1.call-start = ((), (), s32[]{:S(2)}) async-start(), calls=%async_computation.25 | async-start | bytes 12976128 | tf_op jit(solution)/shard_map/all_gather | solution.py:429
  11.9 869.2 %all-gather.23.cloned.1.call-start = ((), (), s32[]{:S(2)}) async-start(), calls=%async_computation.27 | async-start | bytes 12976128 | tf_op jit(solution)/shard_map/all_gather | solution.py:431
  117.5 286.2 %all-to-all-start.4 = ((bf16[128,24,64]{0,2,1:T(8,128)(2,1)}), bf16[128,24,64]{0,2,1:T(8,128)(2,1)S(1)}, u32[]{:S(2)}, u32[]{:S(2)}) async-start(bf16[128,24,64]{0,2,1:T(8,128)(2,1)} %bitcast.13), calls=%async_computation.4 | async-start | bytes 786432 | tf_op jit(solution)/shard_map/all_to_all | solution.py:310
  403.7 36.6 %all-to-all-start = ((bf16[160,24,64]{0,2,1:T(8,128)(2,1)}), bf16[160,24,64]{0,2,1:T(8,128)(2,1)}, u32[]{:S(2)}, u32[]{:S(2)}) async-start(bf16[160,24,64]{0,2,1:T(8,128)(2,1)} %bitcast.2), calls=%async_computation | async-start | bytes 1572864 | tf_op jit(solution)/shard_map/all_to_all | solution.py:303
  440.3 40.6 %all-to-all-start.1 = ((bf16[160,24,64]{0,2,1:T(8,128)(2,1)}), bf16[160,24,64]{0,2,1:T(8,128)(2,1)}, u32[]{:S(2)}, u32[]{:S(2)}) async-start(bf16[160,24,64]{0,2,1:T(8,128)(2,1)} %copy.220), calls=%async_computation.1 | async-start | bytes 1572864 | tf_op jit(solution)/shard_map/all_to_all | solution.py:299
  480.9 49.2 %all-to-all-start.2 = ((bf16[160,24,64]{0,2,1:T(8,128)(2,1)}), bf16[160,24,64]{0,2,1:T(8,128)(2,1)S(1)}, u32[]{:S(2)}, u32[]{:S(2)}) async-start(bf16[160,24,64]{0,2,1:T(8,128)(2,1)} %copy.222), calls=%async_computation.2 | async-start | bytes 1572864 | tf_op jit(solution)/shard_map/all_to_all | solution.py:302
  530.1 25.6 all-to-all-start.3
  1004.2 25.5 all-to-all-start.9
  1047.5 34.7 %all-to-all-start.7 = ((bf16[4,2,30720]{2,1,0:T(2,128)(2,1)}), bf16[4,2,30720]{2,1,0:T(2,128)(2,1)}, u32[]{:S(2)}, u32[]{:S(2)}) async-start(bf16[4,2,30720]{2,1,0:T(2,128)(2,1)} %reshape.565), calls=%async_computation.7 | async-start | bytes 983040 | tf_op jit(solution)/shard_map/all_to_all | solution.py:536
  1051.9 523.5 %all-reduce.15.cloned.1.call-start = ((), (), s32[]{:S(2)}) async-start(), calls=%async_computation.36 | async-start | bytes 163840
  1164.7 413.5 %reduce-scatter.17.cloned.1.call-start = ((), (), s32[]{:S(2)}) async-start(), calls=%async_computation.32 | async-start | bytes 9732096 | tf_op jit(solution)/shard_map/reduce_scatter | solution.py:615
  1181.3 504.5 %reduce-scatter.23.cloned.1.call-start = ((), (), s32[]{:S(2)}) async-start(), calls=%async_computation.35 | async-start | bytes 25952256 | tf_op jit(solution)/shard_map/reduce_scatter | solution.py:520
  1217.7 717.1 %reduce-scatter.21.cloned.1.call-start = ((), (), s32[]{:S(2)}) async-start(), calls=%async_computation.34 | async-start | bytes 25952256 | tf_op jit(solution)/shard_map/reduce_scatter | solution.py:519
  1256.5 927.2 %reduce-scatter.19.cloned.1.call-start = ((), (), s32[]{:S(2)}) async-start(), calls=%async_computation.33 | async-start | bytes 25952256 | tf_op jit(solution)/shard_map/reduce_scatter | solution.py:516
  1294.8 1137.8 %reduce-scatter.13.cloned.1.call-start = ((), (), s32[]{:S(2)}) async-start(), calls=%async_computation.30 | async-start | bytes 25952256 | tf_op jit(solution)/shard_map/reduce_scatter | solution.py:609
  1356.4 1325.1 %reduce-scatter.15.cloned.1.call-start = ((), (), s32[]{:S(2)}) async-start(), calls=%async_computation.31 | async-start | bytes 25952256 | tf_op jit(solution)/shard_map/reduce_scatter | solution.py:612
  1443.2 1507.1 %reduce-scatter.11.cloned.1.call-start = ((), (), s32[]{:S(2)}) async-start(), calls=%async_computation.29 | async-start | bytes 29196288 | tf_op jit(solution)/shard_map/reduce_scatter | solution.py:608
  1489.4 1937.9 %reduce-scatter.9.cloned.1.call-start = ((), (), s32[]{:S(2)}) async-start(), calls=%async_computation.28 | async-start | bytes 58392576 | tf_op jit(solution)/shard_map/reduce_scatter | solution.py:607
  (94 other events, 4870.1 us)
Sparse Core Ops, SparseCore 0:
  10.9 98.1 all-gather.14
  111.9 175.6 all-gather.8
  290.4 100.5 all-gather.10
  393.7 124.3 all-gather.12
  520.8 68.5 all-gather.16
  592.2 95.4 all-gather.20
  690.6 93.7 all-gather.18
  787.3 93.7 all-gather.22
  1164.9 121.8 all-reduce.14
  1292.5 144.7 reduce-scatter.16
  1443.8 242.0 reduce-scatter.22
  1692.1 242.5 reduce-scatter.20
  1941.2 242.5 reduce-scatter.18
  2190.0 242.5 reduce-scatter.12
  2438.9 242.5 reduce-scatter.14
  2687.8 262.3 reduce-scatter.10
  2956.5 470.7 reduce-scatter.8
where the time goes:
time: 3450 us; the launch traced here: 3440 us
  waiting for transfers between devices  2500 us (72%)
  local copies, waits for them, and re-layouts  448 us (13%)
  matrix products  274 us (8%)
  blocking collectives  87.3 us (3%)
  other arithmetic  69.2 us (2%)
  starting transfers between devices  44.5 us (1%)
    reduce_scatter x1, waiting for transfers between devices, body(): lax.psum_scatter(as_rows(ada_grad, count), ('fsdp', 'sp'), scatter_dimens...  475 us
    reduce_scatter x1, waiting for transfers between devices, body(): lax.psum_scatter(as_rows(qkv_grad, count), ('fsdp', 'sp'), scatter_dimens...  267 us
    reduce_scatter x1, waiting for transfers between devices, body(): lax.psum_scatter(as_rows(gate_grad, count), ('fsdp', 'sp'), scatter_dimen...  247 us
    reduce_scatter x1, waiting for transfers between devices, body(): lax.psum_scatter(as_rows(up_grad, count), ('fsdp', 'sp'), scatter_dimensi...  247 us
    reduce_scatter x1, waiting for transfers between devices, body(): lax.psum_scatter(as_rows(text_value_grad, count), ('fsdp', 'sp'), scatter...  247 us
    reduce_scatter x1, waiting for transfers between devices, body(): lax.psum_scatter(as_rows(text_key_grad, count), ('fsdp', 'sp'), scatter_d...  247 us
    reshape x8, local copies, waits for them, and re-layouts, as_rows(): return grad.reshape(8 * count, -1)  224 us
    all_gather x1, waiting for transfers between devices, body(): lax.all_gather(ada_weight, ('fsdp', 'sp'), axis=0, tiled=True)  166 us
  transfers between devices with their start and end apart: 27, of which 18 were waited for; matrix products, arithmetic and copies ran while one was open for 18% of the time, Pallas kernels for 0%

commit v1 on v0

v1 whole, which is shorter than its diff:
```python
import math

import jax
import jax.numpy as jnp
from jax import lax
from jax.sharding import PartitionSpec as P

H = 24
HD = 64
CPG = 4
CAP = 128

HIGHEST = lax.Precision.HIGHEST
EPSILON = 1e-06
NEGATIVE = -1e30
BF16 = jnp.bfloat16
F32 = jnp.float32
ALL = ("fsdp", "sp")


def norm_modulate(values, gain, scale, shift):
    root = lax.rsqrt(jnp.mean(values * values, axis=-1, keepdims=True) + EPSILON)
    return values * root * gain * (1.0 + scale) + shift


def partner(values):
    half = HD // 2
    width = values.shape[1]
    column = lax.broadcasted_iota(jnp.int32, values.shape, 1) % HD
    ahead = jnp.concatenate([values[:, half:], values[:, :half]], axis=1)
    behind = jnp.concatenate([values[:, width - half :], values[:, : width - half]], axis=1)
    return jnp.where(column < half, ahead, behind)


def softmax_rows(scores):
    top = jnp.max(scores, axis=-1, keepdims=True)
    expo = jnp.exp(scores - top)
    return expo / jnp.sum(expo, axis=-1, keepdims=True)


def product(left, right):
    return jnp.dot(left, right, preferred_element_type=F32)


def left_product(left, right):
    return lax.dot_general(left, right, (((0,), (0,)), ((), ())), preferred_element_type=F32)


def right_product(left, right):
    return lax.dot_general(left, right, (((1,), (1,)), ((), ())), preferred_element_type=F32)


def gather(values, axes):
    return lax.all_gather(values, axes, axis=0, tiled=True)


def scatter(values, axes):
    return lax.psum_scatter(values, axes, scatter_dimension=0, tiled=True)


def exchange(values):
    return lax.all_to_all(values, "sp", split_axis=0, concat_axis=0, tiled=True)


def small_sum(values):
    return jnp.sum(lax.all_gather(values, "sp", axis=0), axis=0)


def body(
    tokens,
    condition,
    caption,
    clip_lengths,
    caption_lengths,
    positions,
    ada_weight,
    ada_bias,
    attention_gain,
    qkv_weight,
    query_gain,
    key_gain,
    text_key_weight,
    text_key_gain,
    text_value_weight,
    cross_gate,
    out_weight,
    feedforward_gain,
    gate_weight,
    up_weight,
    down_weight,
    out_grad,
):
    sp = lax.axis_size("sp")
    fsdp = lax.axis_size("fsdp")
    sp_place = lax.axis_index("sp")
    place = lax.axis_index("fsdp") * sp + sp_place
    rows, dim = tokens.shape
    seq = sp * rows
    heads = H // sp
    local = heads * HD
    wrows = qkv_weight.shape[0]
    hidden_dim = gate_weight.shape[1]
    hcols = hidden_dim // (fsdp * sp)
    hlocal = hidden_dim // sp
    text_dim = caption.shape[1]
    tcols = text_dim // (fsdp * sp)
    caps = caption.shape[0] * sp
    bias_rows = ada_bias.shape[0]

    ada_part = gather(ada_weight, "fsdp")
    small = jnp.concatenate(
        [
            ada_bias,
            attention_gain,
            query_gain,
            key_gain,
            text_key_gain,
            cross_gate,
            feedforward_gain,
        ]
    )
    small_all = gather(small[None], ALL).astype(F32)
    bias_full = small_all[:, :bias_rows].reshape(-1)
    gains_full = [
        small_all[:, bias_rows + k * wrows : bias_rows + (k + 1) * wrows].reshape(-1)
        for k in range(6)
    ]
    attention_full, query_full, key_full, text_full, cross_full, feedforward_full = gains_full
    mine = lambda vector: lax.dynamic_slice_in_dim(vector, sp_place * local, local)[None]
    query_mine, key_mine, text_mine = mine(query_full), mine(key_full), mine(text_full)
    gate_tanh = jnp.tanh(mine(cross_full))

    qkv_cols = exchange(
        qkv_weight.reshape(wrows, 3, sp, local)
        .transpose(2, 0, 1, 3)
        .reshape(sp * wrows, 3 * local)
    )
    qkv_full = gather(qkv_cols, "fsdp")
    spread = lambda weight: (
        weight.reshape(wrows, fsdp, sp, hcols)
        .transpose(2, 0, 1, 3)
        .reshape(sp * wrows, hlocal)
    )
    gate_up_cols = exchange(jnp.concatenate([spread(gate_weight), spread(up_weight)], axis=1))
    text_cols = jnp.concatenate(
        [
            text_key_weight.reshape(tcols, sp, 1, local),
            text_value_weight.reshape(tcols, sp, 1, local),
        ],
        axis=2,
    ).reshape(tcols, 2 * dim)
    text_full_weight = gather(text_cols, "fsdp")
    out_full = gather(out_weight, ALL)
    gate_up_full = gather(gate_up_cols, "fsdp")
    gate_full, up_full = gate_up_full[:, :hlocal], gate_up_full[:, hlocal:]
    down_full = gather(down_weight, "fsdp")

    silu_cond = jax.nn.silu(condition.astype(F32)).astype(BF16)
    cond_mine = lax.dynamic_index_in_dim(
        silu_cond.reshape(CPG, fsdp, sp, wrows), sp_place, axis=2, keepdims=False
    ).reshape(CPG, fsdp * wrows)
    modulation = small_sum(product(cond_mine, ada_part)) + bias_full[None]

    lengths = clip_lengths[0]
    ends = jnp.cumsum(lengths)
    token = jnp.arange(seq, dtype=jnp.int32)
    group_clip = jnp.sum((token[:, None] >= ends[None, :]).astype(jnp.int32), axis=1)
    slot = jnp.arange(CPG, dtype=jnp.int32)[None, :]
    group_hot = group_clip[:, None] == slot
    group_place = token - jnp.sum(jnp.where(group_hot, (ends - lengths)[None, :], 0), axis=1)
    token_clip = lax.dynamic_slice_in_dim(group_clip, sp_place * rows, rows)
    one_hot = (token_clip[:, None] == slot).astype(F32)

    def token_mod(k):
        piece = modulation[:, k * dim : (k + 1) * dim]
        value = piece[0:1]
        for c in range(1, CPG):
            value = jnp.where(token_clip[:, None] == c, piece[c : c + 1], value)
        return value

    shift_one, scale_one, gate_one, shift_two, scale_two, gate_two = [
        token_mod(k) for k in range(6)
    ]

    values = tokens.astype(F32)
    normed_one = norm_modulate(values, attention_full[None], scale_one, shift_one).astype(BF16)
    normed_one_all = gather(normed_one, "sp")
    projected = product(normed_one_all, qkv_full)
    q_raw, k_raw, v_raw = (
        projected[:, :local],
        projected[:, local : 2 * local],
        projected[:, 2 * local :],
    )
    qk_squares = small_sum(
        jnp.stack([jnp.sum(q_raw * q_raw, axis=1), jnp.sum(k_raw * k_raw, axis=1)])
    )
    q_root = lax.rsqrt(qk_squares[0] / dim + EPSILON)[:, None]
    k_root = lax.rsqrt(qk_squares[1] / dim + EPSILON)[:, None]
    half = HD // 2
    freqs = jnp.exp(jnp.arange(half, dtype=F32) * (-math.log(10000.0) / half))
    angles = group_place.astype(F32)[:, None] * freqs[None, :]
    cosine = jnp.tile(jnp.cos(angles), (1, 2 * heads))
    sine_half = jnp.sin(angles)
    sine = jnp.tile(jnp.concatenate([-sine_half, sine_half], axis=1), (1, heads))
    rotate = lambda v: v * cosine + partner(v) * sine
    rotate_back = lambda v: v * cosine - partner(v) * sine
    split_heads = lambda v: v.reshape(v.shape[0], heads, HD)
    query = split_heads(rotate(q_raw * q_root * query_mine).astype(BF16))
    key = split_heads(rotate(k_raw * k_root * key_mine).astype(BF16))
    value = split_heads(v_raw.astype(BF16))

    caption_cols = exchange(
        caption.reshape(caption.shape[0], fsdp, sp, tcols)
        .transpose(2, 0, 1, 3)
        .reshape(caps, fsdp * tcols)
    )
    text_parts = jnp.concatenate(
        [
            product(caption_cols, text_full_weight[:, 2 * local * c : 2 * local * (c + 1)]).astype(
                BF16
            )
            for c in range(sp)
        ],
        axis=0,
    )
    text_both = scatter(text_parts, "sp").astype(F32)
    tkey_raw = text_both[:, :local]
    tk_root = lax.rsqrt(small_sum(jnp.sum(tkey_raw * tkey_raw, axis=1)) / dim + EPSILON)[:, None]
    tkey = split_heads((tkey_raw * tk_root * text_mine).astype(BF16))
    tvalue = split_heads(text_both[:, local:].astype(BF16))

    scale = HD**-0.5
    caption_row = jnp.arange(caps, dtype=jnp.int32)
    caption_clip = caption_row // CAP
    caption_limit = jnp.sum(
        jnp.where(caption_clip[:, None] == slot, caption_lengths[None, :], 0), axis=1
    )
    caption_live = caption_row % CAP < caption_limit
    same_clip = (group_clip[:, None] == group_clip[None, :])[None]
    cross_ok = ((group_clip[:, None] == caption_clip[None, :]) & caption_live[None, :])[None]
    to_scores = lambda a, b: jnp.einsum("qhd,khd->hqk", a, b, preferred_element_type=F32)
    to_rows = lambda a, b: jnp.einsum("hqk,khd->qhd", a, b, preferred_element_type=F32)
    to_cols = lambda a, b: jnp.einsum("hqk,qhd->khd", a, b, preferred_element_type=F32)
    self_prob = softmax_rows(jnp.where(same_clip, to_scores(query, key) * scale, NEGATIVE))
    cross_prob = softmax_rows(jnp.where(cross_ok, to_scores(query, tkey) * scale, NEGATIVE))
    self_low = self_prob.astype(BF16)
    cross_low = cross_prob.astype(BF16)
    cross_out = to_rows(cross_low, tvalue).reshape(seq, local)
    mixed_heads = (
        to_rows(self_low, value).reshape(seq, local) + gate_tanh * cross_out
    ).astype(BF16)
    mixed = (
        exchange(mixed_heads).reshape(sp, rows, local).transpose(1, 0, 2).reshape(rows, dim)
    )
    attended = product(mixed, out_full)
    middle = values + gate_one * attended

    normed_two = norm_modulate(middle, feedforward_full[None], scale_two, shift_two).astype(BF16)
    normed_two_all = gather(normed_two, "sp")
    grad_top = out_grad.astype(F32)
    grad_ffn_all = gather((gate_two * grad_top).astype(BF16), "sp")
    gate_act = product(normed_two_all, gate_full)
    up_act = product(normed_two_all, up_full)
    sigmoid = jax.nn.sigmoid(gate_act)
    hidden = (gate_act * sigmoid * up_act).astype(BF16)
    grad_hidden = right_product(grad_ffn_all, down_full)
    grad_gate_act = (grad_hidden * up_act * sigmoid * (1.0 + gate_act * (1.0 - sigmoid))).astype(
        BF16
    )
    grad_up_act = (grad_hidden * gate_act * sigmoid).astype(BF16)
    grad_normed_two = scatter(
        (right_product(grad_gate_act, gate_full) + right_product(grad_up_act, up_full)).astype(
            BF16
        ),
        "sp",
    ).astype(F32)
    ffn_out = scatter(product(hidden, down_full).astype(BF16), "sp").astype(F32)
    output = middle + gate_two * ffn_out
    grad_gate_two = grad_top * ffn_out
    gate_up_rows = scatter(
        jnp.concatenate(
            [
                left_product(normed_two_all, grad_gate_act).astype(BF16),
                left_product(normed_two_all, grad_up_act).astype(BF16),
            ],
            axis=1,
        ),
        "fsdp",
    )
    down_shard = scatter(left_product(hidden, grad_ffn_all).astype(BF16), "fsdp").astype(F32)
    gate_up_back = exchange(gate_up_rows).reshape(sp, wrows, 2, fsdp, hcols)
    gate_up_back = gate_up_back.transpose(2, 1, 3, 0, 4).reshape(2, wrows, hidden_dim).astype(F32)

    unused_two, pull_two = jax.vjp(
        norm_modulate, middle, feedforward_full[None], scale_two, shift_two
    )
    grad_middle_norm, feedforward_grad, grad_scale_two, grad_shift_two = pull_two(grad_normed_two)
    grad_middle = grad_top + grad_middle_norm
    grad_gate_one = grad_middle * attended
    grad_attended = (gate_one * grad_middle).astype(BF16)
    out_shard = scatter(left_product(mixed, grad_attended).astype(BF16), ALL).astype(F32)
    grad_mixed = right_product(grad_attended, out_full).astype(BF16)
    grad_flat = exchange(
        grad_mixed.reshape(rows, sp, local).transpose(1, 0, 2).reshape(seq, local)
    )

    grad_heads = split_heads(grad_flat)
    gate_local = (1.0 - gate_tanh * gate_tanh)[0] * jnp.sum(
        grad_flat.astype(F32) * cross_out, axis=0
    )
    cross_grad = split_heads((gate_tanh * grad_flat.astype(F32)).astype(BF16))
    grad_self = to_scores(grad_heads, value)
    score_grad = (
        self_prob * (grad_self - jnp.sum(self_prob * grad_self, axis=-1, keepdims=True))
    ).astype(BF16)
    grad_cross = to_scores(cross_grad, tvalue)
    cscore_grad = (
        cross_prob * (grad_cross - jnp.sum(cross_prob * grad_cross, axis=-1, keepdims=True))
    ).astype(BF16)
    low = lambda v: v.astype(BF16).reshape(v.shape[0], local).astype(F32)
    query_back = low((to_rows(score_grad, key) + to_rows(cscore_grad, tkey)) * scale)
    key_back = low(to_cols(score_grad, query) * scale)
    value_back = to_cols(self_low, grad_heads).astype(BF16).reshape(seq, local)
    tkey_back = low(to_cols(cscore_grad, query) * scale)
    tvalue_back = to_cols(cross_low, cross_grad).astype(BF16).reshape(caps, local)

    query_turn = rotate_back(query_back)
    key_turn = rotate_back(key_back)
    dots = small_sum(
        jnp.concatenate(
            [
                jnp.sum(query_turn * query_mine * q_raw, axis=1),
                jnp.sum(key_turn * key_mine * k_raw, axis=1),
                jnp.sum(tkey_back * text_mine * tkey_raw, axis=1),
            ]
        )
    )[:, None]

    def norm_back(grad, raw, root, gain, dot):
        raw_grad = root * gain * grad - raw * (root * root * root * dot / dim)
        return raw_grad.astype(BF16), jnp.sum(grad * raw * root, axis=0)

    grad_q, query_gain_grad = norm_back(query_turn, q_raw, q_root, query_mine, dots[:seq])
    grad_k, key_gain_grad = norm_back(key_turn, k_raw, k_root, key_mine, dots[seq : 2 * seq])
    grad_tk, text_gain_grad = norm_back(tkey_back, tkey_raw, tk_root, text_mine, dots[2 * seq :])
    grad_projected = jnp.concatenate([grad_q, grad_k, value_back], axis=1)
    grad_normed_one = scatter(
        right_product(grad_projected, qkv_full).astype(BF16), "sp"
    ).astype(F32)
    qkv_rows = scatter(left_product(normed_one_all, grad_projected).astype(BF16), "fsdp")
    qkv_shard = (
        exchange(qkv_rows)
        .reshape(sp, wrows, 3, local)
        .transpose(1, 2, 0, 3)
        .reshape(wrows, 3 * dim)
        .astype(F32)
    )
    text_grads = gather(jnp.concatenate([grad_tk, tvalue_back], axis=1), "sp")
    text_shard = scatter(
        jnp.concatenate(
            [
                left_product(caption_cols, text_grads[c * caps : (c + 1) * caps]).astype(BF16)
                for c in range(sp)
            ],
            axis=1,
        ),
        "fsdp",
    ).reshape(tcols, sp, 2, local)
    text_key_shard = text_shard[:, :, 0].reshape(tcols, dim).astype(F32)
    text_value_shard = text_shard[:, :, 1].reshape(tcols, dim).astype(F32)

    unused_one, pull_one = jax.vjp(
        norm_modulate, values, attention_full[None], scale_one, shift_one
    )
    grad_tokens_norm, attention_grad, grad_scale_one, grad_shift_one = pull_one(grad_normed_one)
    tokens_grad = grad_middle + grad_tokens_norm

    grad_modulation = lax.dot_general(
        one_hot,
        jnp.concatenate(
            [
                grad_shift_one,
                grad_scale_one,
                grad_gate_one,
                grad_shift_two,
                grad_scale_two,
                grad_gate_two,
            ],
            axis=1,
        ),
        (((0,), (0,)), ((), ())),
        precision=HIGHEST,
        preferred_element_type=F32,
    )
    modulation_all = gather(small_sum(grad_modulation), "fsdp")
    cond_all = gather(silu_cond, "fsdp")
    cond_rows = lax.dynamic_slice_in_dim(cond_all, place * wrows, wrows, axis=1)
    ada_shard = lax.dot_general(
        cond_rows.astype(F32),
        modulation_all,
        (((0,), (0,)), ((), ())),
        precision=HIGHEST,
        preferred_element_type=F32,
    )
    bias_shard = lax.dynamic_slice_in_dim(
        jnp.sum(modulation_all, axis=0), place * bias_rows, bias_rows
    )
    spot = lambda vector: lax.dynamic_update_slice_in_dim(
        jnp.zeros((dim,), F32), vector, sp_place * local, 0
    )
    gain_rows = scatter(
        jnp.stack(
            [
                attention_grad[0],
                spot(query_gain_grad),
                spot(key_gain_grad),
                spot(text_gain_grad),
                spot(gate_local),
                feedforward_grad[0],
            ],
            axis=1,
        )
        .reshape(fsdp * sp, wrows * 6),
        ALL,
    ).reshape(wrows, 6)
    (
        attention_shard,
        query_shard,
        key_shard,
        text_gain_shard,
        cross_shard,
        feedforward_shard,
    ) = [gain_rows[:, k] for k in range(6)]
    return (
        output.astype(BF16),
        tokens_grad,
        ada_shard,
        bias_shard,
        attention_shard,
        qkv_shard,
        query_shard,
        key_shard,
        text_key_shard,
        text_gain_shard,
        text_value_shard,
        cross_shard,
        out_shard,
        feedforward_shard,
        gate_up_back[0],
        gate_up_back[1],
        down_shard,
    )


def solution(mesh):
    return jax.shard_map(
        body,
        mesh=mesh,
        in_specs=(
            P(("fsdp", "sp"), None),
            P("fsdp", None),
            P(("fsdp", "sp"), None),
            P("fsdp", None),
            P("fsdp"),
            P(("fsdp", "sp")),
            P(("fsdp", "sp"), None),
            P(("fsdp", "sp")),
            P(("fsdp", "sp")),
            P(("fsdp", "sp"), None),
            P(("fsdp", "sp")),
            P(("fsdp", "sp")),
            P(("fsdp", "sp"), None),
            P(("fsdp", "sp")),
            P(("fsdp", "sp"), None),
            P(("fsdp", "sp")),
            P(("fsdp", "sp"), None),
            P(("fsdp", "sp")),
            P(("fsdp", "sp"), None),
            P(("fsdp", "sp"), None),
            P(("fsdp", "sp"), None),
            P(("fsdp", "sp"), None),
        ),
        out_specs=(
            P(("fsdp", "sp"), None),
            P(("fsdp", "sp"), None),
            P(("fsdp", "sp"), None),
            P(("fsdp", "sp")),
            P(("fsdp", "sp")),
            P(("fsdp", "sp"), None),
            P(("fsdp", "sp")),
            P(("fsdp", "sp")),
            P(("fsdp", "sp"), None),
            P(("fsdp", "sp")),
            P(("fsdp", "sp"), None),
            P(("fsdp", "sp")),
            P(("fsdp", "sp"), None),
            P(("fsdp", "sp")),
            P(("fsdp", "sp"), None),
            P(("fsdp", "sp"), None),
            P(("fsdp", "sp"), None),
        ),
        check_vma=False,
    )
```

time: 3450 us -> 1230 us (0.36)
  waiting for transfers between devices: 2500 us -> 622 us
  local copies, waits for them, and re-layouts: 448 us -> 105 us
  blocking collectives: 87.3 us -> 217 us
  matrix products: 274 us -> 161 us
    reduce_scatter x8, waiting for transfers between devices: 1830 us -> 282 us  [scatter(): return lax.psum_scatter(values, axes, scatter_dimension=0, tiled=True)]
    all_gather x8 -> x11, waiting for transfers between devices: 591 us -> 241 us  [gather(): return lax.all_gather(values, axes, axis=0, tiled=True)]
    reshape x31 -> x23, local copies, waits for them, and re-layouts: 262 us -> 17.1 us  [the longest x1 3.34 us: body(): cross_out = to_rows(cross_low, tvalue).reshape(seq, local)]
    all_gather x0 -> x6, blocking collectives: none -> 88.3 us  [the longest x5 79.1 us: small_sum(): return jnp.sum(lax.all_gather(values, 'sp', axis=0), axis=0)]
    unnamed x18 -> x21, waiting for transfers between devices: 5.2 us -> 61.7 us
    dot_general x21 -> x22, matrix products: 143 us -> 87.9 us  [the longest x10 35.4 us: product(): return jnp.dot(left, right, preferred_element_type=F32)]
    dot_general x2 -> x0, local copies, waits for them, and re-layouts: 50.4 us -> none  [left_product(): lax.dot_general(left, right, (((0,), (0,)), ((), ())), preferred_element_...]
    dot_general x7 -> x9, matrix products: 72.5 us -> 28.9 us  [left_product(): lax.dot_general(left, right, (((0,), (0,)), ((), ())), preferred_element_...]
  transfers between devices with their start and end apart: 27 -> 25, of which waited for: 18 -> 19; matrix products, arithmetic and copies ran while one was open for 18% -> 18% of each run, Pallas kernels for 0% -> 0%
where the time goes in v1:
time: 1230 us; the launch traced here: 1220 us
  waiting for transfers between devices  622 us (51%)
  blocking collectives  217 us (18%)
  matrix products  161 us (13%)
  local copies, waits for them, and re-layouts  105 us (9%)
  other arithmetic  77 us (6%)
  starting transfers between devices  22.8 us (2%)
  between operations  16.5 us (1%)
    reduce_scatter x8, waiting for transfers between devices, scatter(): return lax.psum_scatter(values, axes, scatter_dimension=0, tiled=True)  282 us
    all_gather x11, waiting for transfers between devices, gather(): return lax.all_gather(values, axes, axis=0, tiled=True)  241 us
    unnamed x2, blocking collectives  85.1 us
    all_gather x5, blocking collectives, small_sum(): return jnp.sum(lax.all_gather(values, 'sp', axis=0), axis=0)  79.1 us
    unnamed x21, waiting for transfers between devices  61.7 us
    all_to_all x2, blocking collectives, exchange(): return lax.all_to_all(values, 'sp', split_axis=0, concat_axis=0, tiled=True)  44 us
    all_to_all x5, waiting for transfers between devices, exchange(): return lax.all_to_all(values, 'sp', split_axis=0, concat_axis=0, tiled=True)  37.2 us
    dot_general x10, matrix products, product(): return jnp.dot(left, right, preferred_element_type=F32)  35.4 us
  transfers between devices with their start and end apart: 25, of which 19 were waited for; matrix products, arithmetic and copies ran while one was open for 18% of the time, Pallas kernels for 0%

profile of v1, /device:TPU:0, one launch (start us, length us, event | category | flops | bytes accessed | tf_op | source)
XLA Modules:
  0.0 1221.6 jit_solution(4860183613529420736)
XLA Ops:
  12.2 19.0 %all_to_all.63 = bf16[4,48,1152]{2,1,0:T(8,128)(2,1)} all-to-all(bf16[4,48,1152]{2,1,0:T(8,128)(2,1)S(1)} %all_to_all.42), channel_id=1, replica_groups=mesh['fsdp'=8,'sp'=4] {'sp'}, dimensions={0} | all-to-all | bytes 884736 | tf_op jit(solution)/shard_map/all_to_all | solution.py:62
  37.5 45.1 %all-reduce = bf16[18432]{0:T(1024)(128)(2,1)S(1)} all-reduce(bf16[18432]{0:T(1024)(128)(2,1)S(1)} %dynamic-update-slice), channel_id=3, replica_groups=mesh['fsdp'=8,'sp'=4] {'fsdp','sp'}, use_global_device_ids=true, to_apply=%add | all-reduce | flops 18432 | bytes 73728
  88.1 16.3 %all-gather.6 = f32[4,4,9216]{2,1,0:T(4,128)S(1)} all-gather(f32[1,4,9216]{2,1,0:T(4,128)S(1)} %convolution_bitcast_fusion.1), channel_id=2, replica_groups=mesh['fsdp'=8,'sp'=4] {'sp'}, dimensions={0}, use_global_device_ids=true | all-gather | bytes 737280 | tf_op jit(solution)/shard_map/all_gather | solution.py:66
  122.2 25.0 %all_to_all.64 = bf16[4,48,2048]{2,1,0:T(8,128)(2,1)} all-to-all(bf16[4,48,2048]{2,1,0:T(8,128)(2,1)S(1)} %pad_maximum_fusion.5), channel_id=1, replica_groups=mesh['fsdp'=8,'sp'=4] {'sp'}, dimensions={0} | all-to-all | bytes 1572864 | tf_op jit(solution)/shard_map/all_to_all | solution.py:62
  156.0 37.0 %all-gather.27.cloned.1.call-done = bf16[640,1536]{1,0:T(8,128)(2,1)} async-done(((bf16[160,1536]{1,0:T(8,128)(2,1)}), bf16[640,1536]{1,0:T(8,128)(2,1)}) %all-gather.27.cloned.1.call-update) | async-done | bytes 1966096 | tf_op jit(solution)/shard_map/all_gather | solution.py:54
  201.6 13.6 %all-gather.7 = f32[4,2,640]{2,1,0:T(2,128)S(1)} all-gather(f32[1,2,640]{2,1,0:T(2,128)S(1)} %maximum_bitcast_fusion), channel_id=4, replica_groups=mesh['fsdp'=8,'sp'=4] {'sp'}, dimensions={0}, use_global_device_ids=true | all-gather | bytes 25600 | tf_op jit(solution)/shard_map/all_gather | solution.py:66
  301.6 23.6 %all-to-all-done.2 = bf16[4,160,384]{2,1,0:T(8,128)(2,1)} async-done(((bf16[4,160,384]{2,1,0:T(8,128)(2,1)}), bf16[4,160,384]{2,1,0:T(8,128)(2,1)}, u32[]{:S(2)}, u32[]{:S(2)}) %all-to-all-start.2) | async-done | bytes 491552 | tf_op jit(solution)/shard_map/all_to_all | solution.py:62
  336.7 36.9 %all-gather.37.cloned.1.call-done = bf16[1536,2048]{1,0:T(8,128)(2,1)} async-done(((bf16[192,2048]{1,0:T(8,128)(2,1)}), bf16[1536,2048]{1,0:T(8,128)(2,1)}) %all-gather.37.cloned.1.call-update) | async-done | bytes 6291472 | tf_op jit(solution)/shard_map/all_gather | solution.py:54
  373.7 45.7 %all-gather.35.cloned.1.call-done = bf16[640,1536]{1,0:T(8,128)(2,1)} async-done(((bf16[160,1536]{1,0:T(8,128)(2,1)}), bf16[640,1536]{1,0:T(8,128)(2,1)}) %all-gather.35.cloned.1.call-update) | async-done | bytes 1966096 | tf_op jit(solution)/shard_map/all_gather | solution.py:54
  429.4 22.9 %all-gather.39.cloned.1.call-done = bf16[1024,1536]{1,0:T(8,128)(2,1)} async-done(((bf16[128,1536]{1,0:T(8,128)(2,1)}), bf16[1024,1536]{1,0:T(8,128)(2,1)}) %all-gather.39.cloned.1.call-update) | async-done | bytes 3145744 | tf_op jit(solution)/shard_map/all_gather | solution.py:54
  452.3 45.5 %all-gather.41.cloned.1.call-done = bf16[640,1536]{1,0:T(8,128)(2,1)} async-done(((bf16[160,1536]{1,0:T(8,128)(2,1)}), bf16[640,1536]{1,0:T(8,128)(2,1)}) %all-gather.41.cloned.1.call-update) | async-done | bytes 1966096 | tf_op jit(solution)/shard_map/all_gather | solution.py:54
  522.7 34.5 %reduce-scatter.18.cloned.1.call-done = bf16[160,1536]{1,0:T(8,128)(2,1)} async-done(((bf16[640,1536]{1,0:T(8,128)(2,1)}), bf16[160,1536]{1,0:T(8,128)(2,1)}) %reduce-scatter.18.cloned.1.call-update) | async-done | bytes 491536 | tf_op jit(solution)/shard_map/reduce_scatter | solution.py:58
  560.4 39.7 %reduce-scatter.16.cloned.1.call-done = bf16[160,1536]{1,0:T(8,128)(2,1)} async-done(((bf16[640,1536]{1,0:T(8,128)(2,1)}), bf16[160,1536]{1,0:T(8,128)(2,1)}) %reduce-scatter.16.cloned.1.call-update) | async-done | bytes 491536 | tf_op jit(solution)/shard_map/reduce_scatter | solution.py:58
  613.1 13.6 %all-to-all-done.4 = bf16[4,160,384]{2,1,0:T(8,128)(2,1)} async-done(((bf16[4,160,384]{2,1,0:T(8,128)(2,1)}), bf16[4,160,384]{2,1,0:T(8,128)(2,1)}, u32[]{:S(2)}, u32[]{:S(2)}) %all-to-all-start.4) | async-done | bytes 491552 | tf_op jit(solution)/shard_map/all_to_all | solution.py:62
  707.4 13.2 %all-gather.9 = f32[4,1,1792]{2,1,0:T(1,128)S(1)} all-gather(f32[1,1,1792]{2,1,0:T(1,128)S(1)} %reshape.531), channel_id=6, replica_groups=mesh['fsdp'=8,'sp'=4] {'sp'}, dimensions={0}, use_global_device_ids=true | all-gather | bytes 35840 | tf_op jit(solution)/shard_map/all_gather | solution.py:66
  785.3 23.7 %all-gather.11 = f32[4,4,9216]{2,1,0:T(4,128)S(1)} all-gather(f32[1,4,9216]{2,1,0:T(4,128)S(1)} %convolution_bitcast_fusion), channel_id=7, replica_groups=mesh['fsdp'=8,'sp'=4] {'sp'}, dimensions={0}, use_global_device_ids=true | all-gather | bytes 737280 | tf_op jit(solution)/shard_map/all_gather | solution.py:66
  809.9 32.6 %all-gather.43.cloned.1.call-done = bf16[2048,768]{1,0:T(8,128)(2,1)} async-done(((bf16[512,768]{1,0:T(8,128)(2,1)}), bf16[2048,768]{1,0:T(8,128)(2,1)}) %all-gather.43.cloned.1.call-update) | async-done | bytes 3145744 | tf_op jit(solution)/shard_map/all_gather | solution.py:54
  860.4 45.7 %reduce-scatter.30.cloned.1.call-done = bf16[192,2048]{1,0:T(8,128)(2,1)} async-done(((bf16[1536,2048]{1,0:T(8,128)(2,1)}), bf16[192,2048]{1,0:T(8,128)(2,1)}) %reduce-scatter.30.cloned.1.call-update) | async-done | bytes 786448 | tf_op jit(solution)/shard_map/reduce_scatter | solution.py:58
  921.1 36.4 %reduce-scatter.22.cloned.1.call-done = bf16[192,1152]{1,0:T(8,128)(2,1)} async-done(((bf16[1536,1152]{1,0:T(8,128)(2,1)}), bf16[192,1152]{1,0:T(8,128)(2,1)}) %reduce-scatter.22.cloned.1.call-update) | async-done | bytes 442384 | tf_op jit(solution)/shard_map/reduce_scatter | solution.py:58
  962.1 44.6 %reduce-scatter.26.cloned.1.call-done = bf16[128,1536]{1,0:T(8,128)(2,1)} async-done(((bf16[1024,1536]{1,0:T(8,128)(2,1)}), bf16[128,1536]{1,0:T(8,128)(2,1)}) %reduce-scatter.26.cloned.1.call-update) | async-done | bytes 393232 | tf_op jit(solution)/shard_map/reduce_scatter | solution.py:58
  1009.4 40.0 %all-reduce.1 = f32[32,288]{1,0:T(8,128)S(1)} all-reduce(f32[32,288]{1,0:T(8,128)S(1)} %reshape.504), channel_id=12, replica_groups=mesh['fsdp'=8,'sp'=4] {'fsdp','sp'}, use_global_device_ids=true, to_apply=%region_36.37.clone | all-reduce | flops 9216 | bytes 73728
  1050.3 69.4 %reduce-scatter.24.cloned.1.call-done = bf16[48,1536]{1,0:T(8,128)(2,1)} async-done(((bf16[1536,1536]{1,0:T(8,128)(2,1)}), bf16[48,1536]{1,0:T(8,128)(2,1)}) %reduce-scatter.24.cloned.1.call-update) | async-done | bytes 147472 | tf_op jit(solution)/shard_map/reduce_scatter | solution.py:58
  1127.3 17.9 %all-gather.45.cloned.1.call-done = f32[8,4,9216]{2,1,0:T(4,128)} async-done(((f32[1,4,9216]{2,1,0:T(4,128)}), f32[8,4,9216]{2,1,0:T(4,128)}) %all-gather.45.cloned.1.call-update) | async-done | bytes 1179664 | tf_op jit(solution)/shard_map/all_gather | solution.py:54
  1151.3 59.0 %reduce-scatter.28.cloned.1.call-done = bf16[128,3072]{1,0:T(8,128)(2,1)} async-done(((bf16[1024,3072]{1,0:T(8,128)(2,1)}), bf16[128,3072]{1,0:T(8,128)(2,1)}) %reduce-scatter.28.cloned.1.call-update) | async-done | bytes 786448
  (512 shorter events, 404.2 us)
Async XLA Ops:
  7.2 76.8 %all-gather.25.cloned.1.call-start = ((), (), s32[]{:S(2)}) async-start(), calls=%async_computation.16 | async-start | bytes 7962624 | tf_op jit(solution)/shard_map/all_gather | solution.py:54
  7.9 103.8 %all-gather.31.cloned.1.call-start = ((), (), s32[]{:S(2)}) async-start(), calls=%async_computation.19 | async-start | bytes 7077888 | tf_op jit(solution)/shard_map/all_gather | solution.py:54
  11.4 144.6 %all-gather.29.cloned.1.call-start = ((), (), s32[]{:S(2)}) async-start(), calls=%async_computation.18 | async-start | bytes 3981312 | tf_op jit(solution)/shard_map/all_gather | solution.py:54
  33.1 75.9 %all-to-all-start.1 = ((bf16[4,128,1024]{1,2,0:T(8,128)(2,1)}), bf16[4,128,1024]{1,2,0:T(8,128)(2,1)S(1)}, u32[]{:S(2)}, u32[]{:S(2)}) async-start(bf16[4,128,1024]{1,2,0:T(8,128)(2,1)} %bitcast.19), calls=%async_computation.1 | async-start | bytes 2097152 | tf_op jit(solution)/shard_map/all_to_all | solution.py:62
  36.6 156.5 %all-gather.27.cloned.1.call-start = ((), (), s32[]{:S(2)}) async-start(), calls=%async_computation.17 | async-start | bytes 2457600 | tf_op jit(solution)/shard_map/all_gather | solution.py:54
  108.8 145.8 %reduce-scatter.14.cloned.1.call-start = ((), (), s32[]{:S(2)}) async-start(), calls=%async_computation.20 | async-start | bytes 3932160 | tf_op jit(solution)/shard_map/reduce_scatter | solution.py:58
  120.1 207.2 %all-gather.33.cloned.1.call-start = ((), (), s32[]{:S(2)}) async-start(), calls=%async_computation.21 | async-start | bytes 4866048 | tf_op jit(solution)/shard_map/all_gather | solution.py:54
  120.7 253.0 %all-gather.37.cloned.1.call-start = ((), (), s32[]{:S(2)}) async-start(), calls=%async_computation.23 | async-start | bytes 7077888 | tf_op jit(solution)/shard_map/all_gather | solution.py:54
  297.3 27.8 %all-to-all-start.2 = ((bf16[4,160,384]{2,1,0:T(8,128)(2,1)}), bf16[4,160,384]{2,1,0:T(8,128)(2,1)}, u32[]{:S(2)}, u32[]{:S(2)}) async-start(bf16[4,160,384]{2,1,0:T(8,128)(2,1)} %copy.246), calls=%async_computation.3 | async-start | bytes 983040 | tf_op jit(solution)/shard_map/all_to_all | solution.py:62
  301.5 117.9 %all-gather.35.cloned.1.call-start = ((), (), s32[]{:S(2)}) async-start(), calls=%async_computation.22 | async-start | bytes 2457600 | tf_op jit(solution)/shard_map/all_gather | solution.py:54
  335.2 117.1 %all-gather.39.cloned.1.call-start = ((), (), s32[]{:S(2)}) async-start(), calls=%async_computation.24 | async-start | bytes 3538944 | tf_op jit(solution)/shard_map/all_gather | solution.py:54
  335.9 161.9 %all-gather.41.cloned.1.call-start = ((), (), s32[]{:S(2)}) async-start(), calls=%async_computation.26 | async-start | bytes 2457600 | tf_op jit(solution)/shard_map/all_gather | solution.py:54
  336.5 220.7 %reduce-scatter.18.cloned.1.call-start = ((), (), s32[]{:S(2)}) async-start(), calls=%async_computation.27 | async-start | bytes 2457600 | tf_op jit(solution)/shard_map/reduce_scatter | solution.py:58
  516.6 83.5 %reduce-scatter.16.cloned.1.call-start = ((), (), s32[]{:S(2)}) async-start(), calls=%async_computation.25 | async-start | bytes 2457600 | tf_op jit(solution)/shard_map/reduce_scatter | solution.py:58
  612.9 162.7 %reduce-scatter.20.cloned.1.call-start = ((), (), s32[]{:S(2)}) async-start(), calls=%async_computation.28 | async-start | bytes 2457600 | tf_op jit(solution)/shard_map/reduce_scatter | solution.py:58
  727.8 114.7 %all-gather.43.cloned.1.call-start = ((), (), s32[]{:S(2)}) async-start(), calls=%async_computation.30 | async-start | bytes 3932160 | tf_op jit(solution)/shard_map/all_gather | solution.py:54
  735.7 170.4 %reduce-scatter.30.cloned.1.call-start = ((), (), s32[]{:S(2)}) async-start(), calls=%async_computation.35 | async-start | bytes 7077888 | tf_op jit(solution)/shard_map/reduce_scatter | solution.py:58
  755.4 202.0 %reduce-scatter.22.cloned.1.call-start = ((), (), s32[]{:S(2)}) async-start(), calls=%async_computation.29 | async-start | bytes 3981312 | tf_op jit(solution)/shard_map/reduce_scatter | solution.py:58
  763.3 243.5 %reduce-scatter.26.cloned.1.call-start = ((), (), s32[]{:S(2)}) async-start(), calls=%async_computation.32 | async-start | bytes 3538944 | tf_op jit(solution)/shard_map/reduce_scatter | solution.py:58
  770.3 349.4 %reduce-scatter.24.cloned.1.call-start = ((), (), s32[]{:S(2)}) async-start(), calls=%async_computation.31 | async-start | bytes 4866048 | tf_op jit(solution)/shard_map/reduce_scatter | solution.py:58
  775.4 369.9 %all-gather.45.cloned.1.call-start = ((), (), s32[]{:S(2)}) async-start(), calls=%async_computation.33 | async-start | bytes 1327104 | tf_op jit(solution)/shard_map/all_gather | solution.py:54
  809.8 400.5 %reduce-scatter.28.cloned.1.call-start = ((), (), s32[]{:S(2)}) async-start(), calls=%async_computation.34 | async-start | bytes 7077888
  906.1 51.3 %all-to-all-start.6 = ((bf16[4,48,2048]{2,1,0:T(8,128)(2,1)}), bf16[4,48,2048]{2,1,0:T(8,128)(2,1)S(1)}, u32[]{:S(2)}, u32[]{:S(2)}) async-start(bf16[4,48,2048]{2,1,0:T(8,128)(2,1)} %bitcast.211), calls=%async_computation.12 | async-start | bytes 1572864 | tf_op jit(solution)/shard_map/all_to_all | solution.py:62
  957.4 167.7 %all-to-all-start.5 = ((bf16[4,48,1152]{2,1,0:T(8,128)(2,1)}), bf16[4,48,1152]{2,1,0:T(8,128)(2,1)S(1)}, u32[]{:S(2)}, u32[]{:S(2)}) async-start(bf16[4,48,1152]{2,1,0:T(8,128)(2,1)} %bitcast.217), calls=%async_computation.10 | async-start | bytes 884736 | tf_op jit(solution)/shard_map/all_to_all | solution.py:62
  (122 other events, 1404.5 us)
Sparse Core Ops, SparseCore 0:
  9.9 52.1 all-gather.24
  64.5 47.1 all-gather.30
  113.6 33.8 all-gather.28
  149.5 43.4 all-gather.26
  195.2 59.4 reduce-scatter.13
  257.3 69.9 all-gather.32
  329.2 44.4 all-gather.36
  375.8 43.4 all-gather.34
  421.2 31.0 all-gather.38
  454.3 43.4 all-gather.40
  516.7 40.4 reduce-scatter.17
  559.3 40.6 reduce-scatter.15
  727.8 40.6 reduce-scatter.19
  770.6 71.8 all-gather.42
  845.7 60.4 reduce-scatter.29
  909.5 47.9 reduce-scatter.21
  960.7 46.0 reduce-scatter.25
  1012.1 107.6 reduce-scatter.23
  1122.2 23.0 all-gather.44
  1148.5 61.7 reduce-scatter.27

commit v2 on v1

v2 whole, which is shorter than its diff:
```python
import functools
import math

import jax
import jax.numpy as jnp
from jax import lax
from jax.experimental import pallas as pl
from jax.experimental.pallas import tpu as pltpu
from jax.sharding import PartitionSpec as P

H = 24
HD = 64
CPG = 4
CAP = 128

HIGHEST = lax.Precision.HIGHEST
EPSILON = 1e-06
NEGATIVE = -1e30
BF16 = jnp.bfloat16
F32 = jnp.float32


def norm_modulate(values, gain, scale, shift):
    root = lax.rsqrt(jnp.mean(values * values, axis=-1, keepdims=True) + EPSILON)
    return values * root * gain * (1.0 + scale) + shift


def partner(values):
    half = HD // 2
    width = values.shape[1]
    column = lax.broadcasted_iota(jnp.int32, values.shape, 1) % HD
    ahead = jnp.concatenate([values[:, half:], values[:, :half]], axis=1)
    behind = jnp.concatenate([values[:, width - half :], values[:, : width - half]], axis=1)
    return jnp.where(column < half, ahead, behind)


def softmax_rows(scores):
    top = jnp.max(scores, axis=-1, keepdims=True)
    expo = jnp.exp(scores - top)
    return expo / jnp.sum(expo, axis=-1, keepdims=True)


def product(left, right):
    return jnp.dot(left, right, preferred_element_type=F32)


def left_product(left, right):
    return lax.dot_general(left, right, (((0,), (0,)), ((), ())), preferred_element_type=F32)


def right_product(left, right):
    return lax.dot_general(left, right, (((1,), (1,)), ((), ())), preferred_element_type=F32)


def gather(values):
    return lax.all_gather(values, "fsdp", axis=0, tiled=True)


def scatter(values):
    return lax.psum_scatter(values, "fsdp", scatter_dimension=0, tiled=True)


def shift(values, axis, step):
    size = lax.axis_size(axis)
    return lax.ppermute(values, axis, [(k, (k + step) % size) for k in range(size)])


def tie(*values):
    return lax.optimization_barrier(values)


def push_kernel(axis, size, block, spot, values, result, send_sems, receive_sems):
    me = lax.axis_index(axis)
    barrier = pltpu.get_barrier_semaphore()
    for step in range(1, size):
        pl.semaphore_signal(
            barrier,
            inc=1,
            device_id={axis: lax.rem(me + step, size)},
            device_id_type=pl.DeviceIdType.MESH,
        )
    pl.semaphore_wait(barrier, size - 1)

    def copy(step, place):
        to = lax.rem(me + step, size)
        return pltpu.make_async_remote_copy(
            src_ref=values if block is None else values.at[block(to, step)],
            dst_ref=result.at[place],
            send_sem=send_sems.at[step],
            recv_sem=receive_sems.at[step],
            device_id={axis: to},
            device_id_type=pl.DeviceIdType.MESH,
        )

    for step in range(1, size):
        copy(step, spot(me, step)).start()
    result[spot(me, 0)] = values[...] if block is None else values[block(me, 0)]
    for step in range(1, size):
        origin = lax.rem(me + size - step, size)
        copy(step, spot(origin, step)).wait()


def push(values, axis, block, spot, collective):
    size = lax.axis_size(axis)
    shape = values.shape if block is None else values.shape[1:]
    return pl.pallas_call(
        functools.partial(push_kernel, axis, size, block, spot),
        out_shape=jax.ShapeDtypeStruct((size,) + shape, values.dtype),
        in_specs=[pl.BlockSpec(memory_space=pltpu.VMEM)],
        out_specs=pl.BlockSpec(memory_space=pltpu.VMEM),
        scratch_shapes=[
            pltpu.SemaphoreType.DMA((size,)),
            pltpu.SemaphoreType.DMA((size,)),
        ],
        compiler_params=pltpu.CompilerParams(collective_id=collective, has_side_effects=True),
        name="push_%d" % collective,
    )(values)


def push_gather(values, axis, collective):
    return push(values, axis, None, lambda me, step: me, collective)


def push_blocks(stack, axis, collective):
    return push(stack, axis, lambda to, step: to, lambda me, step: me, collective)


def pick(stack, index):
    return lax.dynamic_index_in_dim(stack, index, axis=0, keepdims=False)


def spread(values, axis):
    return [values] + [shift(values, axis, s) for s in range(1, lax.axis_size(axis))]


def send(stack, axis):
    size, place = lax.axis_size(axis), lax.axis_index(axis)
    return [pick(stack, place)] + [
        shift(pick(stack, (place + s) % size), axis, s) for s in range(1, size)
    ]


def send_turned(stack):
    return [stack[0]] + [shift(stack[s], "sp", -s) for s in range(1, lax.axis_size("sp"))]


def ordered(blocks, axis, dimension, ahead=False):
    size, place = lax.axis_size(axis), lax.axis_index(axis)
    stack = jnp.stack(blocks)
    spot = lambda b: (b - place) % size if ahead else (place - b) % size
    return jnp.concatenate([pick(stack, spot(b)) for b in range(size)], axis=dimension)


def gather_turned(values):
    return jnp.concatenate(spread(values, "sp"), axis=0)


def total(blocks):
    result = blocks[0].astype(F32)
    for block in blocks[1:]:
        result = result + block.astype(F32)
    return result


def turned_blocks(values):
    sp = lax.axis_size("sp")
    return send_turned(values.reshape(sp, values.shape[0] // sp, values.shape[1]))


def small_sum(values):
    return total(spread(values, "sp"))


def turned_sums(parts, collective):
    sp = lax.axis_size("sp")
    count = sum(part.shape[0] for part in parts)
    lines = jnp.concatenate(parts).reshape(count // 128, 128)
    blocks = push(lines, "sp", None, lambda me, step: step, collective)
    blocks = [blocks[s].reshape(count) for s in range(sp)]
    results, begin = [], 0
    for part in parts:
        count = part.shape[0]
        results.append(
            total(
                [
                    jnp.roll(block[begin : begin + count], s * (count // sp))
                    for s, block in enumerate(blocks)
                ]
            )
        )
        begin += count
    return results


def body(
    tokens,
    condition,
    caption,
    clip_lengths,
    caption_lengths,
    positions,
    ada_weight,
    ada_bias,
    attention_gain,
    qkv_weight,
    query_gain,
    key_gain,
    text_key_weight,
    text_key_gain,
    text_value_weight,
    cross_gate,
    out_weight,
    feedforward_gain,
    gate_weight,
    up_weight,
    down_weight,
    out_grad,
):
    sp = lax.axis_size("sp")
    fsdp = lax.axis_size("fsdp")
    sp_place = lax.axis_index("sp")
    place = lax.axis_index("fsdp") * sp + sp_place
    rows, dim = tokens.shape
    seq = sp * rows
    heads = H // sp
    local = heads * HD
    wrows = qkv_weight.shape[0]
    hidden_dim = gate_weight.shape[1]
    hcols = hidden_dim // (fsdp * sp)
    hlocal = hidden_dim // sp
    text_dim = caption.shape[1]
    tcols = text_dim // (fsdp * sp)
    caps = caption.shape[0] * sp
    bias_rows = ada_bias.shape[0]

    columns = lambda weight, parts: (
        weight.reshape(weight.shape[0], parts, sp, weight.shape[1] // (parts * sp))
        .transpose(2, 0, 1, 3)
        .reshape(sp, weight.shape[0], weight.shape[1] // sp)
    )
    tokens_all = gather_turned(tokens)
    qkv_full = gather(ordered(send(columns(qkv_weight, 3), "sp"), "sp", 0))
    down_full = gather(down_weight)

    silu_cond = jax.nn.silu(condition.astype(F32)).astype(BF16)
    cond_all = lax.all_gather(silu_cond, "fsdp", axis=0)
    cond_rows = lax.dynamic_slice_in_dim(cond_all, place * wrows, wrows, axis=2)
    small = jnp.concatenate(
        [
            ada_bias,
            attention_gain,
            query_gain,
            key_gain,
            text_key_gain,
            cross_gate,
            feedforward_gain,
        ]
    ).astype(F32)
    small_size = small.shape[0]
    wide = lambda values, width: jnp.pad(values, ((0, 0), (0, width - values.shape[1])))
    rounded = lambda width: -(-width // 128) * 128
    partial = product(cond_rows.reshape(fsdp * CPG, wrows), ada_weight)
    partial = partial.reshape(fsdp, CPG, 6 * dim)
    small_rows = wide(small.reshape(8, small_size // 8), rounded(small_size // 8))
    pieces = jnp.concatenate(
        [
            jnp.concatenate([partial[:, :, : 3 * dim], partial[:, :, 3 * dim :]], axis=1),
            jnp.broadcast_to(small_rows[None], (fsdp,) + small_rows.shape),
        ],
        axis=2,
    )
    arrived = push_blocks(pieces, "fsdp", 0)
    small_group = arrived[:, :, 3 * dim : 3 * dim + small_size // 8].reshape(8, -1)
    group_size = small_group.shape[1]
    bundles = push_gather(
        jnp.concatenate(
            [
                jnp.sum(arrived[:, :, : 3 * dim], axis=0),
                wide(small_group, rounded(group_size)),
            ],
            axis=1,
        ),
        "sp",
        1,
    )
    small_all = (
        bundles[:, :, 3 * dim : 3 * dim + group_size]
        .reshape(sp, fsdp, small_size)
        .transpose(1, 0, 2)
        .reshape(fsdp * sp, small_size)
    )
    bias_full = small_all[:, :bias_rows].reshape(-1)
    gains_full = [
        small_all[:, bias_rows + k * wrows : bias_rows + (k + 1) * wrows].reshape(-1)
        for k in range(6)
    ]
    attention_full, query_full, key_full, text_full, cross_full, feedforward_full = gains_full
    mine = lambda vector: lax.dynamic_slice_in_dim(vector, sp_place * local, local)[None]
    query_mine, key_mine, text_mine = mine(query_full), mine(key_full), mine(text_full)
    gate_tanh = jnp.tanh(mine(cross_full))
    modulation = jnp.sum(bundles[:, :, : 3 * dim], axis=0)
    modulation = jnp.concatenate([modulation[:CPG], modulation[CPG:]], axis=1) + bias_full[None]

    modulation, caption, text_key_weight, text_value_weight = tie(
        modulation, caption, text_key_weight, text_value_weight
    )

    text_full_weight = gather(
        ordered(
            send(
                jnp.concatenate(
                    [columns(text_key_weight, 1), columns(text_value_weight, 1)], axis=2
                ),
                "sp",
            ),
            "sp",
            0,
        )
    )
    first = text_dim // 4
    caption_first = gather_turned(caption[:, :first])

    lengths = clip_lengths[0]
    ends = jnp.cumsum(lengths)
    token = jnp.arange(seq, dtype=jnp.int32)
    token = (sp_place - token // rows) % sp * rows + token % rows
    group_clip = jnp.sum((token[:, None] >= ends[None, :]).astype(jnp.int32), axis=1)
    slot = jnp.arange(CPG, dtype=jnp.int32)[None, :]
    group_hot = group_clip[:, None] == slot
    group_place = token - jnp.sum(jnp.where(group_hot, (ends - lengths)[None, :], 0), axis=1)
    token_clip = group_clip[:rows]
    one_hot = (token_clip[:, None] == slot).astype(F32)

    def token_mod(k, clips):
        piece = modulation[:, k * dim : (k + 1) * dim]
        value = piece[0:1]
        for c in range(1, CPG):
            value = jnp.where(clips[:, None] == c, piece[c : c + 1], value)
        return value

    shift_one, scale_one, gate_one, shift_two, scale_two, gate_two = [
        token_mod(k, token_clip) for k in range(6)
    ]

    values = tokens.astype(F32)
    normed_one_all = norm_modulate(
        tokens_all.astype(F32),
        attention_full[None],
        token_mod(1, group_clip),
        token_mod(0, group_clip),
    ).astype(BF16)
    projected = product(normed_one_all, qkv_full)
    q_raw, k_raw, v_raw = (
        projected[:, :local],
        projected[:, local : 2 * local],
        projected[:, 2 * local :],
    )
    qk_squares = turned_sums([jnp.sum(q_raw * q_raw, axis=1), jnp.sum(k_raw * k_raw, axis=1)], 2)
    *qk_squares, caption_rest, gate_weight, up_weight, out_weight = tie(
        *qk_squares, caption[:, first:], gate_weight, up_weight, out_weight
    )
    out_full = gather(ordered(spread(out_weight, "sp"), "sp", 0))
    gate_up_full = gather(
        ordered(
            send(
                jnp.concatenate([columns(gate_weight, fsdp), columns(up_weight, fsdp)], axis=2),
                "sp",
            ),
            "sp",
            0,
        )
    )
    gate_full, up_full = gate_up_full[:, :hlocal], gate_up_full[:, hlocal:]
    caption_rest = gather_turned(caption_rest)
    q_root = lax.rsqrt(qk_squares[0] / dim + EPSILON)[:, None]
    k_root = lax.rsqrt(qk_squares[1] / dim + EPSILON)[:, None]
    half = HD // 2
    freqs = jnp.exp(jnp.arange(half, dtype=F32) * (-math.log(10000.0) / half))
    angles = group_place.astype(F32)[:, None] * freqs[None, :]
    cosine = jnp.tile(jnp.cos(angles), (1, 2 * heads))
    sine_half = jnp.sin(angles)
    sine = jnp.tile(jnp.concatenate([-sine_half, sine_half], axis=1), (1, heads))
    rotate = lambda v: v * cosine + partner(v) * sine
    rotate_back = lambda v: v * cosine - partner(v) * sine
    split_heads = lambda v: v.reshape(v.shape[0], heads, HD)
    query = split_heads(rotate(q_raw * q_root * query_mine).astype(BF16))
    key = split_heads(rotate(k_raw * k_root * key_mine).astype(BF16))
    value = split_heads(v_raw.astype(BF16))

    text_both = product(caption_first, text_full_weight[:first]) + product(
        caption_rest, text_full_weight[first:]
    )
    tkey_raw = text_both[:, :local]
    (tk_squares,) = turned_sums([jnp.sum(tkey_raw * tkey_raw, axis=1)], 3)
    tk_squares, out_grad_late = tie(tk_squares, out_grad)
    out_grad_all = gather_turned(out_grad_late)
    tk_root = lax.rsqrt(tk_squares / dim + EPSILON)[:, None]
    tkey = split_heads((tkey_raw * tk_root * text_mine).astype(BF16))
    tvalue = split_heads(text_both[:, local:].astype(BF16))

    scale = HD**-0.5
    caption_row = jnp.arange(caps, dtype=jnp.int32)
    caption_row = (sp_place - caption_row // caption.shape[0]) % sp * caption.shape[
        0
    ] + caption_row % caption.shape[0]
    caption_clip = caption_row // CAP
    caption_limit = jnp.sum(
        jnp.where(caption_clip[:, None] == slot, caption_lengths[None, :], 0), axis=1
    )
    caption_live = caption_row % CAP < caption_limit
    same_clip = (group_clip[:, None] == group_clip[None, :])[None]
    cross_ok = ((group_clip[:, None] == caption_clip[None, :]) & caption_live[None, :])[None]
    to_scores = lambda a, b: jnp.einsum("qhd,khd->hqk", a, b, preferred_element_type=F32)
    to_rows = lambda a, b: jnp.einsum("hqk,khd->qhd", a, b, preferred_element_type=F32)
    to_cols = lambda a, b: jnp.einsum("hqk,qhd->khd", a, b, preferred_element_type=F32)
    self_prob = softmax_rows(jnp.where(same_clip, to_scores(query, key) * scale, NEGATIVE))
    cross_prob = softmax_rows(jnp.where(cross_ok, to_scores(query, tkey) * scale, NEGATIVE))
    self_low = self_prob.astype(BF16)
    cross_low = cross_prob.astype(BF16)
    cross_out = to_rows(cross_low, tvalue).reshape(seq, local)
    mixed_heads = (
        to_rows(self_low, value).reshape(seq, local) + gate_tanh * cross_out
    ).astype(BF16)
    mixed = push(
        mixed_heads.reshape(sp, rows, local),
        "sp",
        lambda to, step: (sp - step) % sp,
        lambda me, step: me,
        5,
    )
    mixed = mixed.transpose(1, 0, 2).reshape(rows, dim)
    attended = product(mixed, out_full)
    middle = values + gate_one * attended

    normed_two = norm_modulate(middle, feedforward_full[None], scale_two, shift_two).astype(BF16)
    normed_two_all = gather_turned(normed_two)
    grad_top = out_grad.astype(F32)
    grad_ffn_all = (token_mod(5, group_clip) * out_grad_all.astype(F32)).astype(BF16)
    gate_act = product(normed_two_all, gate_full)
    up_act = product(normed_two_all, up_full)
    sigmoid = jax.nn.sigmoid(gate_act)
    hidden = (gate_act * sigmoid * up_act).astype(BF16)
    grad_hidden = right_product(grad_ffn_all, down_full)
    grad_gate_act = (grad_hidden * up_act * sigmoid * (1.0 + gate_act * (1.0 - sigmoid))).astype(
        BF16
    )
    grad_up_act = (grad_hidden * gate_act * sigmoid).astype(BF16)
    grad_normed_blocks = turned_blocks(
        (right_product(grad_gate_act, gate_full) + right_product(grad_up_act, up_full)).astype(
            BF16
        )
    )
    gate_up_terms = jnp.concatenate(
        [
            left_product(normed_two_all, grad_gate_act).astype(BF16),
            left_product(normed_two_all, grad_up_act).astype(BF16),
        ],
        axis=1,
    )
    down_terms = left_product(hidden, grad_ffn_all).astype(BF16)
    gate_up_rows = scatter(gate_up_terms)
    down_rows = scatter(down_terms)
    *grad_normed_blocks, unused_gate_up, unused_down = tie(
        *grad_normed_blocks, gate_up_terms, down_terms
    )
    grad_normed_two = total(grad_normed_blocks)
    unused_two, pull_two = jax.vjp(
        norm_modulate, middle, feedforward_full[None], scale_two, shift_two
    )
    grad_middle_norm, feedforward_grad, grad_scale_two, grad_shift_two = pull_two(grad_normed_two)
    grad_middle = grad_top + grad_middle_norm
    grad_gate_one = grad_middle * attended
    grad_attended = (gate_one * grad_middle).astype(BF16)
    out_terms = left_product(mixed, grad_attended).astype(BF16)
    out_rows = scatter(out_terms)
    grad_mixed = right_product(grad_attended, out_full).astype(BF16)
    grad_flat = push(
        grad_mixed.reshape(rows, sp, local).transpose(1, 0, 2),
        "sp",
        lambda to, step: to,
        lambda me, step: step,
        6,
    ).reshape(seq, local)

    grad_flat, hidden, unused_out = tie(grad_flat, hidden, out_terms)
    ffn_out = total(turned_blocks(product(hidden, down_full).astype(BF16)))
    output = middle + gate_two * ffn_out
    grad_gate_two = grad_top * ffn_out

    grad_heads = split_heads(grad_flat)
    gate_local = (1.0 - gate_tanh * gate_tanh)[0] * jnp.sum(
        grad_flat.astype(F32) * cross_out, axis=0
    )
    cross_grad = split_heads((gate_tanh * grad_flat.astype(F32)).astype(BF16))
    grad_cross = to_scores(cross_grad, tvalue)
    cscore_grad = (
        cross_prob * (grad_cross - jnp.sum(cross_prob * grad_cross, axis=-1, keepdims=True))
    ).astype(BF16)
    low = lambda v: v.astype(BF16).reshape(v.shape[0], local).astype(F32)
    tkey_back = low(to_cols(cscore_grad, query) * scale)
    tvalue_back = to_cols(cross_low, cross_grad).astype(BF16).reshape(caps, local)
    gate_up_rows, tkey_back, tvalue_back, grad_heads = tie(
        gate_up_rows, tkey_back, tvalue_back, grad_heads
    )
    grad_self = to_scores(grad_heads, value)
    score_grad = (
        self_prob * (grad_self - jnp.sum(self_prob * grad_self, axis=-1, keepdims=True))
    ).astype(BF16)
    query_back = low((to_rows(score_grad, key) + to_rows(cscore_grad, tkey)) * scale)
    key_back = low(to_cols(score_grad, query) * scale)
    value_back = to_cols(self_low, grad_heads).astype(BF16).reshape(seq, local)
    down_rows, query_back, key_back = tie(down_rows, query_back, key_back)
    down_shard = down_rows.astype(F32)
    gate_up_back = [
        block.reshape(wrows, 2, fsdp, 1, hcols)
        for block in send(gate_up_rows.reshape(sp, wrows, 2 * hlocal), "sp")
    ]
    gate_up_back = (
        ordered(gate_up_back, "sp", 3)
        .transpose(1, 0, 2, 3, 4)
        .reshape(2, wrows, hidden_dim)
        .astype(F32)
    )


    query_turn = rotate_back(query_back)
    key_turn = rotate_back(key_back)
    q_dots, k_dots, tk_dots = [
        dot[:, None]
        for dot in turned_sums(
            [
                jnp.sum(query_turn * query_mine * q_raw, axis=1),
                jnp.sum(key_turn * key_mine * k_raw, axis=1),
                jnp.sum(tkey_back * text_mine * tkey_raw, axis=1),
            ],
            4,
        )
    ]

    def norm_back(grad, raw, root, gain, dot):
        raw_grad = root * gain * grad - raw * (root * root * root * dot / dim)
        return raw_grad.astype(BF16), jnp.sum(grad * raw * root, axis=0)

    grad_q, query_gain_grad = norm_back(query_turn, q_raw, q_root, query_mine, q_dots)
    grad_k, key_gain_grad = norm_back(key_turn, k_raw, k_root, key_mine, k_dots)
    grad_tk, text_gain_grad = norm_back(tkey_back, tkey_raw, tk_root, text_mine, tk_dots)
    grad_projected = jnp.concatenate([grad_q, grad_k, value_back], axis=1)
    grad_normed_blocks = turned_blocks(right_product(grad_projected, qkv_full).astype(BF16))
    qkv_terms = left_product(normed_one_all, grad_projected).astype(BF16)
    qkv_rows = scatter(qkv_terms)
    qkv_back = [
        block.reshape(wrows, 3, 1, local)
        for block in send(qkv_rows.reshape(sp, wrows, 3 * local), "sp")
    ]
    qkv_shard = ordered(qkv_back, "sp", 2).reshape(wrows, 3 * dim).astype(F32)
    text_grads = jnp.concatenate([grad_tk, tvalue_back], axis=1)
    text_terms = jnp.concatenate(
        [
            left_product(caption_first, text_grads).astype(BF16),
            left_product(caption_rest, text_grads).astype(BF16),
        ],
        axis=0,
    )
    text_rows = scatter(text_terms)
    *grad_normed_blocks, unused_qkv, unused_text, out_rows = tie(
        *grad_normed_blocks, qkv_terms, text_terms, out_rows
    )
    out_shard = total(send(out_rows.reshape(sp, wrows, dim), "sp"))
    grad_normed_one = total(grad_normed_blocks)
    text_back = [
        block.reshape(tcols, 2, 1, local)
        for block in send(text_rows.reshape(sp, tcols, 2 * local), "sp")
    ]
    text_shard = ordered(text_back, "sp", 2).astype(F32)
    text_key_shard = text_shard[:, 0].reshape(tcols, dim)
    text_value_shard = text_shard[:, 1].reshape(tcols, dim)

    unused_one, pull_one = jax.vjp(
        norm_modulate, values, attention_full[None], scale_one, shift_one
    )
    grad_tokens_norm, attention_grad, grad_scale_one, grad_shift_one = pull_one(grad_normed_one)
    tokens_grad = grad_middle + grad_tokens_norm

    by_clip = lambda grads: lax.dot_general(
        one_hot,
        jnp.concatenate(grads, axis=1),
        (((0,), (0,)), ((), ())),
        precision=HIGHEST,
        preferred_element_type=F32,
    )
    sums = by_clip(
        [
            grad_shift_one,
            grad_scale_one,
            grad_gate_one,
            grad_shift_two,
            grad_scale_two,
            grad_gate_two,
        ]
    )
    gains_wide = jnp.concatenate([attention_grad, feedforward_grad], axis=1).reshape(8, dim // 4)
    gains_heads = jnp.concatenate(
        [query_gain_grad, key_gain_grad, text_gain_grad, gate_local]
    ).reshape(8, local // 2)
    sent = jnp.concatenate(
        [
            jnp.concatenate([sums[:, : 3 * dim], sums[:, 3 * dim :]], axis=0),
            gains_wide,
            wide(gains_heads, rounded(local // 2)),
        ],
        axis=1,
    )
    blocks = push_gather(sent, "sp", 7)
    summed = jnp.sum(blocks[:, :, : 3 * dim + dim // 4], axis=0)
    heads_rows = (
        blocks[:, :, 3 * dim + dim // 4 : 3 * dim + dim // 4 + local // 2]
        .reshape(sp, 4, local)
        .transpose(1, 0, 2)
        .reshape(8, dim // 2)
    )
    gathered = push_gather(jnp.concatenate([summed, heads_rows], axis=1), "fsdp", 8)
    half_one = gathered[:, :CPG, : 3 * dim].reshape(fsdp * CPG, 3 * dim)
    half_two = gathered[:, CPG:, : 3 * dim].reshape(fsdp * CPG, 3 * dim)
    gain_sums = jnp.sum(gathered[:, :, 3 * dim :], axis=0)
    wide_sums = gain_sums[:, : dim // 4].reshape(2, dim)
    heads_sums = gain_sums[:, dim // 4 :].reshape(4, dim)
    cond_flat = cond_rows.reshape(fsdp * CPG, wrows).astype(F32)
    ada_grad = lambda rows_all: lax.dot_general(
        cond_flat,
        rows_all,
        (((0,), (0,)), ((), ())),
        precision=HIGHEST,
        preferred_element_type=F32,
    )
    ada_shard = jnp.concatenate([ada_grad(half_one), ada_grad(half_two)], axis=1)
    bias_shard = lax.dynamic_slice_in_dim(
        jnp.concatenate([jnp.sum(half_one, axis=0), jnp.sum(half_two, axis=0)]),
        place * bias_rows,
        bias_rows,
    )
    own = lambda vector: lax.dynamic_slice_in_dim(vector, place * wrows, wrows)
    attention_shard, feedforward_shard = own(wide_sums[0]), own(wide_sums[1])
    query_shard, key_shard, text_gain_shard, cross_shard = [own(heads_sums[k]) for k in range(4)]
    return (
        output.astype(BF16),
        tokens_grad,
        ada_shard,
        bias_shard,
        attention_shard,
        qkv_shard,
        query_shard,
        key_shard,
        text_key_shard,
        text_gain_shard,
        text_value_shard,
        cross_shard,
        out_shard,
        feedforward_shard,
        gate_up_back[0],
        gate_up_back[1],
        down_shard,
    )


def solution(mesh):
    return jax.shard_map(
        body,
        mesh=mesh,
        in_specs=(
            P(("fsdp", "sp"), None),
            P("fsdp", None),
            P(("fsdp", "sp"), None),
            P("fsdp", None),
            P("fsdp"),
            P(("fsdp", "sp")),
            P(("fsdp", "sp"), None),
            P(("fsdp", "sp")),
            P(("fsdp", "sp")),
            P(("fsdp", "sp"), None),
            P(("fsdp", "sp")),
            P(("fsdp", "sp")),
            P(("fsdp", "sp"), None),
            P(("fsdp", "sp")),
            P(("fsdp", "sp"), None),
            P(("fsdp", "sp")),
            P(("fsdp", "sp"), None),
            P(("fsdp", "sp")),
            P(("fsdp", "sp"), None),
            P(("fsdp", "sp"), None),
            P(("fsdp", "sp"), None),
            P(("fsdp", "sp"), None),
        ),
        out_specs=(
            P(("fsdp", "sp"), None),
            P(("fsdp", "sp"), None),
            P(("fsdp", "sp"), None),
            P(("fsdp", "sp")),
            P(("fsdp", "sp")),
            P(("fsdp", "sp"), None),
            P(("fsdp", "sp")),
            P(("fsdp", "sp")),
            P(("fsdp", "sp"), None),
            P(("fsdp", "sp")),
            P(("fsdp", "sp"), None),
            P(("fsdp", "sp")),
            P(("fsdp", "sp"), None),
            P(("fsdp", "sp")),
            P(("fsdp", "sp"), None),
            P(("fsdp", "sp"), None),
            P(("fsdp", "sp"), None),
        ),
        check_vma=False,
    )
```

time: 1230 us -> 892 us (0.73)
  waiting for transfers between devices: 622 us -> 177 us
  blocking collectives: 217 us -> 9.25 us
  Pallas kernels: 0 us -> 156 us
  starting transfers between devices: 22.8 us -> 146 us
  other arithmetic: 77 us -> 99.5 us
  local copies, waits for them, and re-layouts: 105 us -> 119 us
    reduce_scatter x8 -> x4, waiting for transfers between devices: 282 us -> 0.03 us  [scatter(): return lax.psum_scatter(values, 'fsdp', scatter_dimension=0, tiled=True)]
    all_gather x11 -> x5, waiting for transfers between devices: 241 us -> 0.05 us  [gather(): return lax.all_gather(values, 'fsdp', axis=0, tiled=True)]
    ppermute x0 -> x48, waiting for transfers between devices: none -> 177 us  [shift(): lax.ppermute(values, axis, [(k, (k + step) % size) for k in range(size)])]
    pallas_call x0 -> x9, Pallas kernels: none -> 156 us  [push(): pl.pallas_call(functools.partial(push_kernel, axis, size, block, spot), o...]
    ppermute x0 -> x48, starting transfers between devices: none -> 144 us  [shift(): lax.ppermute(values, axis, [(k, (k + step) % size) for k in range(size)])]
    unnamed x2 -> x0, blocking collectives: 85.1 us -> none
    all_gather x6 -> x1, blocking collectives: 88.3 us -> 9.25 us  [body(): cond_all = lax.all_gather(silu_cond, 'fsdp', axis=0)]
    unnamed x21 -> x11, waiting for transfers between devices: 61.7 us -> 0.69 us
  transfers between devices with their start and end apart: 25 -> 58, of which waited for: 19 -> 20; matrix products, arithmetic and copies ran while one was open for 18% -> 37% of each run, Pallas kernels for 0% -> 18%
where the time goes in v2:
time: 892 us; the launch traced here: 882 us
  waiting for transfers between devices  177 us (20%)
  matrix products  157 us (18%)
  Pallas kernels  156 us (17%)
  starting transfers between devices  146 us (16%)
  local copies, waits for them, and re-layouts  119 us (13%)
  other arithmetic  99.5 us (11%)
  between operations  17.5 us (2%)
  blocking collectives  9.25 us (1%)
    ppermute x48, waiting for transfers between devices, shift(): lax.ppermute(values, axis, [(k, (k + step) % size) for k in range(size)])  177 us
    pallas_call x9, Pallas kernels, push(): pl.pallas_call(functools.partial(push_kernel, axis, size, block, spot), o...  156 us
    ppermute x48, starting transfers between devices, shift(): lax.ppermute(values, axis, [(k, (k + step) % size) for k in range(size)])  144 us
    dot_general x8, matrix products, product(): return jnp.dot(left, right, preferred_element_type=F32)  33.6 us
    unnamed x312, local copies, waits for them, and re-layouts  32.6 us
    dot_general x7, matrix products, left_product(): lax.dot_general(left, right, (((0,), (0,)), ((), ())), preferred_element_...  29.7 us
    dot_general x5, matrix products, right_product(): lax.dot_general(left, right, (((1,), (1,)), ((), ())), preferred_element_...  22.3 us
    dot_general x4, matrix products, body(): jnp.einsum('hqk,qhd->khd', a, b, preferred_element_type=F32)  20 us
  transfers between devices with their start and end apart: 58, of which 20 were waited for; matrix products, arithmetic and copies ran while one was open for 37% of the time, Pallas kernels for 18%

profile of v2, /device:TPU:0, one launch (start us, length us, event | category | flops | bytes accessed | tf_op | source)
XLA Modules:
  0.0 881.7 jit_solution(13353532096939209447)
XLA Ops:
  15.3 9.2 %all-gather.1 = bf16[8,4,1536]{2,1,0:T(4,128)(2,1)S(1)} all-gather(bf16[1,4,1536]{2,1,0:T(4,128)(2,1)S(1)} %fusion.95), channel_id=2, replica_groups=mesh['fsdp'=8,'sp'=4] {'fsdp'}, dimensions={0}, use_global_device_ids=true | all-gather | bytes 110592 | tf_op jit(solution)/shard_map/all_gather | solution.py:246
  28.3 22.3 %push_0.1 = f32[8,8,4736]{2,1,0:T(8,128)} custom-call(f32[8,8,4736]{2,1,0:T(8,128)} %pad_maximum_fusion.6.values), custom_call_target="tpu_custom_call" | custom-call | tf_op jit(solution)/shard_map/push_0/pallas_call | solution.py:106
  53.5 18.1 %push_1.1 = f32[4,8,5248]{2,1,0:T(8,128)} custom-call(f32[8,5248]{1,0:T(8,128)} %select_maximum_fusion.values), custom_call_target="tpu_custom_call" | custom-call | tf_op jit(solution)/shard_map/push_1/pallas_call | solution.py:106
  84.3 8.7 collective-permute-done.10
  113.9 20.5 %collective-permute-done.1 = bf16[160,1536]{1,0:T(8,128)(2,1)S(1)} collective-permute-done((bf16[160,1536]{1,0:T(8,128)(2,1)S(1)}, bf16[160,1536]{1,0:T(8,128)(2,1)S(1)}, u32[]{:S(2)}, u32[]{:S(2)}) %collective-permute-start.1) | collective-permute-done | bytes 491552 | tf_op jit(solution)/shard_map/ppermute | solution.py:65
  135.3 7.8 fusion.13
  151.1 16.2 %push_2.1 = f32[4,10,128]{2,1,0:T(8,128)} custom-call(f32[10,128]{1,0:T(8,128)} %pad_maximum_fusion.27.values), custom_call_target="tpu_custom_call" | custom-call | tf_op jit(solution)/shard_map/push_2/pallas_call | solution.py:106
  208.9 10.5 %collective-permute-start.12 = (bf16[128,3072]{1,0:T(8,128)(2,1)}, bf16[128,3072]{1,0:T(8,128)(2,1)}, u32[]{:S(2)}, u32[]{:S(2)}) collective-permute-start(bf16[128,3072]{1,0:T(8,128)(2,1)} %slice.722), channel_id=1, source_target_pairs={{0,1},{1,2},{2,3},{3,0},{4,5},{5,6},{6,7},{7,4},{8,9},{9,10},{10,1... | collective-permute-start | bytes 2359304 | tf_op jit(solution)/shard_map/ppermute | solution.py:65
  219.4 32.8 %collective-permute-done.25 = bf16[48,2048]{1,0:T(8,128)(2,1)S(1)} collective-permute-done((bf16[48,2048]{1,0:T(8,128)(2,1)S(1)}, bf16[48,2048]{1,0:T(8,128)(2,1)S(1)}, u32[]{:S(2)}, u32[]{:S(2)}) %collective-permute-start.25) | collective-permute-done | bytes 196640 | tf_op jit(solution)/shard_map/ppermute | solution.py:65
  302.1 13.6 %push_3.1 = f32[4,4,128]{2,1,0:T(4,128)} custom-call(f32[4,128]{1,0:T(4,128)} %bitcast.420), custom_call_target="tpu_custom_call" | custom-call | tf_op jit(solution)/shard_map/push_3/pallas_call | solution.py:106
  343.1 29.0 %push_5.1 = bf16[4,160,384]{2,1,0:T(8,128)(2,1)} custom-call(bf16[4,160,384]{2,1,0:T(8,128)(2,1)} %add_convert_fusion.3.values), custom_call_target="tpu_custom_call" | custom-call | tf_op jit(solution)/shard_map/push_5/pallas_call | solution.py:106
  396.4 20.0 %collective-permute-done.22 = bf16[160,1536]{1,0:T(8,128)(2,1)} collective-permute-done((bf16[160,1536]{1,0:T(8,128)(2,1)S(1)}, bf16[160,1536]{1,0:T(8,128)(2,1)}, u32[]{:S(2)}, u32[]{:S(2)}) %collective-permute-start.22) | collective-permute-done | bytes 491552 | tf_op jit(solution)/shard_map/ppermute | solution.py:65
  438.1 8.7 copy.404
  458.4 12.5 %collective-permute-start.27 = (bf16[160,1536]{1,0:T(8,128)(2,1)}, bf16[160,1536]{1,0:T(8,128)(2,1)S(1)}, u32[]{:S(2)}, u32[]{:S(2)}) collective-permute-start(bf16[160,1536]{1,0:T(8,128)(2,1)} %get-tuple-element.195), channel_id=1, source_target_pairs={{0,3},{1,0},{2,1},{3,2},{4,7},{5,4},{6,5},{7,6},{8,11},{9,8},{10,9... | collective-permute-start | bytes 1474568 | tf_op jit(solution)/shard_map/ppermute | solution.py:65
  482.8 31.1 %collective-permute-done.28 = bf16[160,1536]{1,0:T(8,128)(2,1)S(1)} collective-permute-done((bf16[160,1536]{1,0:T(8,128)(2,1)}, bf16[160,1536]{1,0:T(8,128)(2,1)S(1)}, u32[]{:S(2)}, u32[]{:S(2)}) %collective-permute-start.28) | collective-permute-done | bytes 491552 | tf_op jit(solution)/shard_map/ppermute | solution.py:65
  521.6 13.4 %push_6.1 = bf16[4,160,384]{2,1,0:T(8,128)(2,1)} custom-call(bf16[4,160,384]{2,1,0:T(8,128)(2,1)} %bitcast.355), custom_call_target="tpu_custom_call" | custom-call | tf_op jit(solution)/shard_map/push_6/pallas_call | solution.py:106
  543.1 7.8 multiply_reduce_fusion.1
  571.0 10.0 %multiply_reduce_fusion = (f32[6,640]{1,0:T(8,128)S(1)}, f32[6,640,640]{1,2,0:T(8,128)}) fusion(f32[6,640,640]{1,2,0:T(8,128)} %get-tuple-element.343, f32[6,640]{1,0:T(8,128)S(1)} %copy-done.90, bf16[640,6,64]{0,2,1:T(8,128)(2,1)} %bitcast.380, bf16[640,6,64]{0,2,1:T(8,128)(2,1)} %bitcast.379), kind=kOutput, calls=%fused_computation.3 | convolution fusion | flops 321941760 | bytes 20674560 | tf_op jit(solution)/shard_map/qhd,khd->hqk/dot_general | solution.py:413
  581.0 11.1 %multiply_convert_fusion = bf16[6,640,640]{1,2,0:T(8,128)(2,1)} fusion(f32[6,640,640]{1,2,0:T(8,128)} %get-tuple-element.350, f32[6,640]{1,0:T(8,128)S(1)} %get-tuple-element.349, f32[6,640,640]{1,2,0:T(8,128)} %get-tuple-element.343, f32[6,640]{1,0:T(8,128)S(1)} %copy-done.90), kind=kLoop, calls=%fused_computation.2 | loop fusion | flops 9830400 | bytes 24606720 | tf_op jit(solution)/shard_map/convert_element_type | solution.py:508
  694.2 12.5 %collective-permute-start.34 = (bf16[160,1536]{1,0:T(8,128)(2,1)}, bf16[160,1536]{1,0:T(8,128)(2,1)}, u32[]{:S(2)}, u32[]{:S(2)}) collective-permute-start(bf16[160,1536]{1,0:T(8,128)(2,1)} %get-tuple-element.187), channel_id=1, source_target_pairs={{0,2},{1,3},{2,0},{3,1},{4,6},{5,7},{6,4},{7,5},{8,10},{9,11},{10,... | collective-permute-start | bytes 1474568 | tf_op jit(solution)/shard_map/ppermute | solution.py:65
  718.1 31.4 %collective-permute-start.32 = (bf16[160,1536]{1,0:T(8,128)(2,1)}, bf16[160,1536]{1,0:T(8,128)(2,1)}, u32[]{:S(2)}, u32[]{:S(2)}) collective-permute-start(bf16[160,1536]{1,0:T(8,128)(2,1)} %get-tuple-element.191), channel_id=1, source_target_pairs={{0,1},{1,2},{2,3},{3,0},{4,5},{5,6},{6,7},{7,4},{8,9},{9,10},{10,1... | collective-permute-start | bytes 1474568 | tf_op jit(solution)/shard_map/ppermute | solution.py:65
  749.5 8.0 collective-permute-done.34
  785.8 14.8 %push_7.1 = f32[4,8,5248]{2,1,0:T(8,128)} custom-call(f32[8,5248]{1,0:T(8,128)} %pad_maximum_fusion.25.values), custom_call_target="tpu_custom_call" | custom-call | tf_op jit(solution)/shard_map/push_7/pallas_call | solution.py:106
  803.2 21.7 %push_8.1 = f32[8,8,5760]{2,1,0:T(8,128)} custom-call(f32[8,5760]{1,0:T(8,128)} %pad_maximum_fusion.22.values), custom_call_target="tpu_custom_call" | custom-call | tf_op jit(solution)/shard_map/push_8/pallas_call | solution.py:106
  (734 shorter events, 472.5 us)
Async XLA Ops:
  7.2 135.9 %all-gather.8.cloned.1.call-start = ((), (), s32[]{:S(2)}) async-start(), calls=%async_computation.5 | async-start | bytes 3981312 | tf_op jit(solution)/shard_map/all_gather | solution.py:56
  26.7 265.7 %all-gather.10.cloned.1.call-start = ((), (), s32[]{:S(2)}) async-start(), calls=%async_computation.6 | async-start | bytes 7077888 | tf_op jit(solution)/shard_map/all_gather | solution.py:56
  95.0 278.1 %all-gather.12.cloned.1.call-start = ((), (), s32[]{:S(2)}) async-start(), calls=%async_computation.7 | async-start | bytes 5308416 | tf_op jit(solution)/shard_map/all_gather | solution.py:56
  183.2 202.7 %all-gather.14.cloned.1.call-start = ((), (), s32[]{:S(2)}) async-start(), calls=%async_computation.8 | async-start | bytes 3538944 | tf_op jit(solution)/shard_map/all_gather | solution.py:56
  183.8 232.6 %all-gather.16.cloned.1.call-start = ((), (), s32[]{:S(2)}) async-start(), calls=%async_computation.9 | async-start | bytes 7077888 | tf_op jit(solution)/shard_map/all_gather | solution.py:56
  185.5 112.8 %collective-permute-start.6 = (bf16[128,1024]{1,0:T(8,128)(2,1)}, bf16[128,1024]{1,0:T(8,128)(2,1)}, u32[]{:S(2)}, u32[]{:S(2)}) collective-permute-start(bf16[128,1024]{1,0:T(8,128)(2,1)} %slice.734), channel_id=1, source_target_pairs={{0,1},{1,2},{2,3},{3,0},{4,5},{5,6},{6,7},{7,4},{8,9},{9,10},{10,1... | collective-permute-start | bytes 786440 | tf_op jit(solution)/shard_map/ppermute | solution.py:65
  188.6 109.7 %collective-permute-start.7 = (bf16[128,1024]{1,0:T(8,128)(2,1)}, bf16[128,1024]{1,0:T(8,128)(2,1)}, u32[]{:S(2)}, u32[]{:S(2)}) collective-permute-start(bf16[128,1024]{1,0:T(8,128)(2,1)} %slice.734), channel_id=1, source_target_pairs={{0,2},{1,3},{2,0},{3,1},{4,6},{5,7},{6,4},{7,5},{8,10},{9,11},{10,... | collective-permute-start | bytes 786440 | tf_op jit(solution)/shard_map/ppermute | solution.py:65
  199.8 52.5 %collective-permute-start.25 = (bf16[48,2048]{1,0:T(8,128)(2,1)S(1)}, bf16[48,2048]{1,0:T(8,128)(2,1)S(1)}, u32[]{:S(2)}, u32[]{:S(2)}) collective-permute-start(bf16[48,2048]{1,0:T(8,128)(2,1)S(1)} %get-tuple-element.245), channel_id=1, source_target_pairs={{0,2},{1,3},{2,0},{3,1},{4,6},{5,7},{6,4},{7,5},{8,10},{9,11},{10,... | collective-permute-start | bytes 589832 | tf_op jit(solution)/shard_map/ppermute | solution.py:65
  208.9 70.8 %collective-permute-start.12 = (bf16[128,3072]{1,0:T(8,128)(2,1)}, bf16[128,3072]{1,0:T(8,128)(2,1)}, u32[]{:S(2)}, u32[]{:S(2)}) collective-permute-start(bf16[128,3072]{1,0:T(8,128)(2,1)} %slice.722), channel_id=1, source_target_pairs={{0,1},{1,2},{2,3},{3,0},{4,5},{5,6},{6,7},{7,4},{8,9},{9,10},{10,1... | collective-permute-start | bytes 2359304 | tf_op jit(solution)/shard_map/ppermute | solution.py:65
  253.4 313.0 %reduce-scatter.16.cloned.1.call-start = ((), (), s32[]{:S(2)}) async-start(), calls=%async_computation.14 | async-start | bytes 7077888
  318.4 66.3 %collective-permute-start.18 = (bf16[160,1536]{1,0:T(8,128)(2,1)}, bf16[160,1536]{1,0:T(8,128)(2,1)}, u32[]{:S(2)}, u32[]{:S(2)}) collective-permute-start(bf16[160,1536]{1,0:T(8,128)(2,1)} %param.42), channel_id=1, source_target_pairs={{0,1},{1,2},{2,3},{3,0},{4,5},{5,6},{6,7},{7,4},{8,9},{9,10},{10,1... | collective-permute-start | bytes 1474568 | tf_op jit(solution)/shard_map/ppermute | solution.py:65
  319.9 66.0 %collective-permute-start.19 = (bf16[160,1536]{1,0:T(8,128)(2,1)}, bf16[160,1536]{1,0:T(8,128)(2,1)}, u32[]{:S(2)}, u32[]{:S(2)}) collective-permute-start(bf16[160,1536]{1,0:T(8,128)(2,1)} %param.42), channel_id=1, source_target_pairs={{0,2},{1,3},{2,0},{3,1},{4,6},{5,7},{6,4},{7,5},{8,10},{9,11},{10,... | collective-permute-start | bytes 1474568 | tf_op jit(solution)/shard_map/ppermute | solution.py:65
  322.3 63.6 %collective-permute-start.20 = (bf16[160,1536]{1,0:T(8,128)(2,1)}, bf16[160,1536]{1,0:T(8,128)(2,1)}, u32[]{:S(2)}, u32[]{:S(2)}) collective-permute-start(bf16[160,1536]{1,0:T(8,128)(2,1)} %param.42), channel_id=1, source_target_pairs={{0,3},{1,0},{2,1},{3,2},{4,7},{5,4},{6,5},{7,6},{8,11},{9,8},{10,9... | collective-permute-start | bytes 1474568 | tf_op jit(solution)/shard_map/ppermute | solution.py:65
  446.8 153.1 %reduce-scatter.8.cloned.1.call-start = ((), (), s32[]{:S(2)}) async-start(), calls=%async_computation.10 | async-start | bytes 3538944 | tf_op jit(solution)/shard_map/reduce_scatter | solution.py:60
  477.8 271.7 %reduce-scatter.10.cloned.1.call-start = ((), (), s32[]{:S(2)}) async-start(), calls=%async_computation.11 | async-start | bytes 5308416 | tf_op jit(solution)/shard_map/reduce_scatter | solution.py:60
  566.2 270.6 %reduce-scatter.12.cloned.1.call-start = ((), (), s32[]{:S(2)}) async-start(), calls=%async_computation.12 | async-start | bytes 3981312 | tf_op jit(solution)/shard_map/reduce_scatter | solution.py:60
  638.7 212.9 %reduce-scatter.14.cloned.1.call-start = ((), (), s32[]{:S(2)}) async-start(), calls=%async_computation.13 | async-start | bytes 7077888 | tf_op jit(solution)/shard_map/reduce_scatter | solution.py:60
  646.5 126.7 %collective-permute-start.30 = (bf16[160,1536]{1,0:T(8,128)(2,1)}, bf16[160,1536]{1,0:T(8,128)(2,1)}, u32[]{:S(2)}, u32[]{:S(2)}) collective-permute-start(bf16[160,1536]{1,0:T(8,128)(2,1)} %get-tuple-element.190), channel_id=1, source_target_pairs={{0,3},{1,0},{2,1},{3,2},{4,7},{5,4},{6,5},{7,6},{8,11},{9,8},{10,9... | collective-permute-start | bytes 1474568 | tf_op jit(solution)/shard_map/ppermute | solution.py:65
  649.3 127.6 %collective-permute-start.31 = (bf16[160,1536]{1,0:T(8,128)(2,1)}, bf16[160,1536]{1,0:T(8,128)(2,1)}, u32[]{:S(2)}, u32[]{:S(2)}) collective-permute-start(bf16[160,1536]{1,0:T(8,128)(2,1)} %get-tuple-element.192), channel_id=1, source_target_pairs={{0,2},{1,3},{2,0},{3,1},{4,6},{5,7},{6,4},{7,5},{8,10},{9,11},{10,... | collective-permute-start | bytes 1474568 | tf_op jit(solution)/shard_map/ppermute | solution.py:65
  694.2 63.3 %collective-permute-start.34 = (bf16[160,1536]{1,0:T(8,128)(2,1)}, bf16[160,1536]{1,0:T(8,128)(2,1)}, u32[]{:S(2)}, u32[]{:S(2)}) collective-permute-start(bf16[160,1536]{1,0:T(8,128)(2,1)} %get-tuple-element.187), channel_id=1, source_target_pairs={{0,2},{1,3},{2,0},{3,1},{4,6},{5,7},{6,4},{7,5},{8,10},{9,11},{10,... | collective-permute-start | bytes 1474568 | tf_op jit(solution)/shard_map/ppermute | solution.py:65
  718.1 58.9 %collective-permute-start.32 = (bf16[160,1536]{1,0:T(8,128)(2,1)}, bf16[160,1536]{1,0:T(8,128)(2,1)}, u32[]{:S(2)}, u32[]{:S(2)}) collective-permute-start(bf16[160,1536]{1,0:T(8,128)(2,1)} %get-tuple-element.191), channel_id=1, source_target_pairs={{0,1},{1,2},{2,3},{3,0},{4,5},{5,6},{6,7},{7,4},{8,9},{9,10},{10,1... | collective-permute-start | bytes 1474568 | tf_op jit(solution)/shard_map/ppermute | solution.py:65
  759.3 75.7 %collective-permute-start.42 = (bf16[48,1536]{1,0:T(8,128)(2,1)}, bf16[48,1536]{1,0:T(8,128)(2,1)}, u32[]{:S(2)}, u32[]{:S(2)}) collective-permute-start(bf16[48,1536]{1,0:T(8,128)(2,1)} %get-tuple-element.255), channel_id=1, source_target_pairs={{0,1},{1,2},{2,3},{3,0},{4,5},{5,6},{6,7},{7,4},{8,9},{9,10},{10,1... | collective-permute-start | bytes 442376 | tf_op jit(solution)/shard_map/ppermute | solution.py:65
  759.6 75.4 %collective-permute-start.43 = (bf16[48,1536]{1,0:T(8,128)(2,1)}, bf16[48,1536]{1,0:T(8,128)(2,1)}, u32[]{:S(2)}, u32[]{:S(2)}) collective-permute-start(bf16[48,1536]{1,0:T(8,128)(2,1)} %get-tuple-element.257), channel_id=1, source_target_pairs={{0,2},{1,3},{2,0},{3,1},{4,6},{5,7},{6,4},{7,5},{8,10},{9,11},{10,... | collective-permute-start | bytes 442376 | tf_op jit(solution)/shard_map/ppermute | solution.py:65
  773.2 61.8 %collective-permute-start.44 = (bf16[48,1536]{1,0:T(8,128)(2,1)}, bf16[48,1536]{1,0:T(8,128)(2,1)S(1)}, u32[]{:S(2)}, u32[]{:S(2)}) collective-permute-start(bf16[48,1536]{1,0:T(8,128)(2,1)} %get-tuple-element.256), channel_id=1, source_target_pairs={{0,3},{1,0},{2,1},{3,2},{4,7},{5,4},{6,5},{7,6},{8,11},{9,8},{10,9... | collective-permute-start | bytes 442376 | tf_op jit(solution)/shard_map/ppermute | solution.py:65
  (182 other events, 3615.1 us)
Sparse Core Ops, SparseCore 0:
  26.8 41.5 all-gather.7
  95.2 48.8 all-gather.9
  183.3 39.0 all-gather.11
  224.2 32.1 all-gather.13
  258.7 45.3 all-gather.15
  447.0 70.7 reduce-scatter.15
  521.2 46.1 reduce-scatter.7
  570.8 53.7 reduce-scatter.9
  638.8 47.7 reduce-scatter.11
  689.8 61.7 reduce-scatter.13

commit v3 on v2

--- a/solution.py
+++ b/solution.py
@@ -18,6 +18,7 @@
 NEGATIVE = -1e30
 BF16 = jnp.bfloat16
 F32 = jnp.float32
+PUSH_BYTES = 50_000_000
 
 
 def norm_modulate(values, gain, scale, shift):
@@ -69,60 +70,79 @@
     return lax.optimization_barrier(values)
 
 
-def push_kernel(axis, size, block, spot, values, result, send_sems, receive_sems):
-    me = lax.axis_index(axis)
+def push_kernel(jobs, *refs):
+    count = len(jobs)
+    sources, results = refs[:count], refs[count : 2 * count]
+    send_sems, receive_sems = refs[2 * count : 3 * count], refs[3 * count :]
+    sizes = dict((axis, size) for axis, size, block, spot in jobs)
+    place = dict((axis, lax.axis_index(axis)) for axis in sizes)
     barrier = pltpu.get_barrier_semaphore()
-    for step in range(1, size):
-        pl.semaphore_signal(
-            barrier,
-            inc=1,
-            device_id={axis: lax.rem(me + step, size)},
-            device_id_type=pl.DeviceIdType.MESH,
-        )
-    pl.semaphore_wait(barrier, size - 1)
-
-    def copy(step, place):
-        to = lax.rem(me + step, size)
+    for axis, size in sizes.items():
+        for step in range(1, size):
+            pl.semaphore_signal(
+                barrier,
+                inc=1,
+                device_id={axis: lax.rem(place[axis] + step, size)},
+                device_id_type=pl.DeviceIdType.MESH,
+            )
+    pl.semaphore_wait(barrier, sum(size - 1 for size in sizes.values()))
+
+    def copy(k, step, spot_there):
+        axis, size, block, spot = jobs[k]
+        to = lax.rem(place[axis] + step, size)
         return pltpu.make_async_remote_copy(
-            src_ref=values if block is None else values.at[block(to, step)],
-            dst_ref=result.at[place],
-            send_sem=send_sems.at[step],
-            recv_sem=receive_sems.at[step],
+            src_ref=sources[k] if block is None else sources[k].at[block(to, step)],
+            dst_ref=results[k].at[spot_there],
+            send_sem=send_sems[k].at[step],
+            recv_sem=receive_sems[k].at[step],
             device_id={axis: to},
             device_id_type=pl.DeviceIdType.MESH,
         )
 
-    for step in range(1, size):
-        copy(step, spot(me, step)).start()
-    result[spot(me, 0)] = values[...] if block is None else values[block(me, 0)]
-    for step in range(1, size):
-        origin = lax.rem(me + size - step, size)
-        copy(step, spot(origin, step)).wait()
+    for k, (axis, size, block, spot) in enumerate(jobs):
+        for step in range(1, size):
+            copy(k, step, spot(place[axis], step)).start()
+    for k, (axis, size, block, spot) in enumerate(jobs):
+        me = place[axis]
+        results[k][spot(me, 0)] = sources[k][...] if block is None else sources[k][block(me, 0)]
+    for k, (axis, size, block, spot) in enumerate(jobs):
+        for step in range(1, size):
+            origin = lax.rem(place[axis] + size - step, size)
+            copy(k, step, spot(origin, step)).wait()
+
+
+def push_many(jobs, collective):
+    sizes = [lax.axis_size(axis) for values, axis, block, spot in jobs]
+    return pl.pallas_call(
+        functools.partial(
+            push_kernel,
+            [(axis, size, block, spot) for (v, axis, block, spot), size in zip(jobs, sizes)],
+        ),
+        out_shape=[
+            jax.ShapeDtypeStruct(
+                (size,) + (values.shape if block is None else values.shape[1:]), values.dtype
+            )
+            for (values, axis, block, spot), size in zip(jobs, sizes)
+        ],
+        in_specs=[pl.BlockSpec(memory_space=pltpu.VMEM)] * len(jobs),
+        out_specs=[pl.BlockSpec(memory_space=pltpu.VMEM)] * len(jobs),
+        scratch_shapes=[pltpu.SemaphoreType.DMA((size,)) for size in sizes] * 2,
+        compiler_params=pltpu.CompilerParams(collective_id=collective, has_side_effects=True),
+        cost_estimate=pl.CostEstimate(flops=0, bytes_accessed=PUSH_BYTES, transcendentals=0),
+        name="push_%d" % collective,
+    )(*[values for values, axis, block, spot in jobs])
 
 
 def push(values, axis, block, spot, collective):
-    size = lax.axis_size(axis)
-    shape = values.shape if block is None else values.shape[1:]
-    return pl.pallas_call(
-        functools.partial(push_kernel, axis, size, block, spot),
-        out_shape=jax.ShapeDtypeStruct((size,) + shape, values.dtype),
-        in_specs=[pl.BlockSpec(memory_space=pltpu.VMEM)],
-        out_specs=pl.BlockSpec(memory_space=pltpu.VMEM),
-        scratch_shapes=[
-            pltpu.SemaphoreType.DMA((size,)),
-            pltpu.SemaphoreType.DMA((size,)),
-        ],
-        compiler_params=pltpu.CompilerParams(collective_id=collective, has_side_effects=True),
-        name="push_%d" % collective,
-    )(values)
-
-
-def push_gather(values, axis, collective):
-    return push(values, axis, None, lambda me, step: me, collective)
-
-
-def push_blocks(stack, axis, collective):
-    return push(stack, axis, lambda to, step: to, lambda me, step: me, collective)
+    return push_many([(values, axis, block, spot)], collective)[0]
+
+
+def to_all(values, axis):
+    return (values, axis, None, lambda me, step: me)
+
+
+def to_each(stack, axis):
+    return (stack, axis, lambda to, step: to, lambda me, step: me)
 
 
 def pick(stack, index):
@@ -171,11 +191,13 @@
     return total(spread(values, "sp"))
 
 
-def turned_sums(parts, collective):
+def row_sums(parts, collective, turned, jobs=()):
     sp = lax.axis_size("sp")
     count = sum(part.shape[0] for part in parts)
     lines = jnp.concatenate(parts).reshape(count // 128, 128)
-    blocks = push(lines, "sp", None, lambda me, step: step, collective)
+    blocks, *others = push_many(
+        [(lines, "sp", None, lambda me, step: step), *jobs], collective
+    )
     blocks = [blocks[s].reshape(count) for s in range(sp)]
     results, begin = [], 0
     for part in parts:
@@ -183,13 +205,13 @@
         results.append(
             total(
                 [
-                    jnp.roll(block[begin : begin + count], s * (count // sp))
+                    jnp.roll(block[begin : begin + count], s * (count // sp) if turned else 0)
                     for s, block in enumerate(blocks)
                 ]
             )
         )
         begin += count
-    return results
+    return results, others
 
 
 def body(
@@ -238,7 +260,6 @@
         .transpose(2, 0, 1, 3)
         .reshape(sp, weight.shape[0], weight.shape[1] // sp)
     )
-    tokens_all = gather_turned(tokens)
     qkv_full = gather(ordered(send(columns(qkv_weight, 3), "sp"), "sp", 0))
     down_full = gather(down_weight)
 
@@ -269,20 +290,23 @@
         ],
         axis=2,
     )
-    arrived = push_blocks(pieces, "fsdp", 0)
+    arrived, tokens_all = push_many(
+        [
+            to_each(pieces, "fsdp"),
+            (tokens, "sp", None, lambda me, step: step),
+        ],
+        0,
+    )
+    tokens_all = tokens_all.reshape(seq, dim)
     small_group = arrived[:, :, 3 * dim : 3 * dim + small_size // 8].reshape(8, -1)
     group_size = small_group.shape[1]
-    bundles = push_gather(
-        jnp.concatenate(
-            [
-                jnp.sum(arrived[:, :, : 3 * dim], axis=0),
-                wide(small_group, rounded(group_size)),
-            ],
-            axis=1,
-        ),
-        "sp",
-        1,
-    )
+    bundle = jnp.concatenate(
+        [jnp.sum(arrived[:, :, : 3 * dim], axis=0), wide(small_group, rounded(group_size))],
+        axis=1,
+    )
+    (bundles,) = push_many([to_all(bundle, "sp")], 1)
+    bundles, down_full, caption = tie(bundles, down_full, caption)
+    caption_all = lax.all_gather(caption, "sp", axis=0, tiled=True)
     small_all = (
         bundles[:, :, 3 * dim : 3 * dim + group_size]
         .reshape(sp, fsdp, small_size)
@@ -301,8 +325,8 @@
     modulation = jnp.sum(bundles[:, :, : 3 * dim], axis=0)
     modulation = jnp.concatenate([modulation[:CPG], modulation[CPG:]], axis=1) + bias_full[None]
 
-    modulation, caption, text_key_weight, text_value_weight = tie(
-        modulation, caption, text_key_weight, text_value_weight
+    modulation, text_key_weight, text_value_weight = tie(
+        modulation, text_key_weight, text_value_weight
     )
 
     text_full_weight = gather(
@@ -317,8 +341,6 @@
             0,
         )
     )
-    first = text_dim // 4
-    caption_first = gather_turned(caption[:, :first])
 
     lengths = clip_lengths[0]
     ends = jnp.cumsum(lengths)
@@ -355,23 +377,7 @@
         projected[:, local : 2 * local],
         projected[:, 2 * local :],
     )
-    qk_squares = turned_sums([jnp.sum(q_raw * q_raw, axis=1), jnp.sum(k_raw * k_raw, axis=1)], 2)
-    *qk_squares, caption_rest, gate_weight, up_weight, out_weight = tie(
-        *qk_squares, caption[:, first:], gate_weight, up_weight, out_weight
-    )
-    out_full = gather(ordered(spread(out_weight, "sp"), "sp", 0))
-    gate_up_full = gather(
-        ordered(
-            send(
-                jnp.concatenate([columns(gate_weight, fsdp), columns(up_weight, fsdp)], axis=2),
-                "sp",
-            ),
-            "sp",
-            0,
-        )
-    )
-    gate_full, up_full = gate_up_full[:, :hlocal], gate_up_full[:, hlocal:]
-    caption_rest = gather_turned(caption_rest)
+    qk_squares, others = row_sums([jnp.sum(q_raw * q_raw, axis=1), jnp.sum(k_raw * k_raw, axis=1)], 2, True)
     q_root = lax.rsqrt(qk_squares[0] / dim + EPSILON)[:, None]
     k_root = lax.rsqrt(qk_squares[1] / dim + EPSILON)[:, None]
     half = HD // 2
@@ -387,22 +393,15 @@
     key = split_heads(rotate(k_raw * k_root * key_mine).astype(BF16))
     value = split_heads(v_raw.astype(BF16))
 
-    text_both = product(caption_first, text_full_weight[:first]) + product(
-        caption_rest, text_full_weight[first:]
-    )
+    text_both = product(caption_all, text_full_weight)
     tkey_raw = text_both[:, :local]
-    (tk_squares,) = turned_sums([jnp.sum(tkey_raw * tkey_raw, axis=1)], 3)
-    tk_squares, out_grad_late = tie(tk_squares, out_grad)
-    out_grad_all = gather_turned(out_grad_late)
+    (tk_squares,), others = row_sums([jnp.sum(tkey_raw * tkey_raw, axis=1)], 3, False)
     tk_root = lax.rsqrt(tk_squares / dim + EPSILON)[:, None]
     tkey = split_heads((tkey_raw * tk_root * text_mine).astype(BF16))
     tvalue = split_heads(text_both[:, local:].astype(BF16))
 
     scale = HD**-0.5
     caption_row = jnp.arange(caps, dtype=jnp.int32)
-    caption_row = (sp_place - caption_row // caption.shape[0]) % sp * caption.shape[
-        0
-    ] + caption_row % caption.shape[0]
     caption_clip = caption_row // CAP
     caption_limit = jnp.sum(
         jnp.where(caption_clip[:, None] == slot, caption_lengths[None, :], 0), axis=1
@@ -418,9 +417,23 @@
     self_low = self_prob.astype(BF16)
     cross_low = cross_prob.astype(BF16)
     cross_out = to_rows(cross_low, tvalue).reshape(seq, local)
-    mixed_heads = (
-        to_rows(self_low, value).reshape(seq, local) + gate_tanh * cross_out
-    ).astype(BF16)
+    self_rows = to_rows(self_low, value).reshape(seq, local)
+    self_rows, gate_weight, up_weight, out_weight, out_grad_late = tie(
+        self_rows, gate_weight, up_weight, out_weight, out_grad
+    )
+    out_grad_all = gather_turned(out_grad_late)
+    out_full = gather(ordered(spread(out_weight, "sp"), "sp", 0))
+    gate_up_full = gather(
+        ordered(
+            send(
+                jnp.concatenate([columns(gate_weight, fsdp), columns(up_weight, fsdp)], axis=2),
+                "sp",
+            ),
+            "sp",
+            0,
+        )
+    )
+    mixed_heads = (self_rows + gate_tanh * cross_out).astype(BF16)
     mixed = push(
         mixed_heads.reshape(sp, rows, local),
         "sp",
@@ -436,8 +449,8 @@
     normed_two_all = gather_turned(normed_two)
     grad_top = out_grad.astype(F32)
     grad_ffn_all = (token_mod(5, group_clip) * out_grad_all.astype(F32)).astype(BF16)
-    gate_act = product(normed_two_all, gate_full)
-    up_act = product(normed_two_all, up_full)
+    gate_up_act = product(normed_two_all, gate_up_full)
+    gate_act, up_act = gate_up_act[:, :hlocal], gate_up_act[:, hlocal:]
     sigmoid = jax.nn.sigmoid(gate_act)
     hidden = (gate_act * sigmoid * up_act).astype(BF16)
     grad_hidden = right_product(grad_ffn_all, down_full)
@@ -445,25 +458,20 @@
         BF16
     )
     grad_up_act = (grad_hidden * gate_act * sigmoid).astype(BF16)
-    grad_normed_blocks = turned_blocks(
-        (right_product(grad_gate_act, gate_full) + right_product(grad_up_act, up_full)).astype(
-            BF16
-        )
-    )
-    gate_up_terms = jnp.concatenate(
-        [
-            left_product(normed_two_all, grad_gate_act).astype(BF16),
-            left_product(normed_two_all, grad_up_act).astype(BF16),
-        ],
-        axis=1,
+    grad_gate_up = jnp.concatenate([grad_gate_act, grad_up_act], axis=1)
+    gate_up_terms = left_product(normed_two_all, grad_gate_up).astype(BF16)
+    gate_up_terms, grad_gate_up = tie(gate_up_terms, grad_gate_up)
+    grad_normed_blocks = push(
+        right_product(grad_gate_up, gate_up_full).astype(BF16).reshape(sp, rows, dim),
+        "sp",
+        lambda to, step: (sp - step) % sp,
+        lambda me, step: step,
+        10,
     )
     down_terms = left_product(hidden, grad_ffn_all).astype(BF16)
     gate_up_rows = scatter(gate_up_terms)
     down_rows = scatter(down_terms)
-    *grad_normed_blocks, unused_gate_up, unused_down = tie(
-        *grad_normed_blocks, gate_up_terms, down_terms
-    )
-    grad_normed_two = total(grad_normed_blocks)
+    grad_normed_two = jnp.sum(grad_normed_blocks.astype(F32), axis=0)
     unused_two, pull_two = jax.vjp(
         norm_modulate, middle, feedforward_full[None], scale_two, shift_two
     )
@@ -483,9 +491,11 @@
     ).reshape(seq, local)
 
     grad_flat, hidden, unused_out = tie(grad_flat, hidden, out_terms)
-    ffn_out = total(turned_blocks(product(hidden, down_full).astype(BF16)))
-    output = middle + gate_two * ffn_out
-    grad_gate_two = grad_top * ffn_out
+    ffn_blocks = turned_blocks(product(hidden, down_full).astype(BF16))
+
+    def norm_back(grad, raw, root, gain, dot):
+        raw_grad = root * gain * grad - raw * (root * root * root * dot / dim)
+        return raw_grad.astype(BF16), jnp.sum(grad * raw * root, axis=0)
 
     grad_heads = split_heads(grad_flat)
     gate_local = (1.0 - gate_tanh * gate_tanh)[0] * jnp.sum(
@@ -499,9 +509,15 @@
     low = lambda v: v.astype(BF16).reshape(v.shape[0], local).astype(F32)
     tkey_back = low(to_cols(cscore_grad, query) * scale)
     tvalue_back = to_cols(cross_low, cross_grad).astype(BF16).reshape(caps, local)
-    gate_up_rows, tkey_back, tvalue_back, grad_heads = tie(
-        gate_up_rows, tkey_back, tvalue_back, grad_heads
-    )
+    (tk_dots,), others = row_sums([jnp.sum(tkey_back * text_mine * tkey_raw, axis=1)], 9, False)
+    grad_tk, text_gain_grad = norm_back(tkey_back, tkey_raw, tk_root, text_mine, tk_dots[:, None])
+    text_grads = jnp.concatenate([grad_tk, tvalue_back], axis=1)
+    text_terms = left_product(caption_all, text_grads).astype(BF16)
+    text_rows = scatter(text_terms)
+    gate_up_rows, grad_heads, cscore_grad, unused_text = tie(
+        gate_up_rows, grad_heads, cscore_grad, text_terms
+    )
+    gate_up_back = send(gate_up_rows.reshape(sp, wrows, 2 * hlocal), "sp")
     grad_self = to_scores(grad_heads, value)
     score_grad = (
         self_prob * (grad_self - jnp.sum(self_prob * grad_self, axis=-1, keepdims=True))
@@ -509,11 +525,16 @@
     query_back = low((to_rows(score_grad, key) + to_rows(cscore_grad, tkey)) * scale)
     key_back = low(to_cols(score_grad, query) * scale)
     value_back = to_cols(self_low, grad_heads).astype(BF16).reshape(seq, local)
-    down_rows, query_back, key_back = tie(down_rows, query_back, key_back)
+    down_rows, query_back, key_back, *backs = tie(
+        down_rows, query_back, key_back, *gate_up_back, *ffn_blocks
+    )
+    gate_up_back, ffn_blocks = backs[:sp], backs[sp:]
+    ffn_out = total(ffn_blocks)
+    output = middle + gate_two * ffn_out
+    grad_gate_two = grad_top * ffn_out
     down_shard = down_rows.astype(F32)
     gate_up_back = [
-        block.reshape(wrows, 2, fsdp, 1, hcols)
-        for block in send(gate_up_rows.reshape(sp, wrows, 2 * hlocal), "sp")
+        block.reshape(wrows, 2, fsdp, 1, hcols) for block in gate_up_back
     ]
     gate_up_back = (
         ordered(gate_up_back, "sp", 3)
@@ -525,56 +546,28 @@
 
     query_turn = rotate_back(query_back)
     key_turn = rotate_back(key_back)
-    q_dots, k_dots, tk_dots = [
-        dot[:, None]
-        for dot in turned_sums(
-            [
-                jnp.sum(query_turn * query_mine * q_raw, axis=1),
-                jnp.sum(key_turn * key_mine * k_raw, axis=1),
-                jnp.sum(tkey_back * text_mine * tkey_raw, axis=1),
-            ],
-            4,
-        )
-    ]
-
-    def norm_back(grad, raw, root, gain, dot):
-        raw_grad = root * gain * grad - raw * (root * root * root * dot / dim)
-        return raw_grad.astype(BF16), jnp.sum(grad * raw * root, axis=0)
+    dots, (out_back,) = row_sums(
+        [
+            jnp.sum(query_turn * query_mine * q_raw, axis=1),
+            jnp.sum(key_turn * key_mine * k_raw, axis=1),
+        ],
+        4,
+        True,
+        [to_each(out_rows.reshape(sp, wrows, dim), "sp")],
+    )
+    q_dots, k_dots = [dot[:, None] for dot in dots]
+    out_shard = jnp.sum(out_back.astype(F32), axis=0)
 
     grad_q, query_gain_grad = norm_back(query_turn, q_raw, q_root, query_mine, q_dots)
     grad_k, key_gain_grad = norm_back(key_turn, k_raw, k_root, key_mine, k_dots)
-    grad_tk, text_gain_grad = norm_back(tkey_back, tkey_raw, tk_root, text_mine, tk_dots)
     grad_projected = jnp.concatenate([grad_q, grad_k, value_back], axis=1)
-    grad_normed_blocks = turned_blocks(right_product(grad_projected, qkv_full).astype(BF16))
+    grad_normed_terms = right_product(grad_projected, qkv_full).astype(BF16)
+    grad_normed_terms, grad_projected = tie(grad_normed_terms, grad_projected)
+    grad_normed_blocks = turned_blocks(grad_normed_terms)
     qkv_terms = left_product(normed_one_all, grad_projected).astype(BF16)
     qkv_rows = scatter(qkv_terms)
-    qkv_back = [
-        block.reshape(wrows, 3, 1, local)
-        for block in send(qkv_rows.reshape(sp, wrows, 3 * local), "sp")
-    ]
-    qkv_shard = ordered(qkv_back, "sp", 2).reshape(wrows, 3 * dim).astype(F32)
-    text_grads = jnp.concatenate([grad_tk, tvalue_back], axis=1)
-    text_terms = jnp.concatenate(
-        [
-            left_product(caption_first, text_grads).astype(BF16),
-            left_product(caption_rest, text_grads).astype(BF16),
-        ],
-        axis=0,
-    )
-    text_rows = scatter(text_terms)
-    *grad_normed_blocks, unused_qkv, unused_text, out_rows = tie(
-        *grad_normed_blocks, qkv_terms, text_terms, out_rows
-    )
-    out_shard = total(send(out_rows.reshape(sp, wrows, dim), "sp"))
+    *grad_normed_blocks, unused_qkv = tie(*grad_normed_blocks, qkv_terms)
     grad_normed_one = total(grad_normed_blocks)
-    text_back = [
-        block.reshape(tcols, 2, 1, local)
-        for block in send(text_rows.reshape(sp, tcols, 2 * local), "sp")
-    ]
-    text_shard = ordered(text_back, "sp", 2).astype(F32)
-    text_key_shard = text_shard[:, 0].reshape(tcols, dim)
-    text_value_shard = text_shard[:, 1].reshape(tcols, dim)
-
     unused_one, pull_one = jax.vjp(
         norm_modulate, values, attention_full[None], scale_one, shift_one
     )
@@ -610,7 +603,7 @@
         ],
         axis=1,
     )
-    blocks = push_gather(sent, "sp", 7)
+    (blocks,) = push_many([to_all(sent, "sp")], 7)
     summed = jnp.sum(blocks[:, :, : 3 * dim + dim // 4], axis=0)
     heads_rows = (
         blocks[:, :, 3 * dim + dim // 4 : 3 * dim + dim // 4 + local // 2]
@@ -618,7 +611,20 @@
         .transpose(1, 0, 2)
         .reshape(8, dim // 2)
     )
-    gathered = push_gather(jnp.concatenate([summed, heads_rows], axis=1), "fsdp", 8)
+    gathered, qkv_back, text_back = push_many(
+        [
+            to_all(jnp.concatenate([summed, heads_rows], axis=1), "fsdp"),
+            to_each(qkv_rows.reshape(sp, wrows, 3 * local), "sp"),
+            to_each(text_rows.reshape(sp, tcols, 2 * local), "sp"),
+        ],
+        8,
+    )
+    qkv_shard = (
+        qkv_back.reshape(sp, wrows, 3, local).transpose(1, 2, 0, 3).reshape(wrows, 3 * dim)
+    ).astype(F32)
+    text_shard = text_back.reshape(sp, tcols, 2, local).transpose(2, 1, 0, 3).astype(F32)
+    text_key_shard = text_shard[0].reshape(tcols, dim)
+    text_value_shard = text_shard[1].reshape(tcols, dim)
     half_one = gathered[:, :CPG, : 3 * dim].reshape(fsdp * CPG, 3 * dim)
     half_two = gathered[:, CPG:, : 3 * dim].reshape(fsdp * CPG, 3 * dim)
     gain_sums = jnp.sum(gathered[:, :, 3 * dim :], axis=0)

time: 892 us -> 788 us (0.88)
  starting transfers between devices: 146 us -> 66 us
  Pallas kernels: 156 us -> 221 us
  waiting for transfers between devices: 177 us -> 125 us
  local copies, waits for them, and re-layouts: 119 us -> 89.9 us
    ppermute x48 -> x27, starting transfers between devices: 144 us -> 64.5 us  [shift(): lax.ppermute(values, axis, [(k, (k + step) % size) for k in range(size)])]
    pallas_call x9 -> x11, Pallas kernels: 156 us -> 221 us  [push_many(): pl.pallas_call(functools.partial(push_kernel, [(axis, size, block, spot)...]
    ppermute x48 -> x27, waiting for transfers between devices: 177 us -> 124 us  [shift(): lax.ppermute(values, axis, [(k, (k + step) % size) for k in range(size)])]
    unnamed x312 -> x275, local copies, waits for them, and re-layouts: 32.6 us -> 13.9 us
    dot_general x8 -> x6, matrix products: 33.6 us -> 28.5 us  [product(): return jnp.dot(left, right, preferred_element_type=F32)]
    dot_general x5 -> x4, matrix products: 22.3 us -> 24.7 us  [right_product(): lax.dot_general(left, right, (((1,), (1,)), ((), ())), preferred_element_...]
    dot_general x7 -> x5, matrix products: 29.7 us -> 31.4 us  [left_product(): lax.dot_general(left, right, (((0,), (0,)), ((), ())), preferred_element_...]
  transfers between devices with their start and end apart: 58 -> 38, of which waited for: 20 -> 12; matrix products, arithmetic and copies ran while one was open for 37% -> 38% of each run, Pallas kernels for 18% -> 24%
where the time goes in v3:
time: 788 us; the launch traced here: 779 us
  Pallas kernels  221 us (28%)
  matrix products  157 us (20%)
  waiting for transfers between devices  125 us (16%)
  other arithmetic  94.9 us (12%)
  local copies, waits for them, and re-layouts  89.9 us (11%)
  starting transfers between devices  66 us (8%)
  between operations  16.6 us (2%)
  blocking collectives  9.24 us (1%)
    pallas_call x11, Pallas kernels, push_many(): pl.pallas_call(functools.partial(push_kernel, [(axis, size, block, spot)...  221 us
    ppermute x27, waiting for transfers between devices, shift(): lax.ppermute(values, axis, [(k, (k + step) % size) for k in range(size)])  124 us
    ppermute x27, starting transfers between devices, shift(): lax.ppermute(values, axis, [(k, (k + step) % size) for k in range(size)])  64.5 us
    dot_general x5, matrix products, left_product(): lax.dot_general(left, right, (((0,), (0,)), ((), ())), preferred_element_...  31.4 us
    dot_general x6, matrix products, product(): return jnp.dot(left, right, preferred_element_type=F32)  28.5 us
    dot_general x4, matrix products, right_product(): lax.dot_general(left, right, (((1,), (1,)), ((), ())), preferred_element_...  24.7 us
    dot_general x4, matrix products, body(): jnp.einsum('hqk,khd->qhd', a, b, preferred_element_type=F32)  19.2 us
    dot_general x4, matrix products, body(): jnp.einsum('hqk,qhd->khd', a, b, preferred_element_type=F32)  17.2 us
  transfers between devices with their start and end apart: 38, of which 12 were waited for; matrix products, arithmetic and copies ran while one was open for 38% of the time, Pallas kernels for 24%

profile of v3, /device:TPU:0, one launch (start us, length us, event | category | flops | bytes accessed | tf_op | source)
XLA Modules:
  0.0 779.4 jit_solution(12168491377664050020)
XLA Ops:
  26.0 9.2 %all-gather.1 = bf16[8,4,1536]{2,1,0:T(4,128)(2,1)S(1)} all-gather(bf16[1,4,1536]{2,1,0:T(4,128)(2,1)S(1)} %fusion.79), channel_id=2, replica_groups=mesh['fsdp'=8,'sp'=4] {'fsdp'}, dimensions={0}, use_global_device_ids=true | all-gather | bytes 110592 | tf_op jit(solution)/shard_map/all_gather | solution.py:267
  37.6 39.9 %push_0.1 = (f32[8,8,4736]{2,1,0:T(8,128)}, bf16[4,160,1536]{2,1,0:T(8,128)(2,1)}) custom-call(f32[8,8,4736]{2,1,0:T(8,128)} %pad_maximum_fusion.4.refs_0_, bf16[160,1536]{1,0:T(8,128)(2,1)} %refs_1_.1), custom_call_target="tpu_custom_call" | custom-call | bytes 50000000 | tf_op jit(solution)/shard_map/push_0/pallas_call | solution.py:116
  80.4 26.8 %push_1.1 = f32[4,8,5248]{2,1,0:T(8,128)} custom-call(f32[8,5248]{1,0:T(8,128)} %select_maximum_fusion.refs_0_), custom_call_target="tpu_custom_call" | custom-call | bytes 50000000 | tf_op jit(solution)/shard_map/push_1/pallas_call | solution.py:116
  124.1 29.1 %collective-permute-done.4 = bf16[128,768]{1,0:T(8,128)(2,1)S(1)} collective-permute-done((bf16[128,768]{1,0:T(8,128)(2,1)S(1)}, bf16[128,768]{1,0:T(8,128)(2,1)S(1)}, u32[]{:S(2)}, u32[]{:S(2)}) %collective-permute-start.4) | collective-permute-done | bytes 196640 | tf_op jit(solution)/shard_map/ppermute | solution.py:66
  167.8 9.9 %fusion.10 = bf16[640,1536]{1,0:T(8,128)(2,1)} fusion(f32[1536]{0:T(1024)S(1)} %get-tuple-element.129, f32[1536]{0:T(1024)S(1)} %get-tuple-element.130, f32[1536]{0:T(1024)S(1)} %get-tuple-element.131, f32[1536]{0:T(1024)S(1)} %get-tuple-element.132, f32[1536]{0:T(1024)S(1)} %get-tuple-element.133, f32[1536]{0:T(1024)S(1)} %get-tuple-element.134, ...), kind=kLoop, calls=%fused_computation.26 | loop fusion | flops 12779520 | bytes 3991936 | tf_op jit(solution)/shard_map/convert_element_type | solution.py:373
  185.6 8.3 %push_2.1 = f32[4,10,128]{2,1,0:T(8,128)} custom-call(f32[10,128]{1,0:T(8,128)} %pad_maximum_fusion.18.refs_0_), custom_call_target="tpu_custom_call" | custom-call | bytes 50000000 | tf_op jit(solution)/shard_map/push_2/pallas_call | solution.py:116
  239.4 7.9 %collective-permute-done.13 = bf16[48,2048]{1,0:T(8,128)(2,1)S(1)} collective-permute-done((bf16[48,2048]{1,0:T(8,128)(2,1)S(1)}, bf16[48,2048]{1,0:T(8,128)(2,1)S(1)}, u32[]{:S(2)}, u32[]{:S(2)}) %collective-permute-start.13) | collective-permute-done | bytes 196640 | tf_op jit(solution)/shard_map/ppermute | solution.py:66
  281.2 10.8 %push_5.1 = bf16[4,160,384]{2,1,0:T(8,128)(2,1)} custom-call(bf16[4,160,384]{2,1,0:T(8,128)(2,1)} %bitcast.310), custom_call_target="tpu_custom_call" | custom-call | bytes 50000000 | tf_op jit(solution)/shard_map/push_5/pallas_call | solution.py:116
  307.7 10.0 %collective-permute-done.11 = bf16[160,1536]{1,0:T(8,128)(2,1)S(1)} collective-permute-done((bf16[160,1536]{1,0:T(8,128)(2,1)S(1)}, bf16[160,1536]{1,0:T(8,128)(2,1)S(1)}, u32[]{:S(2)}, u32[]{:S(2)}) %collective-permute-start.11) | collective-permute-done | bytes 491552 | tf_op jit(solution)/shard_map/ppermute | solution.py:66
  317.7 18.3 %collective-permute-start.15 = (bf16[160,1536]{1,0:T(8,128)(2,1)S(1)}, bf16[160,1536]{1,0:T(8,128)(2,1)}, u32[]{:S(2)}, u32[]{:S(2)}) collective-permute-start(bf16[160,1536]{1,0:T(8,128)(2,1)S(1)} %copy-done.24), channel_id=1, source_target_pairs={{0,1},{1,2},{2,3},{3,0},{4,5},{5,6},{6,7},{7,4},{8,9},{9,10},{10,1... | collective-permute-start | bytes 1474568 | tf_op jit(solution)/shard_map/ppermute | solution.py:66
  336.0 31.2 %collective-permute-done.10 = bf16[160,1536]{1,0:T(8,128)(2,1)S(1)} collective-permute-done((bf16[160,1536]{1,0:T(8,128)(2,1)S(1)}, bf16[160,1536]{1,0:T(8,128)(2,1)S(1)}, u32[]{:S(2)}, u32[]{:S(2)}) %collective-permute-start.10) | collective-permute-done | bytes 491552 | tf_op jit(solution)/shard_map/ppermute | solution.py:66
  374.9 7.8 %collective-permute-done.16 = bf16[160,1536]{1,0:T(8,128)(2,1)} collective-permute-done((bf16[160,1536]{1,0:T(8,128)(2,1)S(1)}, bf16[160,1536]{1,0:T(8,128)(2,1)}, u32[]{:S(2)}, u32[]{:S(2)}) %collective-permute-start.16) | collective-permute-done | bytes 491552 | tf_op jit(solution)/shard_map/ppermute | solution.py:66
  391.6 8.2 %convolution_convert_fusion.1 = bf16[1536,2048]{1,0:T(8,128)(2,1)} fusion(bf16[160,1536]{1,0:T(8,128)(2,1)S(1)} %copy-done.128, bf16[160,1536]{1,0:T(8,128)(2,1)S(1)} %copy-done.130, bf16[160,1536]{1,0:T(8,128)(2,1)} %collective-permute-done.9, bf16[160,1536]{1,0:T(8,128)(2,1)S(1)} %add_convert_fusion.1, bf16[640,1024]{1,0:T(8,128)(2,1)S(1)} %get-tuple-element.147, ...), kind=kOutput, calls=%fused_computation.11 | convolution fusion | flops 4042784768 | bytes 10878976 | tf_op jit(solution)/shard_map/dot_general | solution.py:49
  406.3 10.5 %convolution_convert_fusion.6 = bf16[640,1536]{1,0:T(8,128)(2,1)} fusion(bf16[640,2048]{1,0:T(8,128)(2,1)} %pad_maximum_fusion, bf16[1536,2048]{1,0:T(8,128)(2,1)} %all-gather.19.cloned.1.call-done), kind=kOutput, calls=%fused_computation.36 | convolution fusion | flops 4027514880 | bytes 10878976 | tf_op jit(solution)/shard_map/dot_general | solution.py:53
  416.8 38.5 %push_10.1 = bf16[4,160,1536]{2,1,0:T(8,128)(2,1)} custom-call(bf16[4,160,1536]{2,1,0:T(8,128)(2,1)} %bitcast.309), custom_call_target="tpu_custom_call" | custom-call | bytes 50000000 | tf_op jit(solution)/shard_map/push_10/pallas_call | solution.py:116
  469.0 22.0 %push_6.1 = bf16[4,160,384]{2,1,0:T(8,128)(2,1)} custom-call(bf16[4,160,384]{2,1,0:T(8,128)(2,1)} %bitcast.312), custom_call_target="tpu_custom_call" | custom-call | bytes 50000000 | tf_op jit(solution)/shard_map/push_6/pallas_call | solution.py:116
  525.1 8.2 %push_9.1 = f32[4,4,128]{2,1,0:T(4,128)} custom-call(f32[4,128]{1,0:T(4,128)} %bitcast.367), custom_call_target="tpu_custom_call" | custom-call | bytes 50000000 | tf_op jit(solution)/shard_map/push_9/pallas_call | solution.py:116
  546.8 8.4 %convolution_convert_fusion.3 = bf16[4096,768]{1,0:T(8,128)(2,1)} fusion(bf16[512,4096]{1,0:T(8,128)(2,1)} %all-gather.13.cloned.1.call-done, bf16[512,384]{1,0:T(8,128)(2,1)} %copy.311, bf16[512,384]{1,0:T(8,128)(2,1)S(1)} %subtract_convert_fusion.2), kind=kOutput, calls=%fused_computation.14 | convolution fusion | flops 3225944064 | bytes 11272192 | tf_op jit(solution)/shard_map/dot_general | solution.py:49
  573.2 7.7 multiply_reduce_fusion
  580.8 11.8 %multiply_convert_fusion = bf16[6,640,640]{1,2,0:T(8,128)(2,1)} fusion(f32[6,640,640]{1,2,0:T(8,128)} %get-tuple-element.288, f32[6,640]{1,0:T(8,128)S(1)} %get-tuple-element.287, f32[6,640,640]{1,2,0:T(8,128)} %get-tuple-element.281, f32[6,640]{1,0:T(8,128)S(1)} %copy-done.99), kind=kLoop, calls=%fused_computation.2 | loop fusion | flops 9830400 | bytes 24606720 | tf_op jit(solution)/shard_map/convert_element_type | solution.py:524
  616.7 12.2 %push_4.1 = (f32[4,10,128]{2,1,0:T(8,128)}, bf16[4,48,1536]{2,1,0:T(8,128)(2,1)}) custom-call(f32[10,128]{1,0:T(8,128)} %pad_maximum_fusion.19.refs_0_, bf16[4,48,1536]{2,1,0:T(8,128)(2,1)} %bitcast.334), custom_call_target="tpu_custom_call" | custom-call | bytes 50000000 | tf_op jit(solution)/shard_map/push_4/pallas_call | solution.py:116
  666.2 12.2 %collective-permute-done.25 = bf16[160,1536]{1,0:T(8,128)(2,1)} collective-permute-done((bf16[160,1536]{1,0:T(8,128)(2,1)}, bf16[160,1536]{1,0:T(8,128)(2,1)}, u32[]{:S(2)}, u32[]{:S(2)}) %collective-permute-start.25) | collective-permute-done | bytes 491552 | tf_op jit(solution)/shard_map/ppermute | solution.py:66
  699.4 15.7 %push_7.1 = f32[4,8,5248]{2,1,0:T(8,128)} custom-call(f32[8,5248]{1,0:T(8,128)} %pad_maximum_fusion.16.refs_0_), custom_call_target="tpu_custom_call" | custom-call | bytes 50000000 | tf_op jit(solution)/shard_map/push_7/pallas_call | solution.py:116
  717.8 31.9 %push_8.1 = (f32[8,8,5760]{2,1,0:T(8,128)}, bf16[4,48,1152]{2,1,0:T(8,128)(2,1)}, bf16[4,128,768]{2,1,0:T(8,128)(2,1)}) custom-call(f32[8,5760]{1,0:T(8,128)} %pad_maximum_fusion.15.refs_0_, bf16[4,48,1152]{2,1,0:T(8,128)(2,1)} %bitcast.343, bf16[4,128,768]{2,1,0:T(8,128)(2,1)} %bitcast.333), custom_call_target="tpu_custom_call" | custom-call | bytes 50000000 | tf_op jit(solution)/shard_map/push_8/pallas_call | solution.py:116
  (616 shorter events, 366.5 us)
Async XLA Ops:
  7.3 99.9 %all-gather.9.cloned.1.call-start = ((), (), s32[]{:S(2)}) async-start(), calls=%async_computation.5 | async-start | bytes 3538944 | tf_op jit(solution)/shard_map/all_gather | solution.py:57
  8.0 169.7 %all-gather.11.cloned.1.call-start = ((), (), s32[]{:S(2)}) async-start(), calls=%async_computation.6 | async-start | bytes 3981312 | tf_op jit(solution)/shard_map/all_gather | solution.py:57
  25.7 225.7 %all-gather.13.cloned.1.call-start = ((), (), s32[]{:S(2)}) async-start(), calls=%async_computation.7 | async-start | bytes 5242880 | tf_op jit(solution)/shard_map/all_gather | solution.py:309
  107.2 144.2 %all-gather.15.cloned.1.call-start = ((), (), s32[]{:S(2)}) async-start(), calls=%async_computation.8 | async-start | bytes 7077888 | tf_op jit(solution)/shard_map/all_gather | solution.py:57
  115.5 37.7 %collective-permute-start.4 = (bf16[128,768]{1,0:T(8,128)(2,1)S(1)}, bf16[128,768]{1,0:T(8,128)(2,1)S(1)}, u32[]{:S(2)}, u32[]{:S(2)}) collective-permute-start(bf16[128,768]{1,0:T(8,128)(2,1)S(1)} %bitcast.353), channel_id=1, source_target_pairs={{0,2},{1,3},{2,0},{3,1},{4,6},{5,7},{6,4},{7,5},{8,10},{9,11},{10,... | collective-permute-start | bytes 589832 | tf_op jit(solution)/shard_map/ppermute | solution.py:66
  116.8 36.6 %collective-permute-start.3 = (bf16[128,768]{1,0:T(8,128)(2,1)}, bf16[128,768]{1,0:T(8,128)(2,1)}, u32[]{:S(2)}, u32[]{:S(2)}) collective-permute-start(bf16[128,768]{1,0:T(8,128)(2,1)} %bitcast.42), channel_id=1, source_target_pairs={{0,1},{1,2},{2,3},{3,0},{4,5},{5,6},{6,7},{7,4},{8,9},{9,10},{10,1... | collective-permute-start | bytes 589832 | tf_op jit(solution)/shard_map/ppermute | solution.py:66
  159.5 133.6 %all-gather.17.cloned.1.call-start = ((), (), s32[]{:S(2)}) async-start(), calls=%async_computation.9 | async-start | bytes 5308416 | tf_op jit(solution)/shard_map/all_gather | solution.py:57
  229.6 138.3 %all-gather.19.cloned.1.call-start = ((), (), s32[]{:S(2)}) async-start(), calls=%async_computation.10 | async-start | bytes 7077888 | tf_op jit(solution)/shard_map/all_gather | solution.py:57
  248.5 306.9 %reduce-scatter.8.cloned.1.call-start = ((), (), s32[]{:S(2)}) async-start(), calls=%async_computation.12 | async-start | bytes 7077888 | tf_op jit(solution)/shard_map/reduce_scatter | solution.py:61
  302.7 64.5 %collective-permute-start.10 = (bf16[160,1536]{1,0:T(8,128)(2,1)S(1)}, bf16[160,1536]{1,0:T(8,128)(2,1)S(1)}, u32[]{:S(2)}, u32[]{:S(2)}) collective-permute-start(bf16[160,1536]{1,0:T(8,128)(2,1)S(1)} %add_convert_fusion.1), channel_id=1, source_target_pairs={{0,2},{1,3},{2,0},{3,1},{4,6},{5,7},{6,4},{7,5},{8,10},{9,11},{10,... | collective-permute-start | bytes 1474568 | tf_op jit(solution)/shard_map/ppermute | solution.py:66
  302.7 65.3 %collective-permute-start.9 = (bf16[160,1536]{1,0:T(8,128)(2,1)S(1)}, bf16[160,1536]{1,0:T(8,128)(2,1)}, u32[]{:S(2)}, u32[]{:S(2)}) collective-permute-start(bf16[160,1536]{1,0:T(8,128)(2,1)S(1)} %add_convert_fusion.1), channel_id=1, source_target_pairs={{0,1},{1,2},{2,3},{3,0},{4,5},{5,6},{6,7},{7,4},{8,9},{9,10},{10,1... | collective-permute-start | bytes 1474568 | tf_op jit(solution)/shard_map/ppermute | solution.py:66
  303.4 71.5 %collective-permute-start.17 = (bf16[160,1536]{1,0:T(8,128)(2,1)S(1)}, bf16[160,1536]{1,0:T(8,128)(2,1)S(1)}, u32[]{:S(2)}, u32[]{:S(2)}) collective-permute-start(bf16[160,1536]{1,0:T(8,128)(2,1)S(1)} %copy-done.24), channel_id=1, source_target_pairs={{0,3},{1,0},{2,1},{3,2},{4,7},{5,4},{6,5},{7,6},{8,11},{9,8},{10,9... | collective-permute-start | bytes 1474568 | tf_op jit(solution)/shard_map/ppermute | solution.py:66
  306.6 76.1 %collective-permute-start.16 = (bf16[160,1536]{1,0:T(8,128)(2,1)S(1)}, bf16[160,1536]{1,0:T(8,128)(2,1)}, u32[]{:S(2)}, u32[]{:S(2)}) collective-permute-start(bf16[160,1536]{1,0:T(8,128)(2,1)S(1)} %copy-done.24), channel_id=1, source_target_pairs={{0,2},{1,3},{2,0},{3,1},{4,6},{5,7},{6,4},{7,5},{8,10},{9,11},{10,... | collective-permute-start | bytes 1474568 | tf_op jit(solution)/shard_map/ppermute | solution.py:66
  317.7 65.0 %collective-permute-start.15 = (bf16[160,1536]{1,0:T(8,128)(2,1)S(1)}, bf16[160,1536]{1,0:T(8,128)(2,1)}, u32[]{:S(2)}, u32[]{:S(2)}) collective-permute-start(bf16[160,1536]{1,0:T(8,128)(2,1)S(1)} %copy-done.24), channel_id=1, source_target_pairs={{0,1},{1,2},{2,3},{3,0},{4,5},{5,6},{6,7},{7,4},{8,9},{9,10},{10,1... | collective-permute-start | bytes 1474568 | tf_op jit(solution)/shard_map/ppermute | solution.py:66
  399.8 201.9 %reduce-scatter.6.cloned.1.call-start = ((), (), s32[]{:S(2)}) async-start(), calls=%async_computation.11 | async-start | bytes 3538944 | tf_op jit(solution)/shard_map/reduce_scatter | solution.py:61
  406.2 210.5 %reduce-scatter.10.cloned.1.call-start = ((), (), s32[]{:S(2)}) async-start(), calls=%async_computation.13 | async-start | bytes 5308416 | tf_op jit(solution)/shard_map/reduce_scatter | solution.py:61
  463.3 254.5 %reduce-scatter.14.cloned.1.call-start = ((), (), s32[]{:S(2)}) async-start(), calls=%async_computation.15 | async-start | bytes 7077888 | tf_op jit(solution)/shard_map/reduce_scatter | solution.py:61
  539.1 58.7 %collective-permute-start.21 = (bf16[160,1536]{1,0:T(8,128)(2,1)}, bf16[160,1536]{1,0:T(8,128)(2,1)}, u32[]{:S(2)}, u32[]{:S(2)}) collective-permute-start(bf16[160,1536]{1,0:T(8,128)(2,1)} %get-tuple-element.164), channel_id=1, source_target_pairs={{0,3},{1,0},{2,1},{3,2},{4,7},{5,4},{6,5},{7,6},{8,11},{9,8},{10,9... | collective-permute-start | bytes 1474568 | tf_op jit(solution)/shard_map/ppermute | solution.py:66
  542.3 59.4 %collective-permute-start.22 = (bf16[160,1536]{1,0:T(8,128)(2,1)}, bf16[160,1536]{1,0:T(8,128)(2,1)}, u32[]{:S(2)}, u32[]{:S(2)}) collective-permute-start(bf16[160,1536]{1,0:T(8,128)(2,1)} %get-tuple-element.163), channel_id=1, source_target_pairs={{0,2},{1,3},{2,0},{3,1},{4,6},{5,7},{6,4},{7,5},{8,10},{9,11},{10,... | collective-permute-start | bytes 1474568 | tf_op jit(solution)/shard_map/ppermute | solution.py:66
  542.3 59.4 %collective-permute-start.23 = (bf16[160,1536]{1,0:T(8,128)(2,1)}, bf16[160,1536]{1,0:T(8,128)(2,1)}, u32[]{:S(2)}, u32[]{:S(2)}) collective-permute-start(bf16[160,1536]{1,0:T(8,128)(2,1)} %get-tuple-element.162), channel_id=1, source_target_pairs={{0,1},{1,2},{2,3},{3,0},{4,5},{5,6},{6,7},{7,4},{8,9},{9,10},{10,1... | collective-permute-start | bytes 1474568 | tf_op jit(solution)/shard_map/ppermute | solution.py:66
  555.2 162.6 %reduce-scatter.12.cloned.1.call-start = ((), (), s32[]{:S(2)}) async-start(), calls=%async_computation.14 | async-start | bytes 3981312 | tf_op jit(solution)/shard_map/reduce_scatter | solution.py:61
  569.8 31.9 %collective-permute-start.18 = (bf16[48,2048]{1,0:T(8,128)(2,1)}, bf16[48,2048]{1,0:T(8,128)(2,1)}, u32[]{:S(2)}, u32[]{:S(2)}) collective-permute-start(bf16[48,2048]{1,0:T(8,128)(2,1)} %get-tuple-element.198), channel_id=1, source_target_pairs={{0,1},{1,2},{2,3},{3,0},{4,5},{5,6},{6,7},{7,4},{8,9},{9,10},{10,1... | collective-permute-start | bytes 589832 | tf_op jit(solution)/shard_map/ppermute | solution.py:66
  642.8 35.6 %collective-permute-start.25 = (bf16[160,1536]{1,0:T(8,128)(2,1)}, bf16[160,1536]{1,0:T(8,128)(2,1)}, u32[]{:S(2)}, u32[]{:S(2)}) collective-permute-start(bf16[160,1536]{1,0:T(8,128)(2,1)} %get-tuple-element.159), channel_id=1, source_target_pairs={{0,2},{1,3},{2,0},{3,1},{4,6},{5,7},{6,4},{7,5},{8,10},{9,11},{10,... | collective-permute-start | bytes 1474568 | tf_op jit(solution)/shard_map/ppermute | solution.py:66
  642.8 35.6 %collective-permute-start.26 = (bf16[160,1536]{1,0:T(8,128)(2,1)}, bf16[160,1536]{1,0:T(8,128)(2,1)}, u32[]{:S(2)}, u32[]{:S(2)}) collective-permute-start(bf16[160,1536]{1,0:T(8,128)(2,1)} %get-tuple-element.158), channel_id=1, source_target_pairs={{0,1},{1,2},{2,3},{3,0},{4,5},{5,6},{6,7},{7,4},{8,9},{9,10},{10,1... | collective-permute-start | bytes 1474568 | tf_op jit(solution)/shard_map/ppermute | solution.py:66
  (147 other events, 3305.0 us)
Sparse Core Ops, SparseCore 0:
  10.0 34.8 all-gather.8
  47.4 40.7 all-gather.10
  107.3 93.6 all-gather.12
  203.3 44.1 all-gather.14
  249.8 38.7 all-gather.16
  290.9 45.3 all-gather.18
  399.9 61.0 reduce-scatter.7
  464.4 46.0 reduce-scatter.5
  514.0 53.7 reduce-scatter.9
  571.0 61.7 reduce-scatter.13
  664.3 47.8 reduce-scatter.11

commit v4 on v3

--- a/solution.py
+++ b/solution.py
@@ -260,11 +260,12 @@
         .transpose(2, 0, 1, 3)
         .reshape(sp, weight.shape[0], weight.shape[1] // sp)
     )
-    qkv_full = gather(ordered(send(columns(qkv_weight, 3), "sp"), "sp", 0))
     down_full = gather(down_weight)
 
     silu_cond = jax.nn.silu(condition.astype(F32)).astype(BF16)
     cond_all = lax.all_gather(silu_cond, "fsdp", axis=0)
+    cond_all, qkv_weight = tie(cond_all, qkv_weight)
+    qkv_full = gather(ordered(send(columns(qkv_weight, 3), "sp"), "sp", 0))
     cond_rows = lax.dynamic_slice_in_dim(cond_all, place * wrows, wrows, axis=2)
     small = jnp.concatenate(
         [
@@ -297,6 +298,7 @@
         ],
         0,
     )
+    arrived, caption = tie(arrived, caption)
     tokens_all = tokens_all.reshape(seq, dim)
     small_group = arrived[:, :, 3 * dim : 3 * dim + small_size // 8].reshape(8, -1)
     group_size = small_group.shape[1]
@@ -305,7 +307,7 @@
         axis=1,
     )
     (bundles,) = push_many([to_all(bundle, "sp")], 1)
-    bundles, down_full, caption = tie(bundles, down_full, caption)
+    bundles, down_full = tie(bundles, down_full)
     caption_all = lax.all_gather(caption, "sp", axis=0, tiled=True)
     small_all = (
         bundles[:, :, 3 * dim : 3 * dim + group_size]
@@ -324,23 +326,6 @@
     gate_tanh = jnp.tanh(mine(cross_full))
     modulation = jnp.sum(bundles[:, :, : 3 * dim], axis=0)
     modulation = jnp.concatenate([modulation[:CPG], modulation[CPG:]], axis=1) + bias_full[None]
-
-    modulation, text_key_weight, text_value_weight = tie(
-        modulation, text_key_weight, text_value_weight
-    )
-
-    text_full_weight = gather(
-        ordered(
-            send(
-                jnp.concatenate(
-                    [columns(text_key_weight, 1), columns(text_value_weight, 1)], axis=2
-                ),
-                "sp",
-            ),
-            "sp",
-            0,
-        )
-    )
 
     lengths = clip_lengths[0]
     ends = jnp.cumsum(lengths)
@@ -378,6 +363,21 @@
         projected[:, 2 * local :],
     )
     qk_squares, others = row_sums([jnp.sum(q_raw * q_raw, axis=1), jnp.sum(k_raw * k_raw, axis=1)], 2, True)
+    *qk_squares, text_key_weight, text_value_weight = tie(
+        *qk_squares, text_key_weight, text_value_weight
+    )
+    text_full_weight = gather(
+        ordered(
+            send(
+                jnp.concatenate(
+                    [columns(text_key_weight, 1), columns(text_value_weight, 1)], axis=2
+                ),
+                "sp",
+            ),
+            "sp",
+            0,
+        )
+    )
     q_root = lax.rsqrt(qk_squares[0] / dim + EPSILON)[:, None]
     k_root = lax.rsqrt(qk_squares[1] / dim + EPSILON)[:, None]
     half = HD // 2

time: 788 us -> 795 us (level)
  Pallas kernels: 221 us -> 239 us
    pallas_call x11, Pallas kernels: 221 us -> 239 us  [push_many(): pl.pallas_call(functools.partial(push_kernel, [(axis, size, block, spot)...]
  transfers between devices with their start and end apart: 38 -> 38, of which waited for: 12 -> 13; matrix products, arithmetic and copies ran while one was open for 38% -> 37% of each run, Pallas kernels for 24% -> 26%
where the time goes in v4:
time: 795 us; the launch traced here: 785 us
  Pallas kernels  239 us (30%)
  matrix products  156 us (20%)
  waiting for transfers between devices  121 us (15%)
  other arithmetic  92.5 us (12%)
  local copies, waits for them, and re-layouts  87.5 us (11%)
  starting transfers between devices  60.7 us (8%)
  between operations  16.7 us (2%)
  blocking collectives  10.7 us (1%)
    pallas_call x11, Pallas kernels, push_many(): pl.pallas_call(functools.partial(push_kernel, [(axis, size, block, spot)...  239 us
    ppermute x27, waiting for transfers between devices, shift(): lax.ppermute(values, axis, [(k, (k + step) % size) for k in range(size)])  120 us
    ppermute x27, starting transfers between devices, shift(): lax.ppermute(values, axis, [(k, (k + step) % size) for k in range(size)])  59 us
    dot_general x5, matrix products, left_product(): lax.dot_general(left, right, (((0,), (0,)), ((), ())), preferred_element_...  31.5 us
    dot_general x6, matrix products, product(): return jnp.dot(left, right, preferred_element_type=F32)  28.3 us
    dot_general x4, matrix products, right_product(): lax.dot_general(left, right, (((1,), (1,)), ((), ())), preferred_element_...  24.7 us
    dot_general x4, matrix products, body(): jnp.einsum('hqk,khd->qhd', a, b, preferred_element_type=F32)  19 us
    dot_general x4, matrix products, body(): jnp.einsum('hqk,qhd->khd', a, b, preferred_element_type=F32)  17.2 us
  transfers between devices with their start and end apart: 38, of which 13 were waited for; matrix products, arithmetic and copies ran while one was open for 37% of the time, Pallas kernels for 26%

profile of v4, /device:TPU:0, one launch (start us, length us, event | category | flops | bytes accessed | tf_op | source)
XLA Modules:
  0.0 784.8 jit_solution(6646618768222204144)
XLA Ops:
  8.8 10.7 %all-gather.1 = bf16[8,4,1536]{2,1,0:T(4,128)(2,1)S(1)} all-gather(bf16[1,4,1536]{2,1,0:T(4,128)(2,1)S(1)} %fusion.79), channel_id=2, replica_groups=mesh['fsdp'=8,'sp'=4] {'fsdp'}, dimensions={0}, use_global_device_ids=true | all-gather | bytes 110592 | tf_op jit(solution)/shard_map/all_gather | solution.py:266
  39.2 39.1 %push_0.1 = (f32[8,8,4736]{2,1,0:T(8,128)}, bf16[4,160,1536]{2,1,0:T(8,128)(2,1)}) custom-call(f32[8,8,4736]{2,1,0:T(8,128)} %pad_maximum_fusion.4.refs_0_, bf16[160,1536]{1,0:T(8,128)(2,1)} %refs_1_.1), custom_call_target="tpu_custom_call" | custom-call | bytes 50000000 | tf_op jit(solution)/shard_map/push_0/pallas_call | solution.py:116
  81.4 35.8 %push_1.1 = f32[4,8,5248]{2,1,0:T(8,128)} custom-call(f32[8,5248]{1,0:T(8,128)} %select_maximum_fusion.refs_0_), custom_call_target="tpu_custom_call" | custom-call | bytes 50000000 | tf_op jit(solution)/shard_map/push_1/pallas_call | solution.py:116
  122.7 8.6 %fusion.10 = bf16[640,1536]{1,0:T(8,128)(2,1)} fusion(f32[1536]{0:T(1024)S(1)} %get-tuple-element.137, f32[1536]{0:T(1024)S(1)} %get-tuple-element.138, f32[1536]{0:T(1024)S(1)} %get-tuple-element.139, f32[1536]{0:T(1024)S(1)} %get-tuple-element.140, f32[1536]{0:T(1024)S(1)} %get-tuple-element.141, f32[1536]{0:T(1024)S(1)} %get-tuple-element.142, ...), kind=kLoop, calls=%fused_computation.26 | loop fusion | flops 12779520 | bytes 3991936 | tf_op jit(solution)/shard_map/convert_element_type | solution.py:358
  139.2 18.1 %push_2.1 = f32[4,10,128]{2,1,0:T(8,128)} custom-call(f32[10,128]{1,0:T(8,128)} %pad_maximum_fusion.18.refs_0_), custom_call_target="tpu_custom_call" | custom-call | bytes 50000000 | tf_op jit(solution)/shard_map/push_2/pallas_call | solution.py:116
  164.7 8.5 %collective-permute-done.5 = bf16[128,768]{1,0:T(8,128)(2,1)S(1)} collective-permute-done((bf16[128,768]{1,0:T(8,128)(2,1)S(1)}, bf16[128,768]{1,0:T(8,128)(2,1)S(1)}, u32[]{:S(2)}, u32[]{:S(2)}) %collective-permute-start.5) | collective-permute-done | bytes 196640 | tf_op jit(solution)/shard_map/ppermute | solution.py:66
  173.4 20.0 %collective-permute-done.4 = bf16[128,768]{1,0:T(8,128)(2,1)S(1)} collective-permute-done((bf16[128,768]{1,0:T(8,128)(2,1)S(1)}, bf16[128,768]{1,0:T(8,128)(2,1)S(1)}, u32[]{:S(2)}, u32[]{:S(2)}) %collective-permute-start.4) | collective-permute-done | bytes 196640 | tf_op jit(solution)/shard_map/ppermute | solution.py:66
  241.6 11.4 %collective-permute-done.13 = bf16[48,2048]{1,0:T(8,128)(2,1)S(1)} collective-permute-done((bf16[48,2048]{1,0:T(8,128)(2,1)S(1)}, bf16[48,2048]{1,0:T(8,128)(2,1)S(1)}, u32[]{:S(2)}, u32[]{:S(2)}) %collective-permute-start.13) | collective-permute-done | bytes 196640 | tf_op jit(solution)/shard_map/ppermute | solution.py:66
  287.3 10.7 %push_5.1 = bf16[4,160,384]{2,1,0:T(8,128)(2,1)} custom-call(bf16[4,160,384]{2,1,0:T(8,128)(2,1)} %bitcast.311), custom_call_target="tpu_custom_call" | custom-call | bytes 50000000 | tf_op jit(solution)/shard_map/push_5/pallas_call | solution.py:116
  313.6 10.1 %collective-permute-done.11 = bf16[160,1536]{1,0:T(8,128)(2,1)S(1)} collective-permute-done((bf16[160,1536]{1,0:T(8,128)(2,1)S(1)}, bf16[160,1536]{1,0:T(8,128)(2,1)S(1)}, u32[]{:S(2)}, u32[]{:S(2)}) %collective-permute-start.11) | collective-permute-done | bytes 491552 | tf_op jit(solution)/shard_map/ppermute | solution.py:66
  324.5 19.0 %collective-permute-start.15 = (bf16[160,1536]{1,0:T(8,128)(2,1)S(1)}, bf16[160,1536]{1,0:T(8,128)(2,1)}, u32[]{:S(2)}, u32[]{:S(2)}) collective-permute-start(bf16[160,1536]{1,0:T(8,128)(2,1)S(1)} %copy-done.24), channel_id=1, source_target_pairs={{0,1},{1,2},{2,3},{3,0},{4,5},{5,6},{6,7},{7,4},{8,9},{9,10},{10,1... | collective-permute-start | bytes 1474568 | tf_op jit(solution)/shard_map/ppermute | solution.py:66
  343.5 29.7 %collective-permute-done.10 = bf16[160,1536]{1,0:T(8,128)(2,1)} collective-permute-done((bf16[160,1536]{1,0:T(8,128)(2,1)S(1)}, bf16[160,1536]{1,0:T(8,128)(2,1)}, u32[]{:S(2)}, u32[]{:S(2)}) %collective-permute-start.10) | collective-permute-done | bytes 491552 | tf_op jit(solution)/shard_map/ppermute | solution.py:66
  379.9 8.6 %collective-permute-done.16 = bf16[160,1536]{1,0:T(8,128)(2,1)} collective-permute-done((bf16[160,1536]{1,0:T(8,128)(2,1)S(1)}, bf16[160,1536]{1,0:T(8,128)(2,1)}, u32[]{:S(2)}, u32[]{:S(2)}) %collective-permute-start.16) | collective-permute-done | bytes 491552 | tf_op jit(solution)/shard_map/ppermute | solution.py:66
  397.4 8.3 %convolution_convert_fusion.1 = bf16[1536,2048]{1,0:T(8,128)(2,1)} fusion(bf16[160,1536]{1,0:T(8,128)(2,1)S(1)} %copy-done.130, bf16[160,1536]{1,0:T(8,128)(2,1)} %collective-permute-done.10, bf16[160,1536]{1,0:T(8,128)(2,1)} %collective-permute-done.9, bf16[160,1536]{1,0:T(8,128)(2,1)S(1)} %add_convert_fusion.1, ...), kind=kOutput, calls=%fused_computation.11 | convolution fusion | flops 4042784768 | bytes 10878976 | tf_op jit(solution)/shard_map/dot_general | solution.py:49
  412.5 10.4 %convolution_convert_fusion.6 = bf16[640,1536]{1,0:T(8,128)(2,1)} fusion(bf16[640,2048]{1,0:T(8,128)(2,1)} %pad_maximum_fusion, bf16[1536,2048]{1,0:T(8,128)(2,1)} %all-gather.19.cloned.1.call-done), kind=kOutput, calls=%fused_computation.36 | convolution fusion | flops 4027514880 | bytes 10878976 | tf_op jit(solution)/shard_map/dot_general | solution.py:53
  422.9 38.0 %push_10.1 = bf16[4,160,1536]{2,1,0:T(8,128)(2,1)} custom-call(bf16[4,160,1536]{2,1,0:T(8,128)(2,1)} %bitcast.310), custom_call_target="tpu_custom_call" | custom-call | bytes 50000000 | tf_op jit(solution)/shard_map/push_10/pallas_call | solution.py:116
  474.6 22.1 %push_6.1 = bf16[4,160,384]{2,1,0:T(8,128)(2,1)} custom-call(bf16[4,160,384]{2,1,0:T(8,128)(2,1)} %bitcast.313), custom_call_target="tpu_custom_call" | custom-call | bytes 50000000 | tf_op jit(solution)/shard_map/push_6/pallas_call | solution.py:116
  530.7 7.8 push_9.1
  552.0 8.4 %convolution_convert_fusion.3 = bf16[4096,768]{1,0:T(8,128)(2,1)} fusion(bf16[512,4096]{1,0:T(8,128)(2,1)} %all-gather.13.cloned.1.call-done, bf16[512,384]{1,0:T(8,128)(2,1)} %copy.311, bf16[512,384]{1,0:T(8,128)(2,1)S(1)} %subtract_convert_fusion.2), kind=kOutput, calls=%fused_computation.14 | convolution fusion | flops 3225944064 | bytes 11272192 | tf_op jit(solution)/shard_map/dot_general | solution.py:49
  585.9 12.0 %multiply_convert_fusion = bf16[6,640,640]{1,2,0:T(8,128)(2,1)} fusion(f32[6,640,640]{1,2,0:T(8,128)} %get-tuple-element.296, f32[6,640]{1,0:T(8,128)S(1)} %get-tuple-element.295, f32[6,640,640]{1,2,0:T(8,128)} %get-tuple-element.289, f32[6,640]{1,0:T(8,128)S(1)} %copy-done.102), kind=kLoop, calls=%fused_computation.2 | loop fusion | flops 9830400 | bytes 24606720 | tf_op jit(solution)/shard_map/convert_element_type | solution.py:524
  621.7 12.4 %push_4.1 = (f32[4,10,128]{2,1,0:T(8,128)}, bf16[4,48,1536]{2,1,0:T(8,128)(2,1)}) custom-call(f32[10,128]{1,0:T(8,128)} %pad_maximum_fusion.19.refs_0_, bf16[4,48,1536]{2,1,0:T(8,128)(2,1)} %bitcast.335), custom_call_target="tpu_custom_call" | custom-call | bytes 50000000 | tf_op jit(solution)/shard_map/push_4/pallas_call | solution.py:116
  671.6 11.7 %collective-permute-done.25 = bf16[160,1536]{1,0:T(8,128)(2,1)} collective-permute-done((bf16[160,1536]{1,0:T(8,128)(2,1)}, bf16[160,1536]{1,0:T(8,128)(2,1)}, u32[]{:S(2)}, u32[]{:S(2)}) %collective-permute-start.25) | collective-permute-done | bytes 491552 | tf_op jit(solution)/shard_map/ppermute | solution.py:66
  703.9 16.4 %push_7.1 = f32[4,8,5248]{2,1,0:T(8,128)} custom-call(f32[8,5248]{1,0:T(8,128)} %pad_maximum_fusion.16.refs_0_), custom_call_target="tpu_custom_call" | custom-call | bytes 50000000 | tf_op jit(solution)/shard_map/push_7/pallas_call | solution.py:116
  723.0 32.2 %push_8.1 = (f32[8,8,5760]{2,1,0:T(8,128)}, bf16[4,48,1152]{2,1,0:T(8,128)(2,1)}, bf16[4,128,768]{2,1,0:T(8,128)(2,1)}) custom-call(f32[8,5760]{1,0:T(8,128)} %pad_maximum_fusion.15.refs_0_, bf16[4,48,1152]{2,1,0:T(8,128)(2,1)} %bitcast.344, bf16[4,128,768]{2,1,0:T(8,128)(2,1)} %bitcast.334), custom_call_target="tpu_custom_call" | custom-call | bytes 50000000 | tf_op jit(solution)/shard_map/push_8/pallas_call | solution.py:116
  (619 shorter events, 358.3 us)
Async XLA Ops:
  7.3 110.8 %all-gather.9.cloned.1.call-start = ((), (), s32[]{:S(2)}) async-start(), calls=%async_computation.5 | async-start | bytes 3538944 | tf_op jit(solution)/shard_map/all_gather | solution.py:57
  8.0 123.3 %all-gather.11.cloned.1.call-start = ((), (), s32[]{:S(2)}) async-start(), calls=%async_computation.6 | async-start | bytes 3981312 | tf_op jit(solution)/shard_map/all_gather | solution.py:57
  36.5 221.0 %all-gather.13.cloned.1.call-start = ((), (), s32[]{:S(2)}) async-start(), calls=%async_computation.7 | async-start | bytes 5242880 | tf_op jit(solution)/shard_map/all_gather | solution.py:311
  78.3 179.2 %all-gather.15.cloned.1.call-start = ((), (), s32[]{:S(2)}) async-start(), calls=%async_computation.8 | async-start | bytes 7077888 | tf_op jit(solution)/shard_map/all_gather | solution.py:57
  163.9 29.5 %collective-permute-start.4 = (bf16[128,768]{1,0:T(8,128)(2,1)S(1)}, bf16[128,768]{1,0:T(8,128)(2,1)S(1)}, u32[]{:S(2)}, u32[]{:S(2)}) collective-permute-start(bf16[128,768]{1,0:T(8,128)(2,1)S(1)} %bitcast.354), channel_id=1, source_target_pairs={{0,2},{1,3},{2,0},{3,1},{4,6},{5,7},{6,4},{7,5},{8,10},{9,11},{10,... | collective-permute-start | bytes 589832 | tf_op jit(solution)/shard_map/ppermute | solution.py:66
  195.4 103.7 %all-gather.17.cloned.1.call-start = ((), (), s32[]{:S(2)}) async-start(), calls=%async_computation.9 | async-start | bytes 5308416 | tf_op jit(solution)/shard_map/all_gather | solution.py:57
  234.3 109.2 %all-gather.19.cloned.1.call-start = ((), (), s32[]{:S(2)}) async-start(), calls=%async_computation.10 | async-start | bytes 7077888 | tf_op jit(solution)/shard_map/all_gather | solution.py:57
  254.2 306.5 %reduce-scatter.8.cloned.1.call-start = ((), (), s32[]{:S(2)}) async-start(), calls=%async_computation.12 | async-start | bytes 7077888 | tf_op jit(solution)/shard_map/reduce_scatter | solution.py:61
  308.7 64.5 %collective-permute-start.10 = (bf16[160,1536]{1,0:T(8,128)(2,1)S(1)}, bf16[160,1536]{1,0:T(8,128)(2,1)}, u32[]{:S(2)}, u32[]{:S(2)}) collective-permute-start(bf16[160,1536]{1,0:T(8,128)(2,1)S(1)} %add_convert_fusion.1), channel_id=1, source_target_pairs={{0,2},{1,3},{2,0},{3,1},{4,6},{5,7},{6,4},{7,5},{8,10},{9,11},{10,... | collective-permute-start | bytes 1474568 | tf_op jit(solution)/shard_map/ppermute | solution.py:66
  308.7 64.5 %collective-permute-start.9 = (bf16[160,1536]{1,0:T(8,128)(2,1)S(1)}, bf16[160,1536]{1,0:T(8,128)(2,1)}, u32[]{:S(2)}, u32[]{:S(2)}) collective-permute-start(bf16[160,1536]{1,0:T(8,128)(2,1)S(1)} %add_convert_fusion.1), channel_id=1, source_target_pairs={{0,1},{1,2},{2,3},{3,0},{4,5},{5,6},{6,7},{7,4},{8,9},{9,10},{10,1... | collective-permute-start | bytes 1474568 | tf_op jit(solution)/shard_map/ppermute | solution.py:66
  309.3 70.6 %collective-permute-start.17 = (bf16[160,1536]{1,0:T(8,128)(2,1)S(1)}, bf16[160,1536]{1,0:T(8,128)(2,1)S(1)}, u32[]{:S(2)}, u32[]{:S(2)}) collective-permute-start(bf16[160,1536]{1,0:T(8,128)(2,1)S(1)} %copy-done.24), channel_id=1, source_target_pairs={{0,3},{1,0},{2,1},{3,2},{4,7},{5,4},{6,5},{7,6},{8,11},{9,8},{10,9... | collective-permute-start | bytes 1474568 | tf_op jit(solution)/shard_map/ppermute | solution.py:66
  312.5 76.0 %collective-permute-start.16 = (bf16[160,1536]{1,0:T(8,128)(2,1)S(1)}, bf16[160,1536]{1,0:T(8,128)(2,1)}, u32[]{:S(2)}, u32[]{:S(2)}) collective-permute-start(bf16[160,1536]{1,0:T(8,128)(2,1)S(1)} %copy-done.24), channel_id=1, source_target_pairs={{0,2},{1,3},{2,0},{3,1},{4,6},{5,7},{6,4},{7,5},{8,10},{9,11},{10,... | collective-permute-start | bytes 1474568 | tf_op jit(solution)/shard_map/ppermute | solution.py:66
  324.5 63.9 %collective-permute-start.15 = (bf16[160,1536]{1,0:T(8,128)(2,1)S(1)}, bf16[160,1536]{1,0:T(8,128)(2,1)}, u32[]{:S(2)}, u32[]{:S(2)}) collective-permute-start(bf16[160,1536]{1,0:T(8,128)(2,1)S(1)} %copy-done.24), channel_id=1, source_target_pairs={{0,1},{1,2},{2,3},{3,0},{4,5},{5,6},{6,7},{7,4},{8,9},{9,10},{10,1... | collective-permute-start | bytes 1474568 | tf_op jit(solution)/shard_map/ppermute | solution.py:66
  405.8 201.3 %reduce-scatter.6.cloned.1.call-start = ((), (), s32[]{:S(2)}) async-start(), calls=%async_computation.11 | async-start | bytes 3538944 | tf_op jit(solution)/shard_map/reduce_scatter | solution.py:61
  412.2 209.5 %reduce-scatter.10.cloned.1.call-start = ((), (), s32[]{:S(2)}) async-start(), calls=%async_computation.13 | async-start | bytes 5308416 | tf_op jit(solution)/shard_map/reduce_scatter | solution.py:61
  468.9 254.0 %reduce-scatter.14.cloned.1.call-start = ((), (), s32[]{:S(2)}) async-start(), calls=%async_computation.15 | async-start | bytes 7077888 | tf_op jit(solution)/shard_map/reduce_scatter | solution.py:61
  544.4 58.3 %collective-permute-start.21 = (bf16[160,1536]{1,0:T(8,128)(2,1)}, bf16[160,1536]{1,0:T(8,128)(2,1)}, u32[]{:S(2)}, u32[]{:S(2)}) collective-permute-start(bf16[160,1536]{1,0:T(8,128)(2,1)} %get-tuple-element.172), channel_id=1, source_target_pairs={{0,3},{1,0},{2,1},{3,2},{4,7},{5,4},{6,5},{7,6},{8,11},{9,8},{10,9... | collective-permute-start | bytes 1474568 | tf_op jit(solution)/shard_map/ppermute | solution.py:66
  547.5 59.5 %collective-permute-start.22 = (bf16[160,1536]{1,0:T(8,128)(2,1)}, bf16[160,1536]{1,0:T(8,128)(2,1)}, u32[]{:S(2)}, u32[]{:S(2)}) collective-permute-start(bf16[160,1536]{1,0:T(8,128)(2,1)} %get-tuple-element.171), channel_id=1, source_target_pairs={{0,2},{1,3},{2,0},{3,1},{4,6},{5,7},{6,4},{7,5},{8,10},{9,11},{10,... | collective-permute-start | bytes 1474568 | tf_op jit(solution)/shard_map/ppermute | solution.py:66
  547.5 59.5 %collective-permute-start.23 = (bf16[160,1536]{1,0:T(8,128)(2,1)}, bf16[160,1536]{1,0:T(8,128)(2,1)}, u32[]{:S(2)}, u32[]{:S(2)}) collective-permute-start(bf16[160,1536]{1,0:T(8,128)(2,1)} %get-tuple-element.170), channel_id=1, source_target_pairs={{0,1},{1,2},{2,3},{3,0},{4,5},{5,6},{6,7},{7,4},{8,9},{9,10},{10,1... | collective-permute-start | bytes 1474568 | tf_op jit(solution)/shard_map/ppermute | solution.py:66
  560.4 162.5 %reduce-scatter.12.cloned.1.call-start = ((), (), s32[]{:S(2)}) async-start(), calls=%async_computation.14 | async-start | bytes 3981312 | tf_op jit(solution)/shard_map/reduce_scatter | solution.py:61
  575.1 32.0 %collective-permute-start.18 = (bf16[48,2048]{1,0:T(8,128)(2,1)}, bf16[48,2048]{1,0:T(8,128)(2,1)}, u32[]{:S(2)}, u32[]{:S(2)}) collective-permute-start(bf16[48,2048]{1,0:T(8,128)(2,1)} %get-tuple-element.206), channel_id=1, source_target_pairs={{0,1},{1,2},{2,3},{3,0},{4,5},{5,6},{6,7},{7,4},{8,9},{9,10},{10,1... | collective-permute-start | bytes 589832 | tf_op jit(solution)/shard_map/ppermute | solution.py:66
  577.5 29.6 %collective-permute-start.19 = (bf16[48,2048]{1,0:T(8,128)(2,1)}, bf16[48,2048]{1,0:T(8,128)(2,1)}, u32[]{:S(2)}, u32[]{:S(2)}) collective-permute-start(bf16[48,2048]{1,0:T(8,128)(2,1)} %get-tuple-element.205), channel_id=1, source_target_pairs={{0,2},{1,3},{2,0},{3,1},{4,6},{5,7},{6,4},{7,5},{8,10},{9,11},{10,... | collective-permute-start | bytes 589832 | tf_op jit(solution)/shard_map/ppermute | solution.py:66
  648.2 35.1 %collective-permute-start.25 = (bf16[160,1536]{1,0:T(8,128)(2,1)}, bf16[160,1536]{1,0:T(8,128)(2,1)}, u32[]{:S(2)}, u32[]{:S(2)}) collective-permute-start(bf16[160,1536]{1,0:T(8,128)(2,1)} %get-tuple-element.167), channel_id=1, source_target_pairs={{0,2},{1,3},{2,0},{3,1},{4,6},{5,7},{6,4},{7,5},{8,10},{9,11},{10,... | collective-permute-start | bytes 1474568 | tf_op jit(solution)/shard_map/ppermute | solution.py:66
  648.2 35.1 %collective-permute-start.26 = (bf16[160,1536]{1,0:T(8,128)(2,1)}, bf16[160,1536]{1,0:T(8,128)(2,1)}, u32[]{:S(2)}, u32[]{:S(2)}) collective-permute-start(bf16[160,1536]{1,0:T(8,128)(2,1)} %get-tuple-element.166), channel_id=1, source_target_pairs={{0,1},{1,2},{2,3},{3,0},{4,5},{5,6},{6,7},{7,4},{8,9},{9,10},{10,1... | collective-permute-start | bytes 1474568 | tf_op jit(solution)/shard_map/ppermute | solution.py:66
  (147 other events, 3316.0 us)
Sparse Core Ops, SparseCore 0:
  10.0 34.8 all-gather.8
  47.4 35.0 all-gather.10
  84.0 110.9 all-gather.12
  197.3 43.2 all-gather.14
  243.0 38.7 all-gather.16
  284.1 45.4 all-gather.18
  405.9 60.7 reduce-scatter.7
  470.0 46.0 reduce-scatter.5
  519.6 53.7 reduce-scatter.9
  576.6 61.7 reduce-scatter.13
  669.7 47.9 reduce-scatter.11
